TPU v7x, 256 devices: a whole 4x4x8 slice. The times are simulated.
256 devices in a mesh: branch: 4 (over z_lo), row: 4 (over x), col: 16 (over y, z_hi, core).
Axes of the slice: x: 4, y: 4, z: 8 (z_hi: 2, z_lo: 4; z = z_hi * 4 + z_lo), core: 2. Of those that a mesh axis runs over, the one named last changes fastest.
Arguments:
- section_in: bfloat16 [4, 4, 16, 48, 4096], P('branch', 'row', 'col'), may hold values from -6 to 6
- conv_weight: bfloat16 [4, 2, 3, 3, 384, 384], P('branch'), may hold values from -1 to 1, as said below
- conv_bias: float32 [4, 2, 384], P('branch'), may hold values from -3 to 3
- join_weight: bfloat16 [720, 720], replicated, may hold values from -0.4375 to 0.4375
- join_bias: float32 [720], replicated, may hold values from -3 to 3
Outputs:
- joined_first: bfloat16 [48, 128, 2048], P(None, ('branch', 'row'), 'col')
- joined_second: bfloat16 [96, 64, 1024], P(None, ('branch', 'row'), 'col')
- joined_third: bfloat16 [192, 32, 512], P(None, ('branch', 'row'), 'col')
- joined_fourth: bfloat16 [384, 16, 256], P(None, ('branch', 'row'), 'col')
Inputs may be any that keep to these rules, and one draw needn't show every extreme that they name: `conv_weight`: entries of branch b's kernels have standard deviation (9 * 2^b * 48) ** -0.5; entries outside the C_b x C_b corner are drawn too and unused.
All inputs are finite; a program needn't handle non-finite values.
Results may differ from a plain program's by a relative error of at most 0.0075.
Values may be sent and summed in bfloat16 or wider, within the bound.
No kernel may reach another device: no remote copies, remote signals or barrier semaphores. Data moves between devices by JAX's collectives and lax.ppermute only.
A program may use at most 128 MiB of HBM per device.

v0:
```python
import jax
import jax.numpy as jnp
from jax import lax
from jax.experimental import pallas as pl
from jax.experimental.pallas import tpu as pltpu
from jax.sharding import PartitionSpec as P

WIDTH = 48
TH = 32
TW = 128
MARGIN = 128
BF = jnp.bfloat16
F32 = jnp.float32
VMEM = pl.BlockSpec(memory_space=pltpu.VMEM)


def up128(n):
    return -(-n // 128) * 128


class Geo:
    def __init__(self, b):
        self.b = b
        self.parts = 1 << b
        self.channels = WIDTH << b
        self.rows = TH >> b
        self.cols = TW >> b
        self.pixels = self.rows * self.cols
        self.pitch = self.cols + 4
        self.high = self.rows + 4
        self.n1 = up128((self.high - 2) * self.pitch)
        self.n2 = up128((self.high - 4) * self.pitch)
        self.width_x = up128(MARGIN + 2 * self.pitch + 1 + self.n1)
        self.width_h = up128(MARGIN + 2 * self.pitch + 1 + self.n2)
        self.start = ((1 << b) - 1) * WIDTH


GEO = [Geo(b) for b in range(4)]


def place():
    return lax.axis_index("branch"), lax.axis_index("row"), lax.axis_index("col")


def per_branch(body):
    branch = place()[0]
    for g in GEO:

        @pl.when(branch == g.b)
        def _(g=g):
            body(g)


def rows_kernel(x, top, bottom):
    def body(g):
        n = 2 * g.cols
        for q in range(g.parts):
            base = q * g.pixels
            top[:, q * n : (q + 1) * n] = x[:, base : base + n]
            bottom[:, q * n : (q + 1) * n] = x[:, base + g.pixels - n : base + g.pixels]

    per_branch(body)


def source_row(g, x, above, below, q, y):
    if y < 2:
        return above, q * 2 * g.cols + y * g.cols
    if y < g.rows + 2:
        return x, q * g.pixels + (y - 2) * g.cols
    return below, q * 2 * g.cols + (y - g.rows - 2) * g.cols


def cols_kernel(x, above, below, west, east):
    def body(g):
        for q in range(g.parts):
            for y in range(g.high):
                ref, lane = source_row(g, x, above, below, q, y)
                at = q * 2 * g.high + 2 * y
                west[:, at : at + 2] = ref[:, lane : lane + 2]
                last = lane + g.cols - 2
                east[:, at : at + 2] = ref[:, last : last + 2]

    per_branch(body)


def channel_order(g):
    out = lax.broadcasted_iota(jnp.int32, (g.channels, g.channels), 0)
    k = lax.broadcasted_iota(jnp.int32, (g.channels, g.channels), 1)
    part = jnp.zeros_like(k)
    for m in range(1, g.parts):
        part = part + (k >= WIDTH * m).astype(jnp.int32)
    at = (k - WIDTH * part) * g.parts + part
    return (at == out).astype(F32).astype(BF)


def inside(g, row_place, col_place):
    p = lax.broadcasted_iota(jnp.int32, (8, g.n1), 1).astype(F32)
    y = jnp.floor((p + 0.5) * (1.0 / g.pitch))
    x = p - y * g.pitch
    y = y + 1.0
    outside = (
        ((y == 1.0) & (row_place == 0))
        | ((y == g.rows + 2.0) & (row_place == 3))
        | ((x == 1.0) & (col_place == 0))
        | ((x == g.cols + 2.0) & (col_place == 15))
    )
    return jnp.where(outside, 0.0, 1.0)[0:1, :]


def block_kernel(x, above, below, left, right, weight, bias, o0, o1, o2, o3, *scratch):
    outs = (o0, o1, o2, o3)
    wbuf, sems, wcat, col, z0 = scratch[:5]
    xs_all = (None,) + scratch[5:8]
    xp_all = scratch[8:12]
    hp_all = scratch[12:16]
    zt_all = (None,) + scratch[16:19]
    _, row_place, col_place = place()

    def body(g):
        c = g.channels
        cl = up128(c)

        def fetch(layer):
            return pltpu.make_async_copy(
                weight.at[0, layer, :, :, 0:c, 0:cl],
                wbuf.at[layer, :, :, 0:c, 0:cl],
                sems.at[layer],
            )

        fetch(0).start()
        fetch(1).start()
        xp, hp = xp_all[g.b], hp_all[g.b]
        xs = xp if g.b == 0 else xs_all[g.b]
        for q in range(g.parts):
            rows = slice(q * WIDTH, (q + 1) * WIDTH)
            for y in range(g.high):
                ref, lane = source_row(g, x, above, below, q, y)
                at = MARGIN + y * g.pitch
                edge = q * 2 * g.high + 2 * y
                xs[rows, at : at + 2] = left[:, edge : edge + 2]
                xs[rows, at + 2 : at + 2 + g.cols] = ref[:, lane : lane + g.cols]
                xs[rows, at + 2 + g.cols : at + g.pitch] = right[:, edge : edge + 2]
        if g.b:
            xp[...] = jnp.dot(channel_order(g), xs[...], preferred_element_type=F32).astype(BF)

        mask = inside(g, row_place, col_place)

        def column(layer):
            wide = jnp.broadcast_to(bias[0, layer : layer + 1, :], (8, 8 * WIDTH))
            return wide.T[0:c, 0:1]

        def taps():
            for dy in range(3):
                for dx in range(3):
                    yield dy, dx, MARGIN + dy * g.pitch + dx - 1

        def conv(layer, source, n, finish):
            fetch(layer).wait()
            if g.b == 0:
                for dy, dx, lane in taps():
                    t = 3 * dy + dx
                    wcat[:, WIDTH * t : WIDTH * (t + 1)] = wbuf[layer, dy, dx, 0:c, 0:c]
                    col[WIDTH * t : WIDTH * (t + 1), 0:n] = source[:, lane : lane + n]
                step = 384
                for at in range(0, n, step):
                    size = min(step, n - at)
                    finish(
                        at,
                        size,
                        jnp.dot(
                            wcat[...], col[:, at : at + size], preferred_element_type=F32
                        ),
                    )
            else:
                total = None
                for dy, dx, lane in taps():
                    term = jnp.dot(
                        wbuf[layer, dy, dx, 0:c, 0:c],
                        source[:, lane : lane + n],
                        preferred_element_type=F32,
                    )
                    total = term if total is None else total + term
                finish(0, n, total)

        bias0 = column(0)

        def finish_first(at, size, total):
            h = jnp.maximum(total + bias0, 0.0) * mask[:, at : at + size]
            hp[:, MARGIN + at : MARGIN + at + size] = h.astype(BF)

        conv(0, xp, g.n1, finish_first)

        bias1 = column(1)

        def finish_second(at, size, total):
            lane = MARGIN + 2 * g.pitch + at
            own = xp[:, lane : lane + size].astype(F32)
            z = jnp.maximum(total + bias1 + own, 0.0)
            if g.b == 0:
                z0[:, at : at + size] = z.astype(BF)
            else:
                zt_all[g.b][...] = z.T

        conv(1, hp, g.n2, finish_second)

        strip = g.rows // 4
        for y in range(g.rows):
            out = outs[(y // strip - g.b) % 4]
            at = y * g.pitch + 2
            if g.b == 0:
                r = (y % strip) * WIDTH
                out[r : r + WIDTH, :] = z0[:, at : at + g.cols]
                continue
            values = zt_all[g.b][at : at + g.cols, :].astype(BF)
            for m in range(cl // 128):
                r = m * strip * g.cols + (y % strip) * g.cols
                lanes = min(128, c - 128 * m)
                out[r : r + g.cols, 0:lanes] = values[:, 128 * m : 128 * m + lanes]

    per_branch(body)


def repeat_map(j, i):
    gj, gi = GEO[j], GEO[i]
    shape = (gj.pixels // 4, gi.pixels // 4)
    fine = lax.broadcasted_iota(jnp.int32, shape, 0)
    coarse = lax.broadcasted_iota(jnp.int32, shape, 1)
    return cover(fine, coarse, gj, i - j)


def cover(fine, coarse, g, d):
    bits = 7 - g.b
    y = fine >> bits
    x = fine & (g.cols - 1)
    return (((y >> d) << (bits - d)) + (x >> d) == coarse).astype(F32).astype(BF)


def repeat_map_t(j, i):
    gj, gi = GEO[j], GEO[i]
    shape = (gi.pixels // 4, gj.pixels // 4)
    coarse = lax.broadcasted_iota(jnp.int32, shape, 0)
    fine = lax.broadcasted_iota(jnp.int32, shape, 1)
    return cover(fine, coarse, gj, i - j)


def nn(a, b):
    return jnp.dot(a, b, preferred_element_type=F32)


def nt(a, b):
    return lax.dot_general(a, b, (((1,), (1,)), ((), ())), preferred_element_type=F32)


def join_kernel(r0, r1, r2, r3, weight, bias, out0, out1, out2, out3, zb, z0s, s0):
    received = (r0, r1, r2, r3)
    row_place = place()[1]
    for g in GEO:
        used = (384, 256, 128, 48)[g.b]
        for j in range(4):

            @pl.when((row_place + 4 - g.b) % 4 == j)
            def _(g=g, j=j, used=used):
                zb[g.b, 0:used, :] = received[j][0:used, :]

    for y in range(8):
        z0s[:, 128 * y : 128 * (y + 1)] = zb[0, WIDTH * y : WIDTH * (y + 1), :]
    z = [
        z0s[...],
        zb[1, 0:256, 0:96],
        jnp.concatenate([zb[2, 0:64, :], zb[2, 64:128, 0:64]], axis=1),
        jnp.concatenate([zb[3, 0:16, :], zb[3, 16:32, :], zb[3, 32:48, :]], axis=1),
    ]

    def block(j, i):
        gj, gi = GEO[j], GEO[i]
        return weight[gj.start : gj.start + gj.channels, gi.start : gi.start + gi.channels]

    total = None
    for i in (1, 2, 3):
        term = nn(nt(block(0, i), z[i]).astype(BF), repeat_map_t(0, i))
        total = term if total is None else total + term
    wide = jnp.broadcast_to(bias[:, 0:WIDTH], (8, WIDTH))
    total = jnp.maximum(total + z[0].astype(F32) + wide.T[:, 0:1], 0.0)
    for y in range(8):
        s0[:, y, :] = total[:, 128 * y : 128 * (y + 1)]
    out0[...] = s0[...].astype(BF)

    for j, out in ((1, out1), (2, out2), (3, out3)):
        g = GEO[j]
        total = z[j].astype(F32) + bias[:, g.start : g.start + g.channels]
        for i in range(4):
            if i == j:
                continue
            if i < j:
                sums = (nt if i == 0 else nn)(repeat_map_t(i, j), z[i])
                mean = (sums * (0.25 ** (j - i))).astype(BF)
                total = total + nt(mean, block(j, i)).astype(BF).astype(F32)
            else:
                total = total + nn(repeat_map(j, i), nt(z[i], block(j, i)).astype(BF))
        out[...] = jnp.maximum(total, 0.0).astype(BF)


def params():
    return pltpu.CompilerParams(vmem_limit_bytes=40 * 1024 * 1024)


def like(*shapes):
    return tuple(jax.ShapeDtypeStruct(s, BF) for s in shapes)


def call_rows(x):
    return pl.pallas_call(
        rows_kernel,
        out_shape=like((WIDTH, 256), (WIDTH, 256)),
        in_specs=[VMEM],
        out_specs=(VMEM, VMEM),
        compiler_params=params(),
    )(x)


def call_cols(x, above, below):
    return pl.pallas_call(
        cols_kernel,
        out_shape=like((WIDTH, 128), (WIDTH, 128)),
        in_specs=[VMEM] * 3,
        out_specs=(VMEM, VMEM),
        compiler_params=params(),
    )(x, above, below)


def call_block(x, above, below, left, right, weight, bias):
    scratch = [
        pltpu.VMEM((2, 3, 3, 384, 384), BF),
        pltpu.SemaphoreType.DMA((2,)),
        pltpu.VMEM((WIDTH, 9 * WIDTH), BF),
        pltpu.VMEM((9 * WIDTH, GEO[0].n1), BF),
        pltpu.VMEM((WIDTH, GEO[0].n2), BF),
    ]
    scratch += [pltpu.VMEM((g.channels, g.width_x), BF) for g in GEO[1:]]
    scratch += [pltpu.VMEM((g.channels, g.width_x), BF) for g in GEO]
    scratch += [pltpu.VMEM((g.channels, g.width_h), BF) for g in GEO]
    scratch += [pltpu.VMEM((g.n2, g.channels), F32) for g in GEO[1:]]
    return pl.pallas_call(
        block_kernel,
        out_shape=like(*[(384, 128)] * 4),
        in_specs=[VMEM] * 5 + [pl.BlockSpec(memory_space=pl.ANY), VMEM],
        out_specs=(VMEM,) * 4,
        scratch_shapes=scratch,
        compiler_params=params(),
    )(x, above, below, left, right, weight, bias)


def call_join(received, weight, bias):
    return pl.pallas_call(
        join_kernel,
        out_shape=like((WIDTH, 8, 128), (256, 96), (64, 192), (16, 384)),
        in_specs=[VMEM] * 6,
        out_specs=(VMEM,) * 4,
        scratch_shapes=[
            pltpu.VMEM((4, 384, 128), BF),
            pltpu.VMEM((WIDTH, 1024), BF),
            pltpu.VMEM((WIDTH, 8, 128), F32),
        ],
        compiler_params=params(),
    )(*received, weight, bias)


def shifted(shard, axis, by):
    size = lax.axis_size(axis)
    pairs = [(i, i + by) for i in range(size) if 0 <= i + by < size]
    return lax.ppermute(shard, axis, pairs)


def exchanged(parts):
    return [
        lax.ppermute(
            part,
            ("branch", "row"),
            [(b * 4 + r, r * 4 + (b + j) % 4) for b in range(4) for r in range(4)],
        )
        for j, part in enumerate(parts)
    ]


def local(section_in, conv_weight, conv_bias, join_weight, join_bias):
    x = section_in[0, 0, 0]
    top, bottom = call_rows(x)
    above = shifted(bottom, "row", 1)
    below = shifted(top, "row", -1)
    west, east = call_cols(x, above, below)
    left = shifted(east, "col", 1)
    right = shifted(west, "col", -1)
    parts = call_block(x, above, below, left, right, conv_weight, conv_bias)
    received = exchanged(parts)
    out = call_join(received, join_weight, join_bias[None, :])
    first = [out[0]]
    for g in GEO[1:]:
        pixel_major = out[g.b].reshape(g.rows // 4, g.cols, g.channels)
        first.append(pixel_major.transpose(2, 0, 1))
    return tuple(first)


def solution(mesh):
    in_specs = (
        P("branch", "row", "col", None, None),
        P("branch", None, None, None, None, None),
        P("branch", None, None),
        P(),
        P(),
    )
    out_specs = (P(None, ("branch", "row"), "col"),) * 4
    return jax.shard_map(local, mesh=mesh, in_specs=in_specs, out_specs=out_specs, check_vma=False)
```

profile of v0, /device:TPU:1, one launch (start us, length us, event | category | flops | bytes accessed | tf_op | source)
XLA Modules:
  0.0 66.3 jit_solution(13730157643970777142)
XLA Ops:
  0.6 0.0 copy-start.1
  0.6 1.0 %copy-done.1 = bf16[1,1,1,48,4096]{4,3,2,1,0:T(8,128)(2,1)S(1)} copy-done((bf16[1,1,1,48,4096]{4,3,2,1,0:T(8,128)(2,1)S(1)}, bf16[1,1,1,48,4096]{4,3,2,1,0:T(8,128)(2,1)}, u32[]{:S(2)}) %copy-start.1) | copy-done | bytes 393240
  1.6 4.1 %collective-permute-start = (bf16[48,256]{1,0:T(8,128)(2,1)S(1)}, bf16[48,256]{1,0:T(8,128)(2,1)S(1)}, u32[]{:S(2)}, u32[]{:S(2)}) collective-permute-start(bf16[48,256]{1,0:T(8,128)(2,1)S(1)} %get-tuple-element.16), channel_id=1, source_target_pairs={{0,16},{16,32},{32,48},{1,17},{17,33},{33,49},{2,18},{18,34},{34,5... | collective-permute-start | bytes 73736 | tf_op jit(solution)/shard_map/ppermute | solution.py:371
  5.7 1.3 %collective-permute-start.1 = (bf16[48,256]{1,0:T(8,128)(2,1)S(1)}, bf16[48,256]{1,0:T(8,128)(2,1)S(1)}, u32[]{:S(2)}, u32[]{:S(2)}) collective-permute-start(bf16[48,256]{1,0:T(8,128)(2,1)S(1)} %get-tuple-element.17), channel_id=1, source_target_pairs={{16,0},{32,16},{48,32},{17,1},{33,17},{49,33},{18,2},{34,18},{50,3... | collective-permute-start | bytes 73736 | tf_op jit(solution)/shard_map/ppermute | solution.py:371
  7.0 0.0 collective-permute-done.above
  7.0 3.3 %collective-permute-done.1.below = bf16[48,256]{1,0:T(8,128)(2,1)S(1)} collective-permute-done((bf16[48,256]{1,0:T(8,128)(2,1)S(1)}, bf16[48,256]{1,0:T(8,128)(2,1)S(1)}, u32[]{:S(2)}, u32[]{:S(2)}) %collective-permute-start.1) | collective-permute-done | bytes 24608 | tf_op jit(solution)/shard_map/ppermute | solution.py:371
  10.3 0.5 shard_map.85
  10.8 10.8 %collective-permute-start.2 = (bf16[48,128]{1,0:T(8,128)(2,1)S(1)}, bf16[48,128]{1,0:T(8,128)(2,1)S(1)}, u32[]{:S(2)}, u32[]{:S(2)}) collective-permute-start(bf16[48,128]{1,0:T(8,128)(2,1)S(1)} %get-tuple-element.18), channel_id=1, source_target_pairs={{0,1},{1,2},{2,3},{3,4},{4,5},{5,6},{6,7},{7,8},{8,9},{9,10},{10,1... | collective-permute-start | bytes 36872 | tf_op jit(solution)/shard_map/ppermute | solution.py:371
  21.6 1.9 %collective-permute-start.3 = (bf16[48,128]{1,0:T(8,128)(2,1)S(1)}, bf16[48,128]{1,0:T(8,128)(2,1)S(1)}, u32[]{:S(2)}, u32[]{:S(2)}) collective-permute-start(bf16[48,128]{1,0:T(8,128)(2,1)S(1)} %get-tuple-element.19), channel_id=1, source_target_pairs={{1,0},{2,1},{3,2},{4,3},{5,4},{6,5},{7,6},{8,7},{9,8},{10,9},{11,1... | collective-permute-start | bytes 36872 | tf_op jit(solution)/shard_map/ppermute | solution.py:371
  23.5 0.0 collective-permute-done.2.left
  23.6 7.0 %collective-permute-done.3.right = bf16[48,128]{1,0:T(8,128)(2,1)S(1)} collective-permute-done((bf16[48,128]{1,0:T(8,128)(2,1)S(1)}, bf16[48,128]{1,0:T(8,128)(2,1)S(1)}, u32[]{:S(2)}, u32[]{:S(2)}) %collective-permute-start.3) | collective-permute-done | bytes 12320 | tf_op jit(solution)/shard_map/ppermute | solution.py:371
  30.5 2.5 %copy-done = bf16[1,2,3,3,384,384]{5,4,3,2,1,0:T(8,128)(2,1)S(1)} copy-done((bf16[1,2,3,3,384,384]{5,4,3,2,1,0:T(8,128)(2,1)S(1)}, bf16[1,2,3,3,384,384]{5,4,3,2,1,0:T(8,128)(2,1)}, u32[]{:S(2)}) %copy-start) | copy-done | bytes 5308440
  33.1 0.7 %copy-done.3 = f32[1,2,384]{2,1,0:T(2,128)S(1)} copy-done((f32[1,2,384]{2,1,0:T(2,128)S(1)}, f32[1,2,384]{2,1,0:T(2,128)}, u32[]{:S(2)}) %copy-start.3) | copy-done | bytes 3096
  33.7 4.3 %shard_map.86 = (bf16[384,128]{1,0:T(8,128)(2,1)S(1)}, bf16[384,128]{1,0:T(8,128)(2,1)S(1)}, bf16[384,128]{1,0:T(8,128)(2,1)S(1)}, bf16[384,128]{1,0:T(8,128)(2,1)S(1)}) custom-call(bf16[48,4096]{1,0:T(8,128)(2,1)S(1)} %bitcast.12, bf16[48,256]{1,0:T(8,128)(2,1)S(1)} %collective-permute-done.above, bf16[48,256]{1,0:T(8,128)(2,1)S(1)} %collective-permute-done.1.below, ...), custom_call_target="tpu_custom_call" | custom-call | tf_op jit(solution)/shard_map/pallas_call | solution.py:343
  38.0 0.7 %collective-permute-start.4 = (bf16[384,128]{1,0:T(8,128)(2,1)S(1)}, bf16[384,128]{1,0:T(8,128)(2,1)S(1)}, u32[]{:S(2)}, u32[]{:S(2)}) collective-permute-start(bf16[384,128]{1,0:T(8,128)(2,1)S(1)} %get-tuple-element.20), channel_id=1, source_target_pairs={{0,0},{16,64},{32,128},{48,192},{64,16},{80,80},{96,144},{112,208}... | collective-permute-start | bytes 294920 | tf_op jit(solution)/shard_map/ppermute | solution.py:376
  38.7 2.7 %collective-permute-start.5 = (bf16[384,128]{1,0:T(8,128)(2,1)S(1)}, bf16[384,128]{1,0:T(8,128)(2,1)S(1)}, u32[]{:S(2)}, u32[]{:S(2)}) collective-permute-start(bf16[384,128]{1,0:T(8,128)(2,1)S(1)} %get-tuple-element.21), channel_id=1, source_target_pairs={{0,16},{16,80},{32,144},{48,208},{64,32},{80,96},{96,160},{112,224... | collective-permute-start | bytes 294920 | tf_op jit(solution)/shard_map/ppermute | solution.py:376
  41.4 3.4 %collective-permute-start.6 = (bf16[384,128]{1,0:T(8,128)(2,1)S(1)}, bf16[384,128]{1,0:T(8,128)(2,1)S(1)}, u32[]{:S(2)}, u32[]{:S(2)}) collective-permute-start(bf16[384,128]{1,0:T(8,128)(2,1)S(1)} %get-tuple-element.22), channel_id=1, source_target_pairs={{0,32},{16,96},{32,160},{48,224},{64,48},{80,112},{96,176},{112,24... | collective-permute-start | bytes 294920 | tf_op jit(solution)/shard_map/ppermute | solution.py:376
  44.7 3.7 %collective-permute-start.7 = (bf16[384,128]{1,0:T(8,128)(2,1)S(1)}, bf16[384,128]{1,0:T(8,128)(2,1)S(1)}, u32[]{:S(2)}, u32[]{:S(2)}) collective-permute-start(bf16[384,128]{1,0:T(8,128)(2,1)S(1)} %get-tuple-element.23), channel_id=1, source_target_pairs={{0,48},{16,112},{32,176},{48,240},{64,0},{80,64},{96,128},{112,192... | collective-permute-start | bytes 294920 | tf_op jit(solution)/shard_map/ppermute | solution.py:376
  48.5 0.0 collective-permute-done.4.r0
  48.5 0.0 collective-permute-done.5.r1
  48.5 6.7 %collective-permute-done.6.r2 = bf16[384,128]{1,0:T(8,128)(2,1)S(1)} collective-permute-done((bf16[384,128]{1,0:T(8,128)(2,1)S(1)}, bf16[384,128]{1,0:T(8,128)(2,1)S(1)}, u32[]{:S(2)}, u32[]{:S(2)}) %collective-permute-start.6) | collective-permute-done | bytes 98336 | tf_op jit(solution)/shard_map/ppermute | solution.py:376
  55.2 8.3 %collective-permute-done.7.r3 = bf16[384,128]{1,0:T(8,128)(2,1)S(1)} collective-permute-done((bf16[384,128]{1,0:T(8,128)(2,1)S(1)}, bf16[384,128]{1,0:T(8,128)(2,1)S(1)}, u32[]{:S(2)}, u32[]{:S(2)}) %collective-permute-start.7) | collective-permute-done | bytes 98336 | tf_op jit(solution)/shard_map/ppermute | solution.py:376
  63.5 0.0 copy-done.2
  63.5 2.8 %shard_map.87 = (bf16[48,8,128]{2,1,0:T(8,128)(2,1)}, bf16[256,96]{1,0:T(8,128)(2,1)}, bf16[64,192]{1,0:T(8,128)(2,1)}, bf16[16,384]{1,0:T(8,128)(2,1)}) custom-call(bf16[384,128]{1,0:T(8,128)(2,1)S(1)} %collective-permute-done.4.r0, bf16[384,128]{1,0:T(8,128)(2,1)S(1)} %collective-permute-done.5.r1, bf16[384,128]{1,0:T(8,128)(2,1)S(1)} %collective-permute-done.6.r2, ...), custom_call_target="tpu_custom_call" | custom-call | tf_op jit(solution)/shard_map/pallas_call | solution.py:354
  (7 shorter events, 0.0 us)
Async XLA Ops:
  0.6 1.0 %copy-start.1 = (bf16[1,1,1,48,4096]{4,3,2,1,0:T(8,128)(2,1)S(1)}, bf16[1,1,1,48,4096]{4,3,2,1,0:T(8,128)(2,1)}, u32[]{:S(2)}) copy-start(bf16[1,1,1,48,4096]{4,3,2,1,0:T(8,128)(2,1)} %param.5) | copy-start | bytes 1179652
  1.6 46.8 %copy-start.4 = (f32[720]{0:T(1024)S(1)}, f32[720]{0:T(1024)}, u32[]{:S(2)}) copy-start(f32[720]{0:T(1024)} %param.9) | copy-start | bytes 8644
  1.6 5.4 %collective-permute-start = (bf16[48,256]{1,0:T(8,128)(2,1)S(1)}, bf16[48,256]{1,0:T(8,128)(2,1)S(1)}, u32[]{:S(2)}, u32[]{:S(2)}) collective-permute-start(bf16[48,256]{1,0:T(8,128)(2,1)S(1)} %get-tuple-element.16), channel_id=1, source_target_pairs={{0,16},{16,32},{32,48},{1,17},{17,33},{33,49},{2,18},{18,34},{34,5... | collective-permute-start | bytes 73736 | tf_op jit(solution)/shard_map/ppermute | solution.py:371
  5.7 4.6 %collective-permute-start.1 = (bf16[48,256]{1,0:T(8,128)(2,1)S(1)}, bf16[48,256]{1,0:T(8,128)(2,1)S(1)}, u32[]{:S(2)}, u32[]{:S(2)}) collective-permute-start(bf16[48,256]{1,0:T(8,128)(2,1)S(1)} %get-tuple-element.17), channel_id=1, source_target_pairs={{16,0},{32,16},{48,32},{17,1},{33,17},{49,33},{18,2},{34,18},{50,3... | collective-permute-start | bytes 73736 | tf_op jit(solution)/shard_map/ppermute | solution.py:371
  10.8 12.7 %collective-permute-start.2 = (bf16[48,128]{1,0:T(8,128)(2,1)S(1)}, bf16[48,128]{1,0:T(8,128)(2,1)S(1)}, u32[]{:S(2)}, u32[]{:S(2)}) collective-permute-start(bf16[48,128]{1,0:T(8,128)(2,1)S(1)} %get-tuple-element.18), channel_id=1, source_target_pairs={{0,1},{1,2},{2,3},{3,4},{4,5},{5,6},{6,7},{7,8},{8,9},{9,10},{10,1... | collective-permute-start | bytes 36872 | tf_op jit(solution)/shard_map/ppermute | solution.py:371
  21.6 8.9 %collective-permute-start.3 = (bf16[48,128]{1,0:T(8,128)(2,1)S(1)}, bf16[48,128]{1,0:T(8,128)(2,1)S(1)}, u32[]{:S(2)}, u32[]{:S(2)}) collective-permute-start(bf16[48,128]{1,0:T(8,128)(2,1)S(1)} %get-tuple-element.19), channel_id=1, source_target_pairs={{1,0},{2,1},{3,2},{4,3},{5,4},{6,5},{7,6},{8,7},{9,8},{10,9},{11,1... | collective-permute-start | bytes 36872 | tf_op jit(solution)/shard_map/ppermute | solution.py:371
  30.5 2.5 %copy-start = (bf16[1,2,3,3,384,384]{5,4,3,2,1,0:T(8,128)(2,1)S(1)}, bf16[1,2,3,3,384,384]{5,4,3,2,1,0:T(8,128)(2,1)}, u32[]{:S(2)}) copy-start(bf16[1,2,3,3,384,384]{5,4,3,2,1,0:T(8,128)(2,1)} %weight.2) | copy-start | bytes 15925252
  33.0 0.7 %copy-start.3 = (f32[1,2,384]{2,1,0:T(2,128)S(1)}, f32[1,2,384]{2,1,0:T(2,128)}, u32[]{:S(2)}) copy-start(f32[1,2,384]{2,1,0:T(2,128)} %bias.1) | copy-start | bytes 9220
  33.7 29.8 %copy-start.2 = (bf16[720,720]{1,0:T(8,128)(2,1)S(1)}, bf16[720,720]{1,0:T(8,128)(2,1)}, u32[]{:S(2)}) copy-start(bf16[720,720]{1,0:T(8,128)(2,1)} %weight.3) | copy-start | bytes 3110404
  38.0 10.4 %collective-permute-start.4 = (bf16[384,128]{1,0:T(8,128)(2,1)S(1)}, bf16[384,128]{1,0:T(8,128)(2,1)S(1)}, u32[]{:S(2)}, u32[]{:S(2)}) collective-permute-start(bf16[384,128]{1,0:T(8,128)(2,1)S(1)} %get-tuple-element.20), channel_id=1, source_target_pairs={{0,0},{16,64},{32,128},{48,192},{64,16},{80,80},{96,144},{112,208}... | collective-permute-start | bytes 294920 | tf_op jit(solution)/shard_map/ppermute | solution.py:376
  38.7 9.7 %collective-permute-start.5 = (bf16[384,128]{1,0:T(8,128)(2,1)S(1)}, bf16[384,128]{1,0:T(8,128)(2,1)S(1)}, u32[]{:S(2)}, u32[]{:S(2)}) collective-permute-start(bf16[384,128]{1,0:T(8,128)(2,1)S(1)} %get-tuple-element.21), channel_id=1, source_target_pairs={{0,16},{16,80},{32,144},{48,208},{64,32},{80,96},{96,160},{112,224... | collective-permute-start | bytes 294920 | tf_op jit(solution)/shard_map/ppermute | solution.py:376
  41.4 13.8 %collective-permute-start.6 = (bf16[384,128]{1,0:T(8,128)(2,1)S(1)}, bf16[384,128]{1,0:T(8,128)(2,1)S(1)}, u32[]{:S(2)}, u32[]{:S(2)}) collective-permute-start(bf16[384,128]{1,0:T(8,128)(2,1)S(1)} %get-tuple-element.22), channel_id=1, source_target_pairs={{0,32},{16,96},{32,160},{48,224},{64,48},{80,112},{96,176},{112,24... | collective-permute-start | bytes 294920 | tf_op jit(solution)/shard_map/ppermute | solution.py:376
  44.7 18.7 %collective-permute-start.7 = (bf16[384,128]{1,0:T(8,128)(2,1)S(1)}, bf16[384,128]{1,0:T(8,128)(2,1)S(1)}, u32[]{:S(2)}, u32[]{:S(2)}) collective-permute-start(bf16[384,128]{1,0:T(8,128)(2,1)S(1)} %get-tuple-element.23), channel_id=1, source_target_pairs={{0,48},{16,112},{32,176},{48,240},{64,0},{80,64},{96,128},{112,192... | collective-permute-start | bytes 294920 | tf_op jit(solution)/shard_map/ppermute | solution.py:376
where the time goes:
time: 66.6 us; the launch traced here: 66.3 us
  starting transfers between devices  28.5 us (43%)
  waiting for transfers between devices  25.3 us (38%)
  Pallas kernels  7.62 us (11%)
  local copies, waits for them, and re-layouts  4.19 us (6%)
  between operations  0.73 us (1%)
    ppermute x4, starting transfers between devices, shifted(): return lax.ppermute(shard, axis, pairs)  18.1 us
    ppermute x4, waiting for transfers between devices, exchanged(): lax.ppermute(part, ('branch', 'row'), [(b * 4 + r, r * 4 + (b + j) % 4) f...  15 us
    ppermute x4, starting transfers between devices, exchanged(): lax.ppermute(part, ('branch', 'row'), [(b * 4 + r, r * 4 + (b + j) % 4) f...  10.4 us
    ppermute x4, waiting for transfers between devices, shifted(): return lax.ppermute(shard, axis, pairs)  10.2 us
    pallas_call x1, Pallas kernels, call_block(): pl.pallas_call(block_kernel, out_shape=like(*[(384, 128)] * 4), in_specs=...  4.31 us
    unnamed x10, local copies, waits for them, and re-layouts  4.18 us
    pallas_call x1, Pallas kernels, call_join(): pl.pallas_call(join_kernel, out_shape=like((WIDTH, 8, 128), (256, 96), (6...  2.79 us
  transfers between devices with their start and end apart: 8, of which 4 were waited for; matrix products, arithmetic and copies ran while one was open for 0% of the time, Pallas kernels for 0%

commit v1 on v0

v1 whole, which is shorter than its diff:
```python
import jax
import jax.numpy as jnp
from jax import lax
from jax.experimental import pallas as pl
from jax.experimental.pallas import tpu as pltpu
from jax.sharding import PartitionSpec as P

WIDTH = 48
TH = 32
TW = 128
MARGIN = 128
BF = jnp.bfloat16
F32 = jnp.float32
VMEM = pl.BlockSpec(memory_space=pltpu.VMEM)


def up128(n):
    return -(-n // 128) * 128


class Geo:
    def __init__(self, b):
        self.b = b
        self.parts = 1 << b
        self.channels = WIDTH << b
        self.rows = TH >> b
        self.cols = TW >> b
        self.pixels = self.rows * self.cols
        self.strip = self.rows // 4
        self.high = self.strip + 4
        self.main = self.high * self.cols
        self.side = self.high * 2
        self.slot = up128(self.main + 2 * self.side)
        self.pitch = self.cols + 4
        self.wide = 4 * self.pitch
        self.n1 = up128((self.strip + 2) * self.wide)
        self.n2 = up128(self.strip * self.wide)
        self.width_x = up128(MARGIN + 2 * self.wide + 1 + self.n1)
        self.width_h = up128(max(MARGIN + 2 * self.wide + 1 + self.n2, MARGIN + self.n1))
        self.start = ((1 << b) - 1) * WIDTH


GEO = [Geo(b) for b in range(4)]
MAIN = 1536
SIDE = 256


def place():
    return lax.axis_index("branch"), lax.axis_index("row"), lax.axis_index("col")


def per_branch(body):
    branch = place()[0]
    for g in GEO:

        @pl.when(branch == g.b)
        def _(g=g):
            body(g)


def cols_kernel(x, west, east):
    def body(g):
        for q in range(g.parts):
            for y in range(g.rows):
                lane = q * g.pixels + y * g.cols
                at = 2 * (q * g.rows + y)
                west[:, at : at + 2] = x[:, lane : lane + 2]
                last = lane + g.cols - 2
                east[:, at : at + 2] = x[:, last : last + 2]

    per_branch(body)


def runs(g, k):
    i = 0
    while i < g.high:
        y = (k * g.strip - 2 + i) % g.rows
        n = min(g.high - i, g.rows - y)
        yield i, y, n
        i += n


def strips_kernel(x, out):
    def body(g):
        for k in range(4):
            for q in range(g.parts):
                for i, y, n in runs(g, k):
                    at = q * g.main + i * g.cols
                    lane = q * g.pixels + y * g.cols
                    out[k, :, at : at + n * g.cols] = x[:, lane : lane + n * g.cols]

    per_branch(body)


def sides_kernel(left, right, _, out):
    def body(g):
        for k in range(4):
            for q in range(g.parts):
                for i, y, n in runs(g, k):
                    at = q * g.side + 2 * i
                    lane = 2 * (q * g.rows + y)
                    out[k, :, at : at + 2 * n] = left[:, lane : lane + 2 * n]
                    at += 128
                    out[k, :, at : at + 2 * n] = right[:, lane : lane + 2 * n]

    per_branch(body)


def channel_order(g):
    out = lax.broadcasted_iota(jnp.int32, (g.channels, g.channels), 0)
    k = lax.broadcasted_iota(jnp.int32, (g.channels, g.channels), 1)
    part = jnp.zeros_like(k)
    for m in range(1, g.parts):
        part = part + (k >= WIDTH * m).astype(jnp.int32)
    at = (k - WIDTH * part) * g.parts + part
    return (at == out).astype(F32).astype(BF)


def inside(g, row_place, col_place):
    p = lax.broadcasted_iota(jnp.int32, (8, g.n1), 1).astype(F32)
    row = jnp.floor((p + 0.5) * (1.0 / g.wide))
    rest = p - row * g.wide
    tile = jnp.floor((rest + 0.5) * (1.0 / g.pitch))
    x = rest - tile * g.pitch
    y = row - 1.0 + (row_place * g.strip).astype(F32)
    outside = (
        ((tile == 0.0) & (y < 0.0))
        | ((tile == 3.0) & (y > g.rows - 1.0))
        | ((x == 1.0) & (col_place == 0))
        | ((x == g.cols + 2.0) & (col_place == 15))
    )
    return jnp.where(outside, 0.0, 1.0)[0:1, :]


def block_kernel(strips, sides, weight, bias, out, *scratch):
    wbuf, sems, wcat, col, z0 = scratch[:5]
    st_all = scratch[5:9]
    xp_all = scratch[9:13]
    hp_all = scratch[13:17]
    zt_all = (None,) + scratch[17:20]
    _, row_place, col_place = place()

    def body(g):
        c = g.channels
        cl = up128(c)

        def fetch(layer, dy):
            return pltpu.make_async_copy(
                weight.at[0, layer, dy, :, 0:c, 0:cl],
                wbuf.at[layer, dy, :, 0:c, 0:cl],
                sems.at[layer, dy],
            )

        for layer in range(2):
            for dy in range(3):
                fetch(layer, dy).start()

        st, xp, hp = st_all[g.b], xp_all[g.b], hp_all[g.b]
        ends = (0, g.main, g.main + g.side, g.main + 2 * g.side)

        def fill(tile, source, i=None):
            for q in range(g.parts):
                rows = slice(q * WIDTH, (q + 1) * WIDTH)
                for at, ref, lane, n in (
                    (ends[0], strips, q * g.main, g.cols),
                    (ends[1], sides, q * g.side, 2),
                    (ends[2], sides, 128 + q * g.side, 2),
                ):
                    first, size = (0, n * g.high) if i is None else (i * n, n)
                    at = tile * g.slot + at + first
                    if 0 <= source < 4:
                        piece = ref[source, :, lane + first : lane + first + size]
                    else:
                        piece = jnp.zeros((WIDTH, size), BF)
                    st[rows, at : at + size] = piece

        for tile in range(4):
            fill(tile, tile)
        for i in range(g.high):
            low = [k for k in range(4) if k * g.strip - 2 + i < 0]
            high = [k for k in range(4) if k * g.strip - 2 + i >= g.rows]
            if low:

                @pl.when(row_place <= max(low))
                def _(i=i):
                    for tile in range(4):
                        fill(tile, tile - 1, i)

            if high:

                @pl.when(row_place >= min(high))
                def _(i=i):
                    for tile in range(4):
                        fill(tile, tile + 1, i)

        if g.b:
            st[...] = jnp.dot(channel_order(g), st[...], preferred_element_type=F32).astype(BF)
        for i in range(g.high):
            for tile in range(4):
                at = MARGIN + i * g.wide + tile * g.pitch
                base = tile * g.slot
                for to, lane, n in (
                    (at, base + ends[1] + 2 * i, 2),
                    (at + 2, base + i * g.cols, g.cols),
                    (at + 2 + g.cols, base + ends[2] + 2 * i, 2),
                ):
                    xp[:, to : to + n] = st[:, lane : lane + n]

        mask = inside(g, row_place, col_place)

        def column(layer):
            wide = jnp.broadcast_to(bias[0, layer : layer + 1, :], (8, 8 * WIDTH))
            return wide.T[0:c, 0:1]

        def conv(layer, source, n, finish):
            total = None
            for dy in range(3):
                fetch(layer, dy).wait()
                for dx in range(3):
                    lane = MARGIN + dy * g.wide + dx - 1
                    if g.b == 0:
                        t = 3 * dy + dx
                        wcat[:, WIDTH * t : WIDTH * (t + 1)] = wbuf[layer, dy, dx, 0:c, 0:c]
                        col[WIDTH * t : WIDTH * (t + 1), 0:n] = source[:, lane : lane + n]
                    else:
                        term = jnp.dot(
                            wbuf[layer, dy, dx, 0:c, 0:c],
                            source[:, lane : lane + n],
                            preferred_element_type=F32,
                        )
                        total = term if total is None else total + term
            if g.b:
                finish(0, n, total)
                return
            for at in range(0, n, 384):
                size = min(384, n - at)
                finish(
                    at,
                    size,
                    jnp.dot(wcat[...], col[:, at : at + size], preferred_element_type=F32),
                )

        bias0 = column(0)

        def finish_first(at, size, total):
            h = jnp.maximum(total + bias0, 0.0) * mask[:, at : at + size]
            hp[:, MARGIN + at : MARGIN + at + size] = h.astype(BF)

        conv(0, xp, g.n1, finish_first)

        bias1 = column(1)

        def finish_second(at, size, total):
            lane = MARGIN + 2 * g.wide + at
            own = xp[:, lane : lane + size].astype(F32)
            z = jnp.maximum(total + bias1 + own, 0.0)
            if g.b == 0:
                z0[:, at : at + size] = z.astype(BF)
            else:
                zt_all[g.b][...] = z.T

        conv(1, hp, g.n2, finish_second)

        for tile in range(4):
            for i in range(g.strip):
                at = i * g.wide + tile * g.pitch + 2
                if g.b == 0:
                    out[tile, i * WIDTH : (i + 1) * WIDTH, :] = z0[:, at : at + g.cols]
                    continue
                values = zt_all[g.b][at : at + g.cols, :].astype(BF)
                for m in range(cl // 128):
                    r = (m * g.strip + i) * g.cols
                    lanes = min(128, c - 128 * m)
                    out[tile, r : r + g.cols, 0:lanes] = values[:, 128 * m : 128 * m + lanes]

    per_branch(body)


def repeat_map(j, i):
    gj, gi = GEO[j], GEO[i]
    shape = (gj.pixels // 4, gi.pixels // 4)
    fine = lax.broadcasted_iota(jnp.int32, shape, 0)
    coarse = lax.broadcasted_iota(jnp.int32, shape, 1)
    return cover(fine, coarse, gj, i - j)


def cover(fine, coarse, g, d):
    bits = 7 - g.b
    y = fine >> bits
    x = fine & (g.cols - 1)
    return (((y >> d) << (bits - d)) + (x >> d) == coarse).astype(F32).astype(BF)


def repeat_map_t(j, i):
    gj, gi = GEO[j], GEO[i]
    shape = (gi.pixels // 4, gj.pixels // 4)
    coarse = lax.broadcasted_iota(jnp.int32, shape, 0)
    fine = lax.broadcasted_iota(jnp.int32, shape, 1)
    return cover(fine, coarse, gj, i - j)


def nn(a, b):
    return jnp.dot(a, b, preferred_element_type=F32)


def nt(a, b):
    return lax.dot_general(a, b, (((1,), (1,)), ((), ())), preferred_element_type=F32)


def join_kernel(zb, weight, bias, out0, out1, out2, out3, z0s, s0):
    for y in range(8):
        z0s[:, 128 * y : 128 * (y + 1)] = zb[0, WIDTH * y : WIDTH * (y + 1), :]
    z = [
        z0s[...],
        zb[1, 0:256, 0:96],
        jnp.concatenate([zb[2, 0:64, :], zb[2, 64:128, 0:64]], axis=1),
        jnp.concatenate([zb[3, 0:16, :], zb[3, 16:32, :], zb[3, 32:48, :]], axis=1),
    ]

    def block(j, i):
        gj, gi = GEO[j], GEO[i]
        return weight[gj.start : gj.start + gj.channels, gi.start : gi.start + gi.channels]

    total = None
    for i in (1, 2, 3):
        term = nn(nt(block(0, i), z[i]).astype(BF), repeat_map_t(0, i))
        total = term if total is None else total + term
    wide = jnp.broadcast_to(bias[:, 0:WIDTH], (8, WIDTH))
    total = jnp.maximum(total + z[0].astype(F32) + wide.T[:, 0:1], 0.0)
    for y in range(8):
        s0[:, y, :] = total[:, 128 * y : 128 * (y + 1)]
    out0[...] = s0[...].astype(BF)

    for j, out in ((1, out1), (2, out2), (3, out3)):
        g = GEO[j]
        total = z[j].astype(F32) + bias[:, g.start : g.start + g.channels]
        for i in range(4):
            if i == j:
                continue
            if i < j:
                sums = (nt if i == 0 else nn)(repeat_map_t(i, j), z[i])
                mean = (sums * (0.25 ** (j - i))).astype(BF)
                total = total + nt(mean, block(j, i)).astype(BF).astype(F32)
            else:
                total = total + nn(repeat_map(j, i), nt(z[i], block(j, i)).astype(BF))
        out[...] = jnp.maximum(total, 0.0).astype(BF)


def params(mib=40):
    return pltpu.CompilerParams(vmem_limit_bytes=mib * 1024 * 1024)


def like(*shapes):
    return tuple(jax.ShapeDtypeStruct(s, BF) for s in shapes)


def call_cols(x):
    return pl.pallas_call(
        cols_kernel,
        out_shape=like((WIDTH, 128), (WIDTH, 128)),
        in_specs=[VMEM],
        out_specs=(VMEM, VMEM),
        compiler_params=params(),
    )(x)


def call_strips(x):
    return pl.pallas_call(
        strips_kernel,
        out_shape=like((4, WIDTH, MAIN))[0],
        in_specs=[VMEM],
        out_specs=VMEM,
        compiler_params=params(),
    )(x)


def call_sides(left, right, after):
    return pl.pallas_call(
        sides_kernel,
        out_shape=like((4, WIDTH, SIDE))[0],
        in_specs=[VMEM] * 2 + [pl.BlockSpec(memory_space=pl.ANY)],
        out_specs=VMEM,
        compiler_params=params(),
    )(left, right, after)


def call_block(strips, sides, weight, bias):
    scratch = [
        pltpu.VMEM((2, 3, 3, 384, 384), BF),
        pltpu.SemaphoreType.DMA((2, 3)),
        pltpu.VMEM((WIDTH, 9 * WIDTH), BF),
        pltpu.VMEM((9 * WIDTH, GEO[0].n1), BF),
        pltpu.VMEM((WIDTH, GEO[0].n2), BF),
    ]
    scratch += [pltpu.VMEM((g.channels, 4 * g.slot), BF) for g in GEO]
    scratch += [pltpu.VMEM((g.channels, g.width_x), BF) for g in GEO]
    scratch += [pltpu.VMEM((g.channels, g.width_h), BF) for g in GEO]
    scratch += [pltpu.VMEM((g.n2, g.channels), F32) for g in GEO[1:]]
    return pl.pallas_call(
        block_kernel,
        out_shape=like((4, 384, 128))[0],
        in_specs=[VMEM, VMEM, pl.BlockSpec(memory_space=pltpu.HBM), VMEM],
        out_specs=VMEM,
        scratch_shapes=scratch,
        compiler_params=params(60),
    )(strips, sides, weight, bias)


def call_join(received, weight, bias):
    return pl.pallas_call(
        join_kernel,
        out_shape=like((WIDTH, 8, 128), (256, 96), (64, 192), (16, 384)),
        in_specs=[VMEM] * 3,
        out_specs=(VMEM,) * 4,
        scratch_shapes=[
            pltpu.VMEM((WIDTH, 1024), BF),
            pltpu.VMEM((WIDTH, 8, 128), F32),
        ],
        compiler_params=params(),
    )(received, weight, bias)


def shifted(shard, axis, by):
    size = lax.axis_size(axis)
    pairs = [(i, i + by) for i in range(size) if 0 <= i + by < size]
    return lax.ppermute(shard, axis, pairs)


def swapped(parts, axis):
    return lax.all_to_all(parts, axis, split_axis=0, concat_axis=0, tiled=True)


def local(section_in, conv_weight, conv_bias, join_weight, join_bias):
    x = section_in[0, 0, 0]
    west, east = call_cols(x)
    left = shifted(east, "col", 1)
    right = shifted(west, "col", -1)
    strips = swapped(call_strips(x), "row")
    sides = swapped(call_sides(left, right, strips), "row")
    settled = call_block(strips, sides, conv_weight, conv_bias)
    out = call_join(swapped(settled, "branch"), join_weight, join_bias[None, :])
    first = [out[0]]
    for g in GEO[1:]:
        pixel_major = out[g.b].reshape(g.strip, g.cols, g.channels)
        first.append(pixel_major.transpose(2, 0, 1))
    return tuple(first)


def solution(mesh):
    in_specs = (
        P("branch", "row", "col", None, None),
        P("branch", None, None, None, None, None),
        P("branch", None, None),
        P(),
        P(),
    )
    out_specs = (P(None, ("branch", "row"), "col"),) * 4
    return jax.shard_map(local, mesh=mesh, in_specs=in_specs, out_specs=out_specs, check_vma=False)
```

time: 66.6 us -> 64.9 us (0.974)
  the two profiles are of different devices: /device:TPU:1 before, /device:TPU:25 now
where the time goes in v1:
time: 64.9 us; the launch traced here: 64.5 us
  starting transfers between devices  23.4 us (36%)
  waiting for transfers between devices  17.9 us (28%)
  Pallas kernels  11.4 us (18%)
  blocking collectives  9.07 us (14%)
  local copies, waits for them, and re-layouts  2 us (3%)
  between operations  0.7 us (1%)
    all_to_all x2, starting transfers between devices, swapped(): return lax.all_to_all(parts, axis, split_axis=0, concat_axis=0, tiled=True)  11.8 us
    ppermute x2, starting transfers between devices, shifted(): return lax.ppermute(shard, axis, pairs)  11.6 us
    all_to_all x2, waiting for transfers between devices, swapped(): return lax.all_to_all(parts, axis, split_axis=0, concat_axis=0, tiled=True)  10.9 us
    all_to_all x1, blocking collectives, swapped(): return lax.all_to_all(parts, axis, split_axis=0, concat_axis=0, tiled=True)  9.07 us
    pallas_call x1, Pallas kernels, call_block(): pl.pallas_call(block_kernel, out_shape=like((4, 384, 128))[0], in_specs=[...  7.22 us
    ppermute x2, waiting for transfers between devices, shifted(): return lax.ppermute(shard, axis, pairs)  7 us
    pallas_call x1, Pallas kernels, call_join(): pl.pallas_call(join_kernel, out_shape=like((WIDTH, 8, 128), (256, 96), (6...  2.7 us
    unnamed x10, local copies, waits for them, and re-layouts  2 us
  transfers between devices with their start and end apart: 4, of which 2 were waited for; matrix products, arithmetic and copies ran while one was open for 0% of the time, Pallas kernels for 1%

profile of v1, /device:TPU:25, one launch (start us, length us, event | category | flops | bytes accessed | tf_op | source)
XLA Modules:
  0.0 64.5 jit_solution(8489878881155589158)
XLA Ops:
  0.6 0.0 copy-start.1
  0.6 1.0 %copy-done.1 = bf16[1,1,1,48,4096]{4,3,2,1,0:T(8,128)(2,1)S(1)} copy-done((bf16[1,1,1,48,4096]{4,3,2,1,0:T(8,128)(2,1)S(1)}, bf16[1,1,1,48,4096]{4,3,2,1,0:T(8,128)(2,1)}, u32[]{:S(2)}) %copy-start.1) | copy-done | bytes 393240
  1.6 0.0 copy-start.4
  1.6 0.0 copy-start.3
  1.6 0.9 %shard_map.84 = bf16[4,48,1536]{2,1,0:T(8,128)(2,1)} custom-call(bf16[48,4096]{1,0:T(8,128)(2,1)S(1)} %bitcast.10), custom_call_target="tpu_custom_call" | custom-call | tf_op jit(solution)/shard_map/pallas_call | solution.py:368
  2.5 4.0 %all-to-all-start = ((bf16[4,48,1536]{2,1,0:T(8,128)(2,1)}), bf16[4,48,1536]{2,1,0:T(8,128)(2,1)S(1)}, u32[]{:S(2)}, u32[]{:S(2)}) async-start(bf16[4,48,1536]{2,1,0:T(8,128)(2,1)} %shard_map.84), calls=%async_computation | async-start | bytes 1179648 | tf_op jit(solution)/shard_map/all_to_all | solution.py:430
  6.5 0.0 copy-start.2
  6.5 1.0 %copy-done.2 = bf16[1,1,1,48,4096]{4,3,2,1,0:T(8,128)(2,1)S(1)} copy-done((bf16[1,1,1,48,4096]{4,3,2,1,0:T(8,128)(2,1)S(1)}, bf16[1,1,1,48,4096]{4,3,2,1,0:T(8,128)(2,1)}, u32[]{:S(2)}) %copy-start.2) | copy-done | bytes 393240
  7.5 0.5 shard_map.85
  8.0 9.7 %collective-permute-start = (bf16[48,128]{1,0:T(8,128)(2,1)S(1)}, bf16[48,128]{1,0:T(8,128)(2,1)S(1)}, u32[]{:S(2)}, u32[]{:S(2)}) collective-permute-start(bf16[48,128]{1,0:T(8,128)(2,1)S(1)} %get-tuple-element.10), channel_id=1, source_target_pairs={{0,1},{1,2},{2,3},{3,4},{4,5},{5,6},{6,7},{7,8},{8,9},{9,10},{10,1... | collective-permute-start | bytes 36872 | tf_op jit(solution)/shard_map/ppermute | solution.py:426
  17.7 1.9 %collective-permute-start.1 = (bf16[48,128]{1,0:T(8,128)(2,1)S(1)}, bf16[48,128]{1,0:T(8,128)(2,1)S(1)}, u32[]{:S(2)}, u32[]{:S(2)}) collective-permute-start(bf16[48,128]{1,0:T(8,128)(2,1)S(1)} %get-tuple-element.11), channel_id=1, source_target_pairs={{1,0},{2,1},{3,2},{4,3},{5,4},{6,5},{7,6},{8,7},{9,8},{10,9},{11,1... | collective-permute-start | bytes 36872 | tf_op jit(solution)/shard_map/ppermute | solution.py:426
  19.6 0.0 collective-permute-done.left
  19.6 7.0 %collective-permute-done.1.right = bf16[48,128]{1,0:T(8,128)(2,1)S(1)} collective-permute-done((bf16[48,128]{1,0:T(8,128)(2,1)S(1)}, bf16[48,128]{1,0:T(8,128)(2,1)S(1)}, u32[]{:S(2)}, u32[]{:S(2)}) %collective-permute-start.1) | collective-permute-done | bytes 12320 | tf_op jit(solution)/shard_map/ppermute | solution.py:426
  26.6 0.0 all-to-all-done._.strips
  26.6 0.0 copy-start
  26.6 0.1 shard_map.86
  26.8 9.1 %all_to_all.15.sides = bf16[4,48,256]{2,1,0:T(8,128)(2,1)} all-to-all(bf16[4,48,256]{2,1,0:T(8,128)(2,1)S(1)} %shard_map.86), channel_id=1, replica_groups=mesh['branch'=4,'row'=4,'col'=16] {'row'}, dimensions={0} | all-to-all | bytes 196608 | tf_op jit(solution)/shard_map/all_to_all | solution.py:430
  35.8 0.0 copy-done
  35.8 7.2 %shard_map.87 = bf16[4,384,128]{2,1,0:T(8,128)(2,1)} custom-call(bf16[4,48,1536]{2,1,0:T(8,128)(2,1)} %copy-done, bf16[4,48,256]{2,1,0:T(8,128)(2,1)} %all_to_all.15.sides, bf16[1,2,3,3,384,384]{5,4,3,2,1,0:T(8,128)(2,1)} %weight.2, f32[1,2,384]{2,1,0:T(2,128)} %bias.1), custom_call_target="tpu_custom_call" | custom-call | tf_op jit(solution)/shard_map/pallas_call | solution.py:399
  43.1 7.8 %all-to-all-start.2 = ((bf16[4,384,128]{2,1,0:T(8,128)(2,1)}), bf16[4,384,128]{2,1,0:T(8,128)(2,1)S(1)}, u32[]{:S(2)}, u32[]{:S(2)}) async-start(bf16[4,384,128]{2,1,0:T(8,128)(2,1)} %shard_map.87), calls=%async_computation.2 | async-start | bytes 786432 | tf_op jit(solution)/shard_map/all_to_all | solution.py:430
  50.9 0.0 copy-done.4
  50.9 10.9 %all-to-all-done.2.zb = bf16[4,384,128]{2,1,0:T(8,128)(2,1)S(1)} async-done(((bf16[4,384,128]{2,1,0:T(8,128)(2,1)}), bf16[4,384,128]{2,1,0:T(8,128)(2,1)S(1)}, u32[]{:S(2)}, u32[]{:S(2)}) %all-to-all-start.2) | async-done | bytes 393248 | tf_op jit(solution)/shard_map/all_to_all | solution.py:430
  61.8 0.0 copy-done.3
  61.8 2.7 %shard_map.88 = (bf16[48,8,128]{2,1,0:T(8,128)(2,1)}, bf16[256,96]{1,0:T(8,128)(2,1)}, bf16[64,192]{1,0:T(8,128)(2,1)}, bf16[16,384]{1,0:T(8,128)(2,1)}) custom-call(bf16[4,384,128]{2,1,0:T(8,128)(2,1)S(1)} %all-to-all-done.2.zb, bf16[720,720]{1,0:T(8,128)(2,1)S(1)} %copy-done.3, f32[1,720]{1,0:T(1,128)S(1)} %broadcast_in_dim.3.bias), custom_call_target="tpu_custom_call" | custom-call | tf_op jit(solution)/shard_map/pallas_call | solution.py:410
  (1 shorter events, 0.0 us)
Async XLA Ops:
  0.6 1.0 %copy-start.1 = (bf16[1,1,1,48,4096]{4,3,2,1,0:T(8,128)(2,1)S(1)}, bf16[1,1,1,48,4096]{4,3,2,1,0:T(8,128)(2,1)}, u32[]{:S(2)}) copy-start(bf16[1,1,1,48,4096]{4,3,2,1,0:T(8,128)(2,1)} %param.5) | copy-start | bytes 1179652
  1.6 49.2 %copy-start.4 = (f32[720]{0:T(1024)S(1)}, f32[720]{0:T(1024)}, u32[]{:S(2)}) copy-start(f32[720]{0:T(1024)} %param.9) | copy-start | bytes 8644
  1.6 60.2 %copy-start.3 = (bf16[720,720]{1,0:T(8,128)(2,1)S(1)}, bf16[720,720]{1,0:T(8,128)(2,1)}, u32[]{:S(2)}) copy-start(bf16[720,720]{1,0:T(8,128)(2,1)} %weight.3) | copy-start | bytes 3110404
  2.5 24.1 %all-to-all-start = ((bf16[4,48,1536]{2,1,0:T(8,128)(2,1)}), bf16[4,48,1536]{2,1,0:T(8,128)(2,1)S(1)}, u32[]{:S(2)}, u32[]{:S(2)}) async-start(bf16[4,48,1536]{2,1,0:T(8,128)(2,1)} %shard_map.84), calls=%async_computation | async-start | bytes 1179648 | tf_op jit(solution)/shard_map/all_to_all | solution.py:430
  6.5 1.0 %copy-start.2 = (bf16[1,1,1,48,4096]{4,3,2,1,0:T(8,128)(2,1)S(1)}, bf16[1,1,1,48,4096]{4,3,2,1,0:T(8,128)(2,1)}, u32[]{:S(2)}) copy-start(bf16[1,1,1,48,4096]{4,3,2,1,0:T(8,128)(2,1)} %param.5) | copy-start | bytes 1179652
  8.0 11.6 %collective-permute-start = (bf16[48,128]{1,0:T(8,128)(2,1)S(1)}, bf16[48,128]{1,0:T(8,128)(2,1)S(1)}, u32[]{:S(2)}, u32[]{:S(2)}) collective-permute-start(bf16[48,128]{1,0:T(8,128)(2,1)S(1)} %get-tuple-element.10), channel_id=1, source_target_pairs={{0,1},{1,2},{2,3},{3,4},{4,5},{5,6},{6,7},{7,8},{8,9},{9,10},{10,1... | collective-permute-start | bytes 36872 | tf_op jit(solution)/shard_map/ppermute | solution.py:426
  17.7 8.9 %collective-permute-start.1 = (bf16[48,128]{1,0:T(8,128)(2,1)S(1)}, bf16[48,128]{1,0:T(8,128)(2,1)S(1)}, u32[]{:S(2)}, u32[]{:S(2)}) collective-permute-start(bf16[48,128]{1,0:T(8,128)(2,1)S(1)} %get-tuple-element.11), channel_id=1, source_target_pairs={{1,0},{2,1},{3,2},{4,3},{5,4},{6,5},{7,6},{8,7},{9,8},{10,9},{11,1... | collective-permute-start | bytes 36872 | tf_op jit(solution)/shard_map/ppermute | solution.py:426
  26.6 9.2 %copy-start = (bf16[4,48,1536]{2,1,0:T(8,128)(2,1)}, bf16[4,48,1536]{2,1,0:T(8,128)(2,1)S(1)}, u32[]{:S(2)}) copy-start(bf16[4,48,1536]{2,1,0:T(8,128)(2,1)S(1)} %all-to-all-done._.strips) | copy-start | bytes 1769476
  43.1 18.7 %all-to-all-start.2 = ((bf16[4,384,128]{2,1,0:T(8,128)(2,1)}), bf16[4,384,128]{2,1,0:T(8,128)(2,1)S(1)}, u32[]{:S(2)}, u32[]{:S(2)}) async-start(bf16[4,384,128]{2,1,0:T(8,128)(2,1)} %shard_map.87), calls=%async_computation.2 | async-start | bytes 786432 | tf_op jit(solution)/shard_map/all_to_all | solution.py:430

commit v2 on v1

--- a/solution.py
+++ b/solution.py
@@ -42,7 +42,7 @@
 
 GEO = [Geo(b) for b in range(4)]
 MAIN = 1536
-SIDE = 256
+STEPS = (384, 640, 384, 256)
 
 
 def place():
@@ -58,15 +58,19 @@
             body(g)
 
 
-def cols_kernel(x, west, east):
+def cols_kernel(strips, far, near):
     def body(g):
-        for q in range(g.parts):
-            for y in range(g.rows):
-                lane = q * g.pixels + y * g.cols
-                at = 2 * (q * g.rows + y)
-                west[:, at : at + 2] = x[:, lane : lane + 2]
-                last = lane + g.cols - 2
-                east[:, at : at + 2] = x[:, last : last + 2]
+        size = g.parts * g.main
+        n = g.parts * g.side
+        rows = strips[:, :, 0:size].reshape(4 * WIDTH, size)
+        k = lax.broadcasted_iota(jnp.int32, (size, n), 0)
+        m = lax.broadcasted_iota(jnp.int32, (size, n), 1)
+        first = k - (m >> 1) * g.cols - (m & 1)
+        odd = place()[2] % 2
+        for out, at_end in ((far, odd), (near, 1 - odd)):
+            lane = at_end * (g.cols - 2)
+            pick = (first == lane).astype(F32).astype(BF)
+            out[:, 0:n] = jnp.dot(rows, pick, preferred_element_type=F32).astype(BF)
 
     per_branch(body)
 
@@ -88,20 +92,6 @@
                     at = q * g.main + i * g.cols
                     lane = q * g.pixels + y * g.cols
                     out[k, :, at : at + n * g.cols] = x[:, lane : lane + n * g.cols]
-
-    per_branch(body)
-
-
-def sides_kernel(left, right, _, out):
-    def body(g):
-        for k in range(4):
-            for q in range(g.parts):
-                for i, y, n in runs(g, k):
-                    at = q * g.side + 2 * i
-                    lane = 2 * (q * g.rows + y)
-                    out[k, :, at : at + 2 * n] = left[:, lane : lane + 2 * n]
-                    at += 128
-                    out[k, :, at : at + 2 * n] = right[:, lane : lane + 2 * n]
 
     per_branch(body)
 
@@ -132,53 +122,48 @@
     return jnp.where(outside, 0.0, 1.0)[0:1, :]
 
 
-def block_kernel(strips, sides, weight, bias, out, *scratch):
-    wbuf, sems, wcat, col, z0 = scratch[:5]
-    st_all = scratch[5:9]
-    xp_all = scratch[9:13]
-    hp_all = scratch[13:17]
-    zt_all = (None,) + scratch[17:20]
-    _, row_place, col_place = place()
+def side_places(g, row_place):
+    shape = (8 * g.side, g.width_x)
+    n = lax.broadcasted_iota(jnp.int32, (1, g.width_x), 1).astype(F32) - MARGIN
+    row = jnp.floor((n + 0.5) * (1.0 / g.wide))
+    rest = n - row * g.wide
+    tile = jnp.floor((rest + 0.5) * (1.0 / g.pitch))
+    x = rest - tile * g.pitch
+    y = row - 2.0 + (row_place * g.strip).astype(F32)
+    tile = tile + jnp.where(y < 0.0, -1.0, 0.0) + jnp.where(y > g.rows - 1.0, 1.0, 0.0)
+    right = x > g.cols + 1.0
+    spot = jnp.where(right, x - (g.cols + 2.0), x) + 2.0 * row + g.side * tile
+    spot = spot + jnp.where(right, 4.0 * g.side, 0.0)
+    known = (x < 2.0) | right
+    known = known & (row > -1.0) & (row < g.high) & (tile > -1.0) & (tile < 4.0)
+    spot = jnp.where(known, spot, -1.0)
+    k = lax.broadcasted_iota(jnp.int32, shape, 0).astype(F32)
+    return (k == spot).astype(F32).astype(BF)
+
+
+def prepare_kernel(strips, weight, _, *refs):
+    xp_all, wp_all, orders, places, st_all = refs[:4], refs[4:8], refs[8:11], refs[11:14], refs[14:]
+    row_place = place()[1]
 
     def body(g):
         c = g.channels
-        cl = up128(c)
-
-        def fetch(layer, dy):
-            return pltpu.make_async_copy(
-                weight.at[0, layer, dy, :, 0:c, 0:cl],
-                wbuf.at[layer, dy, :, 0:c, 0:cl],
-                sems.at[layer, dy],
-            )
-
-        for layer in range(2):
-            for dy in range(3):
-                fetch(layer, dy).start()
-
-        st, xp, hp = st_all[g.b], xp_all[g.b], hp_all[g.b]
-        ends = (0, g.main, g.main + g.side, g.main + 2 * g.side)
+        st, xp, wp = st_all[g.b], xp_all[g.b], wp_all[g.b]
 
         def fill(tile, source, i=None):
             for q in range(g.parts):
-                rows = slice(q * WIDTH, (q + 1) * WIDTH)
-                for at, ref, lane, n in (
-                    (ends[0], strips, q * g.main, g.cols),
-                    (ends[1], sides, q * g.side, 2),
-                    (ends[2], sides, 128 + q * g.side, 2),
-                ):
-                    first, size = (0, n * g.high) if i is None else (i * n, n)
-                    at = tile * g.slot + at + first
-                    if 0 <= source < 4:
-                        piece = ref[source, :, lane + first : lane + first + size]
-                    else:
-                        piece = jnp.zeros((WIDTH, size), BF)
-                    st[rows, at : at + size] = piece
+                first, size = (0, g.main) if i is None else (i * g.cols, g.cols)
+                at = tile * g.slot + first
+                lane = q * g.main + first
+                if 0 <= source < 4:
+                    piece = strips[source, :, lane : lane + size]
+                else:
+                    piece = jnp.zeros((WIDTH, size), BF)
+                st[q * WIDTH : (q + 1) * WIDTH, at : at + size] = piece
 
         for tile in range(4):
             fill(tile, tile)
         for i in range(g.high):
-            low = [k for k in range(4) if k * g.strip - 2 + i < 0]
-            high = [k for k in range(4) if k * g.strip - 2 + i >= g.rows]
+            low, high = outside(g, i)
             if low:
 
                 @pl.when(row_place <= max(low))
@@ -194,17 +179,93 @@
                         fill(tile, tile + 1, i)
 
         if g.b:
-            st[...] = jnp.dot(channel_order(g), st[...], preferred_element_type=F32).astype(BF)
+            order = channel_order(g)
+            orders[g.b - 1][...] = order
+            places[g.b - 1][...] = side_places(g, row_place)
+            st[...] = jnp.dot(order, st[...], preferred_element_type=F32).astype(BF)
+        xp[...] = jnp.zeros_like(xp)
         for i in range(g.high):
             for tile in range(4):
+                to = MARGIN + i * g.wide + tile * g.pitch + 2
+                lane = tile * g.slot + i * g.cols
+                xp[:, to : to + g.cols] = st[:, lane : lane + g.cols]
+        for layer in range(2):
+            for dy in range(3):
+                for dx in range(3):
+                    t = 3 * dy + dx
+                    wp[layer, :, c * t : c * (t + 1)] = weight[0, layer, dy, dx, 0:c, 0:c]
+
+    per_branch(body)
+
+
+def outside(g, i):
+    low = [k for k in range(4) if k * g.strip - 2 + i < 0]
+    high = [k for k in range(4) if k * g.strip - 2 + i >= g.rows]
+    return low, high
+
+
+def block_kernel(far, near, bias, *refs):
+    xp_all, wp_all, orders, places = refs[:4], refs[4:8], refs[8:11], refs[11:14]
+    out, refs = refs[14], refs[15:]
+    xs_all, col_all, hp_all, st_all, (z0,) = refs[:4], refs[4:8], refs[8:12], refs[12:15], refs[15:16]
+    zt_all, left, right = refs[16:19], refs[19], refs[20]
+    _, row_place, col_place = place()
+
+    @pl.when(col_place % 2 == 0)
+    def _():
+        left[...] = far[...]
+        right[...] = near[...]
+
+    @pl.when(col_place % 2 == 1)
+    def _():
+        left[...] = near[...]
+        right[...] = far[...]
+
+    def body(g):
+        c = g.channels
+        cl = up128(c)
+        xp, hp, wp, col = xs_all[g.b], hp_all[g.b], wp_all[g.b], col_all[g.b]
+        if g.b == 0:
+            xp[...] = xp_all[0][...]
+
+            def sides(i, tile, source):
                 at = MARGIN + i * g.wide + tile * g.pitch
-                base = tile * g.slot
-                for to, lane, n in (
-                    (at, base + ends[1] + 2 * i, 2),
-                    (at + 2, base + i * g.cols, g.cols),
-                    (at + 2 + g.cols, base + ends[2] + 2 * i, 2),
-                ):
-                    xp[:, to : to + n] = st[:, lane : lane + n]
+                for ref, to in ((left, at), (right, at + 2 + g.cols)):
+                    if 0 <= source < 4:
+                        piece = ref[source * WIDTH : (source + 1) * WIDTH, 2 * i : 2 * i + 2]
+                    else:
+                        piece = jnp.zeros((WIDTH, 2), BF)
+                    xp[:, to : to + 2] = piece
+
+            for i in range(g.high):
+                low, high = outside(g, i)
+                for tile in range(4):
+                    sides(i, tile, tile)
+                if low:
+
+                    @pl.when(row_place <= max(low))
+                    def _(i=i):
+                        for tile in range(4):
+                            sides(i, tile, tile - 1)
+
+                if high:
+
+                    @pl.when(row_place >= min(high))
+                    def _(i=i):
+                        for tile in range(4):
+                            sides(i, tile, tile + 1)
+
+        else:
+            st = st_all[g.b - 1]
+            for q in range(g.parts):
+                for s, ref in enumerate((left, right)):
+                    for tile in range(4):
+                        at = (4 * s + tile) * g.side
+                        st[q * WIDTH : (q + 1) * WIDTH, at : at + g.side] = ref[
+                            tile * WIDTH : (tile + 1) * WIDTH, q * g.side : (q + 1) * g.side
+                        ]
+            stacked = nn(orders[g.b - 1][...], st[...]).astype(BF)
+            xp[...] = xp_all[g.b][...] + nn(stacked, places[g.b - 1][...]).astype(BF)
 
         mask = inside(g, row_place, col_place)
 
@@ -213,32 +274,15 @@
             return wide.T[0:c, 0:1]
 
         def conv(layer, source, n, finish):
-            total = None
             for dy in range(3):
-                fetch(layer, dy).wait()
                 for dx in range(3):
                     lane = MARGIN + dy * g.wide + dx - 1
-                    if g.b == 0:
-                        t = 3 * dy + dx
-                        wcat[:, WIDTH * t : WIDTH * (t + 1)] = wbuf[layer, dy, dx, 0:c, 0:c]
-                        col[WIDTH * t : WIDTH * (t + 1), 0:n] = source[:, lane : lane + n]
-                    else:
-                        term = jnp.dot(
-                            wbuf[layer, dy, dx, 0:c, 0:c],
-                            source[:, lane : lane + n],
-                            preferred_element_type=F32,
-                        )
-                        total = term if total is None else total + term
-            if g.b:
-                finish(0, n, total)
-                return
-            for at in range(0, n, 384):
-                size = min(384, n - at)
-                finish(
-                    at,
-                    size,
-                    jnp.dot(wcat[...], col[:, at : at + size], preferred_element_type=F32),
-                )
+                    t = 3 * dy + dx
+                    col[c * t : c * (t + 1), 0:n] = source[:, lane : lane + n]
+            step = STEPS[g.b]
+            for at in range(0, n, step):
+                size = min(step, n - at)
+                finish(at, size, nn(wp[layer], col[:, at : at + size]))
 
         bias0 = column(0)
 
@@ -257,7 +301,7 @@
             if g.b == 0:
                 z0[:, at : at + size] = z.astype(BF)
             else:
-                zt_all[g.b][...] = z.T
+                zt_all[g.b - 1][at : at + size, :] = z.T
 
         conv(1, hp, g.n2, finish_second)
 
@@ -267,7 +311,7 @@
                 if g.b == 0:
                     out[tile, i * WIDTH : (i + 1) * WIDTH, :] = z0[:, at : at + g.cols]
                     continue
-                values = zt_all[g.b][at : at + g.cols, :].astype(BF)
+                values = zt_all[g.b - 1][at : at + g.cols, :].astype(BF)
                 for m in range(cl // 128):
                     r = (m * g.strip + i) * g.cols
                     lanes = min(128, c - 128 * m)
@@ -354,14 +398,14 @@
     return tuple(jax.ShapeDtypeStruct(s, BF) for s in shapes)
 
 
-def call_cols(x):
+def call_cols(strips):
     return pl.pallas_call(
         cols_kernel,
-        out_shape=like((WIDTH, 128), (WIDTH, 128)),
+        out_shape=like((4 * WIDTH, 128), (4 * WIDTH, 128)),
         in_specs=[VMEM],
         out_specs=(VMEM, VMEM),
         compiler_params=params(),
-    )(x)
+    )(strips)
 
 
 def call_strips(x):
@@ -374,36 +418,43 @@
     )(x)
 
 
-def call_sides(left, right, after):
+def prepared_shapes():
+    shapes = [(g.channels, g.width_x) for g in GEO]
+    shapes += [(2, g.channels, 9 * g.channels) for g in GEO]
+    shapes += [(g.channels, g.channels) for g in GEO[1:]]
+    shapes += [(8 * g.side, g.width_x) for g in GEO[1:]]
+    return shapes
+
+
+def call_prepare(strips, weight, after):
+    shapes = prepared_shapes()
     return pl.pallas_call(
-        sides_kernel,
-        out_shape=like((4, WIDTH, SIDE))[0],
-        in_specs=[VMEM] * 2 + [pl.BlockSpec(memory_space=pl.ANY)],
-        out_specs=VMEM,
+        prepare_kernel,
+        out_shape=like(*shapes),
+        in_specs=[VMEM, VMEM, pl.BlockSpec(memory_space=pl.ANY)],
+        out_specs=(VMEM,) * len(shapes),
+        scratch_shapes=[pltpu.VMEM((g.channels, 4 * g.slot), BF) for g in GEO],
         compiler_params=params(),
-    )(left, right, after)
-
-
-def call_block(strips, sides, weight, bias):
-    scratch = [
-        pltpu.VMEM((2, 3, 3, 384, 384), BF),
-        pltpu.SemaphoreType.DMA((2, 3)),
-        pltpu.VMEM((WIDTH, 9 * WIDTH), BF),
-        pltpu.VMEM((9 * WIDTH, GEO[0].n1), BF),
-        pltpu.VMEM((WIDTH, GEO[0].n2), BF),
-    ]
-    scratch += [pltpu.VMEM((g.channels, 4 * g.slot), BF) for g in GEO]
-    scratch += [pltpu.VMEM((g.channels, g.width_x), BF) for g in GEO]
+        cost_estimate=pl.CostEstimate(flops=10**9, bytes_accessed=12 * 2**20, transcendentals=0),
+    )(strips, weight, after)
+
+
+def call_block(far, near, bias, prepared):
+    scratch = [pltpu.VMEM((g.channels, g.width_x), BF) for g in GEO]
+    scratch += [pltpu.VMEM((9 * g.channels, g.n1), BF) for g in GEO]
     scratch += [pltpu.VMEM((g.channels, g.width_h), BF) for g in GEO]
+    scratch += [pltpu.VMEM((g.channels, 8 * g.side), BF) for g in GEO[1:]]
+    scratch += [pltpu.VMEM((WIDTH, GEO[0].n2), BF)]
     scratch += [pltpu.VMEM((g.n2, g.channels), F32) for g in GEO[1:]]
+    scratch += [pltpu.VMEM((4 * WIDTH, 128), BF)] * 2
     return pl.pallas_call(
         block_kernel,
         out_shape=like((4, 384, 128))[0],
-        in_specs=[VMEM, VMEM, pl.BlockSpec(memory_space=pltpu.HBM), VMEM],
+        in_specs=[VMEM] * (3 + len(prepared)),
         out_specs=VMEM,
         scratch_shapes=scratch,
-        compiler_params=params(60),
-    )(strips, sides, weight, bias)
+        compiler_params=params(),
+    )(far, near, bias, *prepared)
 
 
 def call_join(received, weight, bias):
@@ -420,10 +471,12 @@
     )(received, weight, bias)
 
 
-def shifted(shard, axis, by):
-    size = lax.axis_size(axis)
-    pairs = [(i, i + by) for i in range(size) if 0 <= i + by < size]
-    return lax.ppermute(shard, axis, pairs)
+def paired(shard, first):
+    size = lax.axis_size("col")
+    pairs = []
+    for c in range(first, size - 1, 2):
+        pairs += [(c, c + 1), (c + 1, c)]
+    return lax.ppermute(shard, "col", pairs)
 
 
 def swapped(parts, axis):
@@ -432,12 +485,10 @@
 
 def local(section_in, conv_weight, conv_bias, join_weight, join_bias):
     x = section_in[0, 0, 0]
-    west, east = call_cols(x)
-    left = shifted(east, "col", 1)
-    right = shifted(west, "col", -1)
     strips = swapped(call_strips(x), "row")
-    sides = swapped(call_sides(left, right, strips), "row")
-    settled = call_block(strips, sides, conv_weight, conv_bias)
+    far, near = call_cols(strips)
+    prepared = call_prepare(strips, conv_weight, far)
+    settled = call_block(paired(far, 1), paired(near, 0), conv_bias, prepared)
     out = call_join(swapped(settled, "branch"), join_weight, join_bias[None, :])
     first = [out[0]]
     for g in GEO[1:]:

time: 64.9 us -> 54.4 us (0.84)
  the two profiles are of different devices: /device:TPU:25 before, /device:TPU:16 now
where the time goes in v2:
time: 54.4 us; the launch traced here: 54 us
  blocking collectives  14.3 us (26%)
  starting transfers between devices  14 us (26%)
  Pallas kernels  12.2 us (22%)
  waiting for transfers between devices  11.9 us (22%)
  local copies, waits for them, and re-layouts  1.01 us (2%)
  between operations  0.72 us (1%)
    all_to_all x1, blocking collectives, swapped(): return lax.all_to_all(parts, axis, split_axis=0, concat_axis=0, tiled=True)  14.3 us
    all_to_all x1, waiting for transfers between devices, swapped(): return lax.all_to_all(parts, axis, split_axis=0, concat_axis=0, tiled=True)  11.9 us
    ppermute x2, starting transfers between devices, paired(): return lax.ppermute(shard, 'col', pairs)  9.3 us
    pallas_call x1, Pallas kernels, call_block(): pl.pallas_call(block_kernel, out_shape=like((4, 384, 128))[0], in_specs=[...  5.88 us
    all_to_all x1, starting transfers between devices, swapped(): return lax.all_to_all(parts, axis, split_axis=0, concat_axis=0, tiled=True)  4.72 us
    pallas_call x1, Pallas kernels, call_prepare(): pl.pallas_call(prepare_kernel, out_shape=like(*shapes), in_specs=[VMEM, V...  3.02 us
    pallas_call x1, Pallas kernels, call_join(): pl.pallas_call(join_kernel, out_shape=like((WIDTH, 8, 128), (256, 96), (6...  2.7 us
  transfers between devices with their start and end apart: 3, of which 1 were waited for; matrix products, arithmetic and copies ran while one was open for 0% of the time, Pallas kernels for 6%

profile of v2, /device:TPU:16, one launch (start us, length us, event | category | flops | bytes accessed | tf_op | source)
XLA Modules:
  0.0 54.0 jit_solution(1345218951891799984)
XLA Ops:
  0.6 0.0 copy-start.1
  0.6 1.0 %copy-done.1 = bf16[1,1,1,48,4096]{4,3,2,1,0:T(8,128)(2,1)S(1)} copy-done((bf16[1,1,1,48,4096]{4,3,2,1,0:T(8,128)(2,1)S(1)}, bf16[1,1,1,48,4096]{4,3,2,1,0:T(8,128)(2,1)}, u32[]{:S(2)}) %copy-start.1) | copy-done | bytes 393240
  1.6 0.0 copy-start.2
  1.6 0.1 shard_map.84
  1.7 14.3 %all_to_all.10.strips = bf16[4,48,1536]{2,1,0:T(8,128)(2,1)S(1)} all-to-all(bf16[4,48,1536]{2,1,0:T(8,128)(2,1)S(1)} %shard_map.84), channel_id=1, replica_groups=mesh['branch'=4,'row'=4,'col'=16] {'row'}, dimensions={0} | all-to-all | bytes 1179648 | tf_op jit(solution)/shard_map/all_to_all | solution.py:483
  16.0 0.5 shard_map.85
  16.5 6.9 %collective-permute-start = (bf16[192,128]{1,0:T(8,128)(2,1)S(1)}, bf16[192,128]{1,0:T(8,128)(2,1)S(1)}, u32[]{:S(2)}, u32[]{:S(2)}) collective-permute-start(bf16[192,128]{1,0:T(8,128)(2,1)S(1)} %get-tuple-element.24._), channel_id=1, source_target_pairs={{1,2},{2,1},{3,4},{4,3},{5,6},{6,5},{7,8},{8,7},{9,10},{10,9},{11,... | collective-permute-start | bytes 147464 | tf_op jit(solution)/shard_map/ppermute | solution.py:479
  23.4 2.4 %collective-permute-start.1 = (bf16[192,128]{1,0:T(8,128)(2,1)S(1)}, bf16[192,128]{1,0:T(8,128)(2,1)S(1)}, u32[]{:S(2)}, u32[]{:S(2)}) collective-permute-start(bf16[192,128]{1,0:T(8,128)(2,1)S(1)} %get-tuple-element.25), channel_id=1, source_target_pairs={{0,1},{1,0},{2,3},{3,2},{4,5},{5,4},{6,7},{7,6},{8,9},{9,8},{10,11... | collective-permute-start | bytes 147464 | tf_op jit(solution)/shard_map/ppermute | solution.py:479
  25.8 3.0 %shard_map.86 = (bf16[48,6656]{1,0:T(8,128)(2,1)S(1)}, bf16[96,2432]{1,0:T(8,128)(2,1)S(1)}, bf16[192,1152]{1,0:T(8,128)(2,1)S(1)}, bf16[384,640]{1,0:T(8,128)(2...) custom-call(bf16[4,48,1536]{2,1,0:T(8,128)(2,1)S(1)} %all_to_all.10., ...), custom_call_target="tpu_custom_call" | custom-call | flops 1000000000 | bytes 12582912 | tf_op jit(solution)/shard_map/pallas_call | solution.py:431
  28.8 0.0 collective-permute-done.far
  28.8 0.0 collective-permute-done.1.near
  28.8 0.0 copy-done.2
  28.8 0.0 copy-start.3
  28.9 0.0 copy-start
  28.9 5.9 %shard_map.87 = bf16[4,384,128]{2,1,0:T(8,128)(2,1)} custom-call(bf16[192,128]{1,0:T(8,128)(2,1)S(1)} %collective-permute-done.far, bf16[192,128]{1,0:T(8,128)(2,1)S(1)} %collective-permute-done.1.near, f32[1,2,384]{2,1,0:T(2,128)S(1)} %copy-done.2, bf16[48,6656]{1,0:T(8,128)(2,1)S(1)} %get-tuple-element.26.refs_0_, ...), custom_call_target="tpu_custom_call" | custom-call | tf_op jit(solution)/shard_map/pallas_call | solution.py:450
  34.7 4.7 %all-to-all-start.1 = ((bf16[4,384,128]{2,1,0:T(8,128)(2,1)}), bf16[4,384,128]{2,1,0:T(8,128)(2,1)S(1)}, u32[]{:S(2)}, u32[]{:S(2)}) async-start(bf16[4,384,128]{2,1,0:T(8,128)(2,1)} %shard_map.87), calls=%async_computation.1 | async-start | bytes 786432 | tf_op jit(solution)/shard_map/all_to_all | solution.py:483
  39.5 0.0 copy-done.3
  39.5 11.9 %all-to-all-done.1.zb = bf16[4,384,128]{2,1,0:T(8,128)(2,1)S(1)} async-done(((bf16[4,384,128]{2,1,0:T(8,128)(2,1)}), bf16[4,384,128]{2,1,0:T(8,128)(2,1)S(1)}, u32[]{:S(2)}, u32[]{:S(2)}) %all-to-all-start.1) | async-done | bytes 393248 | tf_op jit(solution)/shard_map/all_to_all | solution.py:483
  51.3 0.0 copy-done
  51.3 2.7 %shard_map.88 = (bf16[48,8,128]{2,1,0:T(8,128)(2,1)}, bf16[256,96]{1,0:T(8,128)(2,1)}, bf16[64,192]{1,0:T(8,128)(2,1)}, bf16[16,384]{1,0:T(8,128)(2,1)}) custom-call(bf16[4,384,128]{2,1,0:T(8,128)(2,1)S(1)} %all-to-all-done.1.zb, bf16[720,720]{1,0:T(8,128)(2,1)S(1)} %copy-done, f32[1,720]{1,0:T(1,128)S(1)} %broadcast_in_dim.3.bias), custom_call_target="tpu_custom_call" | custom-call | tf_op jit(solution)/shard_map/pallas_call | solution.py:461
  (1 shorter events, 0.0 us)
Async XLA Ops:
  0.6 1.0 %copy-start.1 = (bf16[1,1,1,48,4096]{4,3,2,1,0:T(8,128)(2,1)S(1)}, bf16[1,1,1,48,4096]{4,3,2,1,0:T(8,128)(2,1)}, u32[]{:S(2)}) copy-start(bf16[1,1,1,48,4096]{4,3,2,1,0:T(8,128)(2,1)} %param.5) | copy-start | bytes 1179652
  1.6 27.2 %copy-start.2 = (f32[1,2,384]{2,1,0:T(2,128)S(1)}, f32[1,2,384]{2,1,0:T(2,128)}, u32[]{:S(2)}) copy-start(f32[1,2,384]{2,1,0:T(2,128)} %bias.1) | copy-start | bytes 9220
  16.5 12.3 %collective-permute-start = (bf16[192,128]{1,0:T(8,128)(2,1)S(1)}, bf16[192,128]{1,0:T(8,128)(2,1)S(1)}, u32[]{:S(2)}, u32[]{:S(2)}) collective-permute-start(bf16[192,128]{1,0:T(8,128)(2,1)S(1)} %get-tuple-element.24._), channel_id=1, source_target_pairs={{1,2},{2,1},{3,4},{4,3},{5,6},{6,5},{7,8},{8,7},{9,10},{10,9},{11,... | collective-permute-start | bytes 147464 | tf_op jit(solution)/shard_map/ppermute | solution.py:479
  23.4 5.4 %collective-permute-start.1 = (bf16[192,128]{1,0:T(8,128)(2,1)S(1)}, bf16[192,128]{1,0:T(8,128)(2,1)S(1)}, u32[]{:S(2)}, u32[]{:S(2)}) collective-permute-start(bf16[192,128]{1,0:T(8,128)(2,1)S(1)} %get-tuple-element.25), channel_id=1, source_target_pairs={{0,1},{1,0},{2,3},{3,2},{4,5},{5,4},{6,7},{7,6},{8,9},{9,8},{10,11... | collective-permute-start | bytes 147464 | tf_op jit(solution)/shard_map/ppermute | solution.py:479
  28.8 10.6 %copy-start.3 = (f32[720]{0:T(1024)S(1)}, f32[720]{0:T(1024)}, u32[]{:S(2)}) copy-start(f32[720]{0:T(1024)} %param.9) | copy-start | bytes 8644
  28.9 22.5 %copy-start = (bf16[720,720]{1,0:T(8,128)(2,1)S(1)}, bf16[720,720]{1,0:T(8,128)(2,1)}, u32[]{:S(2)}) copy-start(bf16[720,720]{1,0:T(8,128)(2,1)} %weight.3) | copy-start | bytes 3110404
  34.7 16.6 %all-to-all-start.1 = ((bf16[4,384,128]{2,1,0:T(8,128)(2,1)}), bf16[4,384,128]{2,1,0:T(8,128)(2,1)S(1)}, u32[]{:S(2)}, u32[]{:S(2)}) async-start(bf16[4,384,128]{2,1,0:T(8,128)(2,1)} %shard_map.87), calls=%async_computation.1 | async-start | bytes 786432 | tf_op jit(solution)/shard_map/all_to_all | solution.py:483

commit v3 on v1

v3 whole, which is shorter than its diff:
```python
import jax
import jax.numpy as jnp
from jax import lax
from jax.experimental import pallas as pl
from jax.experimental.pallas import tpu as pltpu
from jax.sharding import PartitionSpec as P

WIDTH = 48
TH = 32
TW = 128
MARGIN = 128
BF = jnp.bfloat16
F32 = jnp.float32
VMEM = pl.BlockSpec(memory_space=pltpu.VMEM)


def up128(n):
    return -(-n // 128) * 128


class Geo:
    def __init__(self, b):
        self.b = b
        self.parts = 1 << b
        self.channels = WIDTH << b
        self.rows = TH >> b
        self.cols = TW >> b
        self.pixels = self.rows * self.cols
        self.strip = self.rows // 4
        self.high = self.strip + 4
        self.pitch = self.cols + 4
        self.padded = up128(self.rows * self.pitch)
        self.sides = 4 * self.rows
        self.slot = up128(self.high * self.pitch + 2)
        self.blocks = self.slot // 128
        self.tile_h = (self.strip + 2) * self.pitch
        self.tile_z = self.strip * self.pitch
        self.n1 = up128(4 * self.tile_h)
        self.n2 = up128(4 * self.tile_z)
        self.width_h = up128(2 * MARGIN + self.n1)
        self.start = ((1 << b) - 1) * WIDTH


GEO = [Geo(b) for b in range(4)]
SLOT_ROWS = 624
STEPS = (384, 640, 384, 256)


def place():
    return lax.axis_index("branch"), lax.axis_index("row"), lax.axis_index("col")


def per_branch(body):
    branch = place()[0]
    for g in GEO:

        @pl.when(branch == g.b)
        def _(g=g):
            body(g)


def cols_kernel(x, far, near, west, east):
    def body(g):
        for q in range(g.parts):
            for y in range(g.rows):
                lane = q * g.pixels + y * g.cols
                at = 2 * (q * g.rows + y)
                west[:, at : at + 2] = x[:, lane : lane + 2]
                last = lane + g.cols - 2
                east[:, at : at + 2] = x[:, last : last + 2]

    per_branch(body)
    odd = place()[2] % 2

    @pl.when(odd == 0)
    def _():
        far[...] = west[...]
        near[...] = east[...]

    @pl.when(odd == 1)
    def _():
        far[...] = east[...]
        near[...] = west[...]


def channel_order(g):
    out = lax.broadcasted_iota(jnp.int32, (g.channels, g.channels), 0)
    k = lax.broadcasted_iota(jnp.int32, (g.channels, g.channels), 1)
    part = jnp.zeros_like(k)
    for m in range(1, g.parts):
        part = part + (k >= WIDTH * m).astype(jnp.int32)
    at = (k - WIDTH * part) * g.parts + part
    return (at == out).astype(F32).astype(BF)


def side_places(g):
    n = lax.broadcasted_iota(jnp.int32, (1, g.padded), 1).astype(F32)
    y = jnp.floor((n + 0.5) * (1.0 / g.pitch))
    x = n - y * g.pitch
    right = x > g.cols + 1.0
    spot = 2.0 * y + jnp.where(right, x - (g.cols + 2.0) + 2.0 * g.rows, x)
    spot = jnp.where(((x < 2.0) | right) & (y < g.rows), spot, -1.0)
    k = lax.broadcasted_iota(jnp.int32, (g.sides, g.padded), 0).astype(F32)
    return (k == spot).astype(F32).astype(BF)


def prepare_kernel(x, weight, _, *refs):
    xp_all, wp_all, places, orders = refs[:4], refs[4:8], refs[8:12], (None,) + refs[12:15]
    st_all = (x,) + refs[15:18]

    def body(g):
        c = g.channels
        st, xp, wp = st_all[g.b], xp_all[g.b], wp_all[g.b]
        places[g.b][...] = side_places(g)
        if g.b:
            order = channel_order(g)
            orders[g.b][...] = order
            for q in range(g.parts):
                st[q * WIDTH : (q + 1) * WIDTH, :] = x[:, q * g.pixels : (q + 1) * g.pixels]
            st[...] = nn(order, st[...]).astype(BF)
        xp[...] = jnp.zeros_like(xp)
        for y in range(g.rows):
            to = y * g.pitch + 2
            xp[:, to : to + g.cols] = st[:, y * g.cols : (y + 1) * g.cols]
        for layer in range(2):
            for dy in range(3):
                for dx in range(3):
                    t = 3 * dy + dx
                    wp[layer, :, c * t : c * (t + 1)] = weight[0, layer, dy, dx, 0:c, 0:c]

    per_branch(body)


def runs(g, k):
    i = 0
    while i < g.high:
        y = (k * g.strip - 2 + i) % g.rows
        n = min(g.high - i, g.rows - y)
        yield i, y, n
        i += n


def strips_kernel(far, near, *refs):
    xp_all, places, orders, out = refs[:4], refs[4:8], (None,) + refs[8:11], refs[11]
    left, right = refs[12:14]
    st_all, xf_all, slot_all = refs[14:18], refs[18:22], refs[22:26]
    odd = place()[2] % 2

    @pl.when(odd == 0)
    def _():
        left[...] = far[...]
        right[...] = near[...]

    @pl.when(odd == 1)
    def _():
        left[...] = near[...]
        right[...] = far[...]

    def body(g):
        c, n = g.channels, 2 * g.rows
        st, xf, slot = st_all[g.b], xf_all[g.b], slot_all[g.b]
        for q in range(g.parts):
            for s, ref in enumerate((left, right)):
                st[q * WIDTH : (q + 1) * WIDTH, s * n : (s + 1) * n] = ref[:, q * n : (q + 1) * n]
        stacked = st[...]
        if g.b:
            stacked = nn(orders[g.b][...], stacked).astype(BF)
        xf[...] = xp_all[g.b][...] + nn(stacked, places[g.b][...]).astype(BF)
        for k in range(4):
            for i, y, rows in runs(g, k):
                at, lane, size = 1 + i * g.pitch, y * g.pitch, rows * g.pitch
                slot[:, at : at + size] = xf[:, lane : lane + size]
            for m in range(g.blocks):
                out[k, m * c : (m + 1) * c, :] = slot[:, 128 * m : 128 * (m + 1)]

    per_branch(body)


def inside(g, row_place, col_place):
    p = lax.broadcasted_iota(jnp.int32, (8, g.n1), 1).astype(F32)
    tile = jnp.floor((p + 0.5) * (1.0 / g.tile_h))
    rest = p - tile * g.tile_h
    row = jnp.floor((rest + 0.5) * (1.0 / g.pitch))
    x = rest - row * g.pitch
    y = row - 1.0 + (row_place * g.strip).astype(F32)
    out = (
        ((tile == 0.0) & (y < 0.0))
        | ((tile == 3.0) & (y > g.rows - 1.0))
        | ((x == 1.0) & (col_place == 0))
        | ((x == g.cols + 2.0) & (col_place == 15))
    )
    return jnp.where(out, 0.0, 1.0)[0:1, :]


def block_kernel(strips, bias, *refs):
    wp_all, out = refs[:4], refs[4]
    xs_all, col_all, hp_all, own_all = refs[5:9], refs[9:13], refs[13:17], refs[17:21]
    z0, zt_all = refs[21], (None,) + refs[22:25]
    _, row_place, col_place = place()

    def body(g):
        c = g.channels
        cl = up128(c)
        xs, hp, wp, col, own = xs_all[g.b], hp_all[g.b], wp_all[g.b], col_all[g.b], own_all[g.b]
        for tile in range(4):
            for m in range(g.blocks):
                xs[tile, :, 128 * m : 128 * (m + 1)] = strips[tile, m * c : (m + 1) * c, :]
        for i in range(g.high):
            lanes = slice(1 + i * g.pitch, 1 + (i + 1) * g.pitch)
            low = [k for k in range(4) if k * g.strip - 2 + i < 0]
            high = [k for k in range(4) if k * g.strip - 2 + i >= g.rows]
            if low:

                @pl.when(row_place <= max(low))
                def _(lanes=lanes):
                    for tile in (3, 2, 1):
                        xs[tile, :, lanes] = xs[tile - 1, :, lanes]
                    xs[0, :, lanes] = jnp.zeros((c, g.pitch), BF)

            if high:

                @pl.when(row_place >= min(high))
                def _(lanes=lanes):
                    for tile in (0, 1, 2):
                        xs[tile, :, lanes] = xs[tile + 1, :, lanes]
                    xs[3, :, lanes] = jnp.zeros((c, g.pitch), BF)

        for tile in range(4):
            lane = 1 + 2 * g.pitch
            own[:, tile * g.tile_z : (tile + 1) * g.tile_z] = xs[tile, :, lane : lane + g.tile_z]

        mask = inside(g, row_place, col_place)

        def column(layer):
            wide = jnp.broadcast_to(bias[0, layer : layer + 1, :], (8, 8 * WIDTH))
            return wide.T[0:c, 0:1]

        def conv(layer, view, size, n, finish):
            for dy in range(3):
                for dx in range(3):
                    t = 3 * dy + dx
                    for tile in range(4):
                        col[c * t : c * (t + 1), tile * size : (tile + 1) * size] = view(
                            tile, dy * g.pitch + dx
                        )
            step = STEPS[g.b]
            for at in range(0, n, step):
                width = min(step, n - at)
                finish(at, width, nn(wp[layer], col[:, at : at + width]))

        bias0 = column(0)

        def finish_first(at, size, total):
            h = jnp.maximum(total + bias0, 0.0) * mask[:, at : at + size]
            hp[:, MARGIN + at : MARGIN + at + size] = h.astype(BF)

        conv(0, lambda tile, lane: xs[tile, :, lane : lane + g.tile_h], g.tile_h, g.n1, finish_first)

        bias1 = column(1)

        def finish_second(at, size, total):
            z = jnp.maximum(total + bias1 + own[:, at : at + size].astype(F32), 0.0)
            if g.b == 0:
                z0[:, at : at + size] = z.astype(BF)
            else:
                zt_all[g.b][at : at + size, :] = z.T

        def hidden(tile, lane):
            lane += MARGIN + tile * g.tile_h - 1
            return hp[:, lane : lane + g.tile_z]

        conv(1, hidden, g.tile_z, g.n2, finish_second)

        for tile in range(4):
            for i in range(g.strip):
                at = tile * g.tile_z + i * g.pitch + 2
                if g.b == 0:
                    out[tile, i * WIDTH : (i + 1) * WIDTH, :] = z0[:, at : at + g.cols]
                    continue
                values = zt_all[g.b][at : at + g.cols, :].astype(BF)
                for m in range(cl // 128):
                    r = (m * g.strip + i) * g.cols
                    lanes = min(128, c - 128 * m)
                    out[tile, r : r + g.cols, 0:lanes] = values[:, 128 * m : 128 * m + lanes]

    per_branch(body)


def repeat_map(j, i):
    gj, gi = GEO[j], GEO[i]
    shape = (gj.pixels // 4, gi.pixels // 4)
    fine = lax.broadcasted_iota(jnp.int32, shape, 0)
    coarse = lax.broadcasted_iota(jnp.int32, shape, 1)
    return cover(fine, coarse, gj, i - j)


def cover(fine, coarse, g, d):
    bits = 7 - g.b
    y = fine >> bits
    x = fine & (g.cols - 1)
    return (((y >> d) << (bits - d)) + (x >> d) == coarse).astype(F32).astype(BF)


def repeat_map_t(j, i):
    gj, gi = GEO[j], GEO[i]
    shape = (gi.pixels // 4, gj.pixels // 4)
    coarse = lax.broadcasted_iota(jnp.int32, shape, 0)
    fine = lax.broadcasted_iota(jnp.int32, shape, 1)
    return cover(fine, coarse, gj, i - j)


def nn(a, b):
    return jnp.dot(a, b, preferred_element_type=F32)


def nt(a, b):
    return lax.dot_general(a, b, (((1,), (1,)), ((), ())), preferred_element_type=F32)


def join_kernel(zb, weight, bias, out0, out1, out2, out3, z0s, s0):
    for y in range(8):
        z0s[:, 128 * y : 128 * (y + 1)] = zb[0, WIDTH * y : WIDTH * (y + 1), :]
    z = [
        z0s[...],
        zb[1, 0:256, 0:96],
        jnp.concatenate([zb[2, 0:64, :], zb[2, 64:128, 0:64]], axis=1),
        jnp.concatenate([zb[3, 0:16, :], zb[3, 16:32, :], zb[3, 32:48, :]], axis=1),
    ]

    def block(j, i):
        gj, gi = GEO[j], GEO[i]
        return weight[gj.start : gj.start + gj.channels, gi.start : gi.start + gi.channels]

    total = None
    for i in (1, 2, 3):
        term = nn(nt(block(0, i), z[i]).astype(BF), repeat_map_t(0, i))
        total = term if total is None else total + term
    wide = jnp.broadcast_to(bias[:, 0:WIDTH], (8, WIDTH))
    total = jnp.maximum(total + z[0].astype(F32) + wide.T[:, 0:1], 0.0)
    for y in range(8):
        s0[:, y, :] = total[:, 128 * y : 128 * (y + 1)]
    out0[...] = s0[...].astype(BF)

    for j, out in ((1, out1), (2, out2), (3, out3)):
        g = GEO[j]
        total = z[j].astype(F32) + bias[:, g.start : g.start + g.channels]
        for i in range(4):
            if i == j:
                continue
            if i < j:
                sums = (nt if i == 0 else nn)(repeat_map_t(i, j), z[i])
                mean = (sums * (0.25 ** (j - i))).astype(BF)
                total = total + nt(mean, block(j, i)).astype(BF).astype(F32)
            else:
                total = total + nn(repeat_map(j, i), nt(z[i], block(j, i)).astype(BF))
        out[...] = jnp.maximum(total, 0.0).astype(BF)


def params(mib=24):
    return pltpu.CompilerParams(vmem_limit_bytes=mib * 1024 * 1024)


def like(*shapes):
    return tuple(jax.ShapeDtypeStruct(s, BF) for s in shapes)


def call_cols(x):
    return pl.pallas_call(
        cols_kernel,
        out_shape=like((WIDTH, 128), (WIDTH, 128)),
        in_specs=[VMEM],
        out_specs=(VMEM, VMEM),
        scratch_shapes=[pltpu.VMEM((WIDTH, 128), BF)] * 2,
        compiler_params=params(),
    )(x)


def call_prepare(x, weight, after):
    shapes = [(g.channels, g.padded) for g in GEO]
    shapes += [(2, g.channels, 9 * g.channels) for g in GEO]
    shapes += [(g.sides, g.padded) for g in GEO]
    shapes += [(g.channels, g.channels) for g in GEO[1:]]
    made = pl.pallas_call(
        prepare_kernel,
        out_shape=like(*shapes),
        in_specs=[VMEM, VMEM, pl.BlockSpec(memory_space=pl.ANY)],
        out_specs=(VMEM,) * len(shapes),
        scratch_shapes=[pltpu.VMEM((g.channels, g.pixels), BF) for g in GEO[1:]],
        compiler_params=params(),
        cost_estimate=pl.CostEstimate(flops=10**9, bytes_accessed=12 * 2**20, transcendentals=0),
    )(x, weight, after)
    return made[:4] + made[8:], made[4:8]


def call_strips(far, near, padded):
    scratch = [pltpu.VMEM((WIDTH, 128), BF)] * 2
    scratch += [pltpu.VMEM((g.channels, g.sides), BF) for g in GEO]
    scratch += [pltpu.VMEM((g.channels, g.padded), BF) for g in GEO]
    scratch += [pltpu.VMEM((g.channels, g.slot), BF) for g in GEO]
    return pl.pallas_call(
        strips_kernel,
        out_shape=like((4, SLOT_ROWS, 128))[0],
        in_specs=[VMEM] * (2 + len(padded)),
        out_specs=VMEM,
        scratch_shapes=scratch,
        compiler_params=params(),
    )(far, near, *padded)


def call_block(strips, bias, weights):
    scratch = [pltpu.VMEM((4, g.channels, g.slot), BF) for g in GEO]
    scratch += [pltpu.VMEM((9 * g.channels, g.n1), BF) for g in GEO]
    scratch += [pltpu.VMEM((g.channels, g.width_h), BF) for g in GEO]
    scratch += [pltpu.VMEM((g.channels, g.n2), BF) for g in GEO]
    scratch += [pltpu.VMEM((WIDTH, GEO[0].n2), BF)]
    scratch += [pltpu.VMEM((g.n2, g.channels), F32) for g in GEO[1:]]
    return pl.pallas_call(
        block_kernel,
        out_shape=like((4, 384, 128))[0],
        in_specs=[VMEM] * 6,
        out_specs=VMEM,
        scratch_shapes=scratch,
        compiler_params=params(),
    )(strips, bias, *weights)


def call_join(received, weight, bias):
    return pl.pallas_call(
        join_kernel,
        out_shape=like((WIDTH, 8, 128), (256, 96), (64, 192), (16, 384)),
        in_specs=[VMEM] * 3,
        out_specs=(VMEM,) * 4,
        scratch_shapes=[
            pltpu.VMEM((WIDTH, 1024), BF),
            pltpu.VMEM((WIDTH, 8, 128), F32),
        ],
        compiler_params=params(),
    )(received, weight, bias)


def paired(shard, first):
    size = lax.axis_size("col")
    pairs = []
    for c in range(first, size - 1, 2):
        pairs += [(c, c + 1), (c + 1, c)]
    return lax.ppermute(shard, "col", pairs)


def swapped(parts, axis):
    return lax.all_to_all(parts, axis, split_axis=0, concat_axis=0, tiled=True)


def local(section_in, conv_weight, conv_bias, join_weight, join_bias):
    x = section_in[0, 0, 0]
    far, near = call_cols(x)
    padded, weights = call_prepare(x, conv_weight, far)
    strips = call_strips(paired(far, 1), paired(near, 0), padded)
    settled = call_block(swapped(strips, "row"), conv_bias, weights)
    out = call_join(swapped(settled, "branch"), join_weight, join_bias[None, :])
    first = [out[0]]
    for g in GEO[1:]:
        pixel_major = out[g.b].reshape(g.strip, g.cols, g.channels)
        first.append(pixel_major.transpose(2, 0, 1))
    return tuple(first)


def solution(mesh):
    in_specs = (
        P("branch", "row", "col", None, None),
        P("branch", None, None, None, None, None),
        P("branch", None, None),
        P(),
        P(),
    )
    out_specs = (P(None, ("branch", "row"), "col"),) * 4
    return jax.shard_map(local, mesh=mesh, in_specs=in_specs, out_specs=out_specs, check_vma=False)
```

time: 64.9 us -> 53.9 us (0.83)
  the two profiles are of different devices: /device:TPU:25 before, /device:TPU:16 now
where the time goes in v3:
time: 53.9 us; the launch traced here: 53.6 us
  blocking collectives  15 us (28%)
  starting transfers between devices  14.3 us (27%)
  waiting for transfers between devices  10.6 us (20%)
  Pallas kernels  9.49 us (18%)
  local copies, waits for them, and re-layouts  3.51 us (7%)
  between operations  0.7 us (1%)
    all_to_all x1, blocking collectives, swapped(): return lax.all_to_all(parts, axis, split_axis=0, concat_axis=0, tiled=True)  15 us
    all_to_all x1, waiting for transfers between devices, swapped(): return lax.all_to_all(parts, axis, split_axis=0, concat_axis=0, tiled=True)  10.6 us
    ppermute x2, starting transfers between devices, paired(): return lax.ppermute(shard, 'col', pairs)  9.3 us
    all_to_all x1, starting transfers between devices, swapped(): return lax.all_to_all(parts, axis, split_axis=0, concat_axis=0, tiled=True)  5.03 us
    pallas_call x1, Pallas kernels, call_block(): pl.pallas_call(block_kernel, out_shape=like((4, 384, 128))[0], in_specs=[...  5 us
    unnamed x10, local copies, waits for them, and re-layouts  3.51 us
    pallas_call x1, Pallas kernels, call_join(): pl.pallas_call(join_kernel, out_shape=like((WIDTH, 8, 128), (256, 96), (6...  2.69 us
  transfers between devices with their start and end apart: 3, of which 1 were waited for; matrix products, arithmetic and copies ran while one was open for 0% of the time, Pallas kernels for 1%

profile of v3, /device:TPU:16, one launch (start us, length us, event | category | flops | bytes accessed | tf_op | source)
XLA Modules:
  0.0 53.6 jit_solution(469015633532756153)
XLA Ops:
  0.6 0.0 copy-start.1
  0.6 1.0 %copy-done.1 = bf16[1,1,1,48,4096]{4,3,2,1,0:T(8,128)(2,1)S(1)} copy-done((bf16[1,1,1,48,4096]{4,3,2,1,0:T(8,128)(2,1)S(1)}, bf16[1,1,1,48,4096]{4,3,2,1,0:T(8,128)(2,1)}, u32[]{:S(2)}) %copy-start.1) | copy-done | bytes 393240
  1.6 0.5 shard_map.84
  2.1 8.4 %collective-permute-start = (bf16[48,128]{1,0:T(8,128)(2,1)S(1)}, bf16[48,128]{1,0:T(8,128)(2,1)S(1)}, u32[]{:S(2)}, u32[]{:S(2)}) collective-permute-start(bf16[48,128]{1,0:T(8,128)(2,1)S(1)} %get-tuple-element.25._), channel_id=1, source_target_pairs={{1,2},{2,1},{3,4},{4,3},{5,6},{6,5},{7,8},{8,7},{9,10},{10,9},{11,... | collective-permute-start | bytes 36872 | tf_op jit(solution)/shard_map/ppermute | solution.py:446
  10.6 0.9 %collective-permute-start.1 = (bf16[48,128]{1,0:T(8,128)(2,1)S(1)}, bf16[48,128]{1,0:T(8,128)(2,1)S(1)}, u32[]{:S(2)}, u32[]{:S(2)}) collective-permute-start(bf16[48,128]{1,0:T(8,128)(2,1)S(1)} %get-tuple-element.26), channel_id=1, source_target_pairs={{0,1},{1,0},{2,3},{3,2},{4,5},{5,4},{6,7},{7,6},{8,9},{9,8},{10,11... | collective-permute-start | bytes 36872 | tf_op jit(solution)/shard_map/ppermute | solution.py:446
  11.4 0.0 copy-start
  11.4 2.5 %copy-done = bf16[1,2,3,3,384,384]{5,4,3,2,1,0:T(8,128)(2,1)S(1)} copy-done((bf16[1,2,3,3,384,384]{5,4,3,2,1,0:T(8,128)(2,1)S(1)}, bf16[1,2,3,3,384,384]{5,4,3,2,1,0:T(8,128)(2,1)}, u32[]{:S(2)}) %copy-start) | copy-done | bytes 5308440
  13.9 0.7 %shard_map.85 = (bf16[48,4224]{1,0:T(8,128)(2,1)S(1)}, bf16[96,1152]{1,0:T(8,128)(2,1)S(1)}, bf16[192,384]{1,0:T(8,128)(2,1)S(1)}, bf16[384,128]{1,0:T(8,128)(2,...) custom-call(bf16[48,4096]{1,0:T(8,128)(2,1)S(1)} %bitcast.11, ...), custom_call_target="tpu_custom_call" | custom-call | flops 1000000000 | bytes 12582912 | tf_op jit(solution)/shard_map/pallas_call | solution.py:383
  14.6 0.0 collective-permute-done.far
  14.6 0.0 collective-permute-done.1.near
  14.7 0.0 copy-start.3
  14.7 0.6 %shard_map.86 = bf16[4,624,128]{2,1,0:T(8,128)(2,1)S(1)} custom-call(bf16[48,128]{1,0:T(8,128)(2,1)S(1)} %collective-permute-done.far, bf16[48,128]{1,0:T(8,128)(2,1)S(1)} %collective-permute-done.1.near, bf16[48,4224]{1,0:T(8,128)(2,1)S(1)} %get-tuple-element.27.refs_0_, bf16[96,1152]{1,0:T(8,128)(2,1)S(1)} %get-tuple-element.28.refs_1_, ...), custom_call_target="tpu_custom_call" | custom-call | tf_op jit(solution)/shard_map/pallas_call | solution.py:400
  15.3 15.0 %all_to_all.10.strips = bf16[4,624,128]{2,1,0:T(8,128)(2,1)S(1)} all-to-all(bf16[4,624,128]{2,1,0:T(8,128)(2,1)S(1)} %shard_map.86), channel_id=1, replica_groups=mesh['branch'=4,'row'=4,'col'=16] {'row'}, dimensions={0} | all-to-all | bytes 1277952 | tf_op jit(solution)/shard_map/all_to_all | solution.py:450
  30.3 0.0 copy-done.3
  30.3 0.0 copy-start.4
  30.3 0.0 copy-start.2
  30.3 5.0 %shard_map.87 = bf16[4,384,128]{2,1,0:T(8,128)(2,1)} custom-call(bf16[4,624,128]{2,1,0:T(8,128)(2,1)S(1)} %all_to_all.10.strips, f32[1,2,384]{2,1,0:T(2,128)S(1)} %copy-done.3, bf16[2,48,432]{2,1,0:T(8,128)(2,1)S(1)} %get-tuple-element.38.refs_0_, bf16[2,96,864]{2,1,0:T(8,128)(2,1)S(1)} %get-tuple-element.39.refs_1_, ...), custom_call_target="tpu_custom_call" | custom-call | tf_op jit(solution)/shard_map/pallas_call | solution.py:417
  35.3 5.0 %all-to-all-start.1 = ((bf16[4,384,128]{2,1,0:T(8,128)(2,1)}), bf16[4,384,128]{2,1,0:T(8,128)(2,1)S(1)}, u32[]{:S(2)}, u32[]{:S(2)}) async-start(bf16[4,384,128]{2,1,0:T(8,128)(2,1)} %shard_map.87), calls=%async_computation.1 | async-start | bytes 786432 | tf_op jit(solution)/shard_map/all_to_all | solution.py:450
  40.3 0.0 copy-done.4
  40.3 10.6 %all-to-all-done.1.zb = bf16[4,384,128]{2,1,0:T(8,128)(2,1)S(1)} async-done(((bf16[4,384,128]{2,1,0:T(8,128)(2,1)}), bf16[4,384,128]{2,1,0:T(8,128)(2,1)S(1)}, u32[]{:S(2)}, u32[]{:S(2)}) %all-to-all-start.1) | async-done | bytes 393248 | tf_op jit(solution)/shard_map/all_to_all | solution.py:450
  50.9 0.0 copy-done.2
  50.9 2.7 %shard_map.88 = (bf16[48,8,128]{2,1,0:T(8,128)(2,1)}, bf16[256,96]{1,0:T(8,128)(2,1)}, bf16[64,192]{1,0:T(8,128)(2,1)}, bf16[16,384]{1,0:T(8,128)(2,1)}) custom-call(bf16[4,384,128]{2,1,0:T(8,128)(2,1)S(1)} %all-to-all-done.1.zb, bf16[720,720]{1,0:T(8,128)(2,1)S(1)} %copy-done.2, f32[1,720]{1,0:T(1,128)S(1)} %broadcast_in_dim.3.bias), custom_call_target="tpu_custom_call" | custom-call | tf_op jit(solution)/shard_map/pallas_call | solution.py:428
  (1 shorter events, 0.0 us)
Async XLA Ops:
  0.6 1.0 %copy-start.1 = (bf16[1,1,1,48,4096]{4,3,2,1,0:T(8,128)(2,1)S(1)}, bf16[1,1,1,48,4096]{4,3,2,1,0:T(8,128)(2,1)}, u32[]{:S(2)}) copy-start(bf16[1,1,1,48,4096]{4,3,2,1,0:T(8,128)(2,1)} %param.5) | copy-start | bytes 1179652
  2.1 12.5 %collective-permute-start = (bf16[48,128]{1,0:T(8,128)(2,1)S(1)}, bf16[48,128]{1,0:T(8,128)(2,1)S(1)}, u32[]{:S(2)}, u32[]{:S(2)}) collective-permute-start(bf16[48,128]{1,0:T(8,128)(2,1)S(1)} %get-tuple-element.25._), channel_id=1, source_target_pairs={{1,2},{2,1},{3,4},{4,3},{5,6},{6,5},{7,8},{8,7},{9,10},{10,9},{11,... | collective-permute-start | bytes 36872 | tf_op jit(solution)/shard_map/ppermute | solution.py:446
  10.6 4.1 %collective-permute-start.1 = (bf16[48,128]{1,0:T(8,128)(2,1)S(1)}, bf16[48,128]{1,0:T(8,128)(2,1)S(1)}, u32[]{:S(2)}, u32[]{:S(2)}) collective-permute-start(bf16[48,128]{1,0:T(8,128)(2,1)S(1)} %get-tuple-element.26), channel_id=1, source_target_pairs={{0,1},{1,0},{2,3},{3,2},{4,5},{5,4},{6,7},{7,6},{8,9},{9,8},{10,11... | collective-permute-start | bytes 36872 | tf_op jit(solution)/shard_map/ppermute | solution.py:446
  11.4 2.5 %copy-start = (bf16[1,2,3,3,384,384]{5,4,3,2,1,0:T(8,128)(2,1)S(1)}, bf16[1,2,3,3,384,384]{5,4,3,2,1,0:T(8,128)(2,1)}, u32[]{:S(2)}) copy-start(bf16[1,2,3,3,384,384]{5,4,3,2,1,0:T(8,128)(2,1)} %weight.2) | copy-start | bytes 15925252
  14.7 15.6 %copy-start.3 = (f32[1,2,384]{2,1,0:T(2,128)S(1)}, f32[1,2,384]{2,1,0:T(2,128)}, u32[]{:S(2)}) copy-start(f32[1,2,384]{2,1,0:T(2,128)} %bias.1) | copy-start | bytes 9220
  30.3 10.0 %copy-start.4 = (f32[720]{0:T(1024)S(1)}, f32[720]{0:T(1024)}, u32[]{:S(2)}) copy-start(f32[720]{0:T(1024)} %param.9) | copy-start | bytes 8644
  30.3 20.6 %copy-start.2 = (bf16[720,720]{1,0:T(8,128)(2,1)S(1)}, bf16[720,720]{1,0:T(8,128)(2,1)}, u32[]{:S(2)}) copy-start(bf16[720,720]{1,0:T(8,128)(2,1)} %weight.3) | copy-start | bytes 3110404
  35.3 15.6 %all-to-all-start.1 = ((bf16[4,384,128]{2,1,0:T(8,128)(2,1)}), bf16[4,384,128]{2,1,0:T(8,128)(2,1)S(1)}, u32[]{:S(2)}, u32[]{:S(2)}) async-start(bf16[4,384,128]{2,1,0:T(8,128)(2,1)} %shard_map.87), calls=%async_computation.1 | async-start | bytes 786432 | tf_op jit(solution)/shard_map/all_to_all | solution.py:450

commit v4 on v3

--- a/solution.py
+++ b/solution.py
@@ -104,13 +104,13 @@
     return (k == spot).astype(F32).astype(BF)
 
 
-def prepare_kernel(x, weight, _, *refs):
-    xp_all, wp_all, places, orders = refs[:4], refs[4:8], refs[8:12], (None,) + refs[12:15]
-    st_all = (x,) + refs[15:18]
+def prepare_kernel(x, _, *refs):
+    xp_all, places, orders = refs[:4], refs[4:8], (None,) + refs[8:11]
+    st_all = (x,) + refs[11:14]
 
     def body(g):
         c = g.channels
-        st, xp, wp = st_all[g.b], xp_all[g.b], wp_all[g.b]
+        st, xp = st_all[g.b], xp_all[g.b]
         places[g.b][...] = side_places(g)
         if g.b:
             order = channel_order(g)
@@ -122,11 +122,6 @@
         for y in range(g.rows):
             to = y * g.pitch + 2
             xp[:, to : to + g.cols] = st[:, y * g.cols : (y + 1) * g.cols]
-        for layer in range(2):
-            for dy in range(3):
-                for dx in range(3):
-                    t = 3 * dy + dx
-                    wp[layer, :, c * t : c * (t + 1)] = weight[0, layer, dy, dx, 0:c, 0:c]
 
     per_branch(body)
 
@@ -192,15 +187,27 @@
     return jnp.where(out, 0.0, 1.0)[0:1, :]
 
 
-def block_kernel(strips, bias, *refs):
-    wp_all, out = refs[:4], refs[4]
-    xs_all, col_all, hp_all, own_all = refs[5:9], refs[9:13], refs[13:17], refs[17:21]
-    z0, zt_all = refs[21], (None,) + refs[22:25]
+def block_kernel(strips, bias, weight, out, *refs):
+    wp_all, xs_all, col_all = refs[:4], refs[4:8], refs[8:12]
+    hp_all, own_all = refs[12:16], refs[16:20]
+    z0, zt_all = refs[20], (None,) + refs[21:24]
+    wbuf, sems = refs[24:]
     _, row_place, col_place = place()
 
     def body(g):
         c = g.channels
         cl = up128(c)
+
+        def fetch(layer, dy):
+            return pltpu.make_async_copy(
+                weight.at[0, layer, dy, :, 0:c, 0:cl],
+                wbuf.at[layer, dy, :, 0:c, 0:cl],
+                sems.at[layer, dy],
+            )
+
+        for layer in range(2):
+            for dy in range(3):
+                fetch(layer, dy).start()
         xs, hp, wp, col, own = xs_all[g.b], hp_all[g.b], wp_all[g.b], col_all[g.b], own_all[g.b]
         for tile in range(4):
             for m in range(g.blocks):
@@ -237,8 +244,10 @@
 
         def conv(layer, view, size, n, finish):
             for dy in range(3):
+                fetch(layer, dy).wait()
                 for dx in range(3):
                     t = 3 * dy + dx
+                    wp[:, c * t : c * (t + 1)] = wbuf[layer, dy, dx, 0:c, 0:c]
                     for tile in range(4):
                         col[c * t : c * (t + 1), tile * size : (tile + 1) * size] = view(
                             tile, dy * g.pitch + dx
@@ -246,7 +255,7 @@
             step = STEPS[g.b]
             for at in range(0, n, step):
                 width = min(step, n - at)
-                finish(at, width, nn(wp[layer], col[:, at : at + width]))
+                finish(at, width, nn(wp[...], col[:, at : at + width]))
 
         bias0 = column(0)
 
@@ -317,7 +326,26 @@
     return lax.dot_general(a, b, (((1,), (1,)), ((), ())), preferred_element_type=F32)
 
 
-def join_kernel(zb, weight, bias, out0, out1, out2, out3, z0s, s0):
+PAIRS = [(j, i) for j in range(4) for i in range(4) if i != j]
+FINER = [(i, j) for i in range(4) for j in range(i + 1, 4)]
+
+
+def maps_kernel(weight, _, *refs):
+    blocks, shrink, grow = refs[:12], refs[12:18], refs[18:]
+    for ref, (j, i) in zip(blocks, PAIRS):
+        gj, gi = GEO[j], GEO[i]
+        ref[...] = weight[gj.start : gj.start + gj.channels, gi.start : gi.start + gi.channels]
+    for ref, (i, j) in zip(shrink, FINER):
+        ref[...] = repeat_map_t(i, j)
+    for ref, (i, j) in zip(grow, FINER[3:]):
+        ref[...] = repeat_map(i, j)
+
+
+def join_kernel(zb, bias, *refs):
+    block = dict(zip(PAIRS, refs[:12]))
+    shrink = dict(zip(FINER, refs[12:18]))
+    grow = dict(zip(FINER[3:], refs[18:21]))
+    out0, out1, out2, out3, z0s, s0 = refs[21:]
     for y in range(8):
         z0s[:, 128 * y : 128 * (y + 1)] = zb[0, WIDTH * y : WIDTH * (y + 1), :]
     z = [
@@ -326,14 +354,9 @@
         jnp.concatenate([zb[2, 0:64, :], zb[2, 64:128, 0:64]], axis=1),
         jnp.concatenate([zb[3, 0:16, :], zb[3, 16:32, :], zb[3, 32:48, :]], axis=1),
     ]
-
-    def block(j, i):
-        gj, gi = GEO[j], GEO[i]
-        return weight[gj.start : gj.start + gj.channels, gi.start : gi.start + gi.channels]
-
     total = None
     for i in (1, 2, 3):
-        term = nn(nt(block(0, i), z[i]).astype(BF), repeat_map_t(0, i))
+        term = nn(nt(block[0, i][...], z[i]).astype(BF), shrink[0, i][...])
         total = term if total is None else total + term
     wide = jnp.broadcast_to(bias[:, 0:WIDTH], (8, WIDTH))
     total = jnp.maximum(total + z[0].astype(F32) + wide.T[:, 0:1], 0.0)
@@ -348,15 +371,15 @@
             if i == j:
                 continue
             if i < j:
-                sums = (nt if i == 0 else nn)(repeat_map_t(i, j), z[i])
+                sums = (nt if i == 0 else nn)(shrink[i, j][...], z[i])
                 mean = (sums * (0.25 ** (j - i))).astype(BF)
-                total = total + nt(mean, block(j, i)).astype(BF).astype(F32)
+                total = total + nt(mean, block[j, i][...]).astype(BF).astype(F32)
             else:
-                total = total + nn(repeat_map(j, i), nt(z[i], block(j, i)).astype(BF))
+                total = total + nn(grow[j, i][...], nt(z[i], block[j, i][...]).astype(BF))
         out[...] = jnp.maximum(total, 0.0).astype(BF)
 
 
-def params(mib=24):
+def params(mib=32):
     return pltpu.CompilerParams(vmem_limit_bytes=mib * 1024 * 1024)
 
 
@@ -375,21 +398,19 @@
     )(x)
 
 
-def call_prepare(x, weight, after):
+def call_prepare(x, after):
     shapes = [(g.channels, g.padded) for g in GEO]
-    shapes += [(2, g.channels, 9 * g.channels) for g in GEO]
     shapes += [(g.sides, g.padded) for g in GEO]
     shapes += [(g.channels, g.channels) for g in GEO[1:]]
-    made = pl.pallas_call(
+    return pl.pallas_call(
         prepare_kernel,
         out_shape=like(*shapes),
-        in_specs=[VMEM, VMEM, pl.BlockSpec(memory_space=pl.ANY)],
+        in_specs=[VMEM, pl.BlockSpec(memory_space=pl.ANY)],
         out_specs=(VMEM,) * len(shapes),
         scratch_shapes=[pltpu.VMEM((g.channels, g.pixels), BF) for g in GEO[1:]],
         compiler_params=params(),
-        cost_estimate=pl.CostEstimate(flops=10**9, bytes_accessed=12 * 2**20, transcendentals=0),
-    )(x, weight, after)
-    return made[:4] + made[8:], made[4:8]
+        cost_estimate=pl.CostEstimate(flops=10**9, bytes_accessed=2**20, transcendentals=0),
+    )(x, after)
 
 
 def call_strips(far, near, padded):
@@ -404,38 +425,55 @@
         out_specs=VMEM,
         scratch_shapes=scratch,
         compiler_params=params(),
+        cost_estimate=pl.CostEstimate(flops=10**10, bytes_accessed=2**24, transcendentals=0),
     )(far, near, *padded)
 
 
-def call_block(strips, bias, weights):
-    scratch = [pltpu.VMEM((4, g.channels, g.slot), BF) for g in GEO]
+def call_block(strips, bias, weight):
+    scratch = [pltpu.VMEM((g.channels, 9 * g.channels), BF) for g in GEO]
+    scratch += [pltpu.VMEM((4, g.channels, g.slot), BF) for g in GEO]
     scratch += [pltpu.VMEM((9 * g.channels, g.n1), BF) for g in GEO]
     scratch += [pltpu.VMEM((g.channels, g.width_h), BF) for g in GEO]
     scratch += [pltpu.VMEM((g.channels, g.n2), BF) for g in GEO]
     scratch += [pltpu.VMEM((WIDTH, GEO[0].n2), BF)]
     scratch += [pltpu.VMEM((g.n2, g.channels), F32) for g in GEO[1:]]
+    scratch += [pltpu.VMEM((2, 3, 3, 384, 384), BF), pltpu.SemaphoreType.DMA((2, 3))]
     return pl.pallas_call(
         block_kernel,
         out_shape=like((4, 384, 128))[0],
-        in_specs=[VMEM] * 6,
+        in_specs=[VMEM, VMEM, pl.BlockSpec(memory_space=pltpu.HBM)],
         out_specs=VMEM,
         scratch_shapes=scratch,
         compiler_params=params(),
-    )(strips, bias, *weights)
-
-
-def call_join(received, weight, bias):
+    )(strips, bias, weight)
+
+
+def call_maps(weight, after):
+    shapes = [(GEO[j].channels, GEO[i].channels) for j, i in PAIRS]
+    shapes += [(GEO[j].pixels // 4, GEO[i].pixels // 4) for i, j in FINER]
+    shapes += [(GEO[i].pixels // 4, GEO[j].pixels // 4) for i, j in FINER[3:]]
+    return pl.pallas_call(
+        maps_kernel,
+        out_shape=like(*shapes),
+        in_specs=[VMEM, pl.BlockSpec(memory_space=pl.ANY)],
+        out_specs=(VMEM,) * len(shapes),
+        compiler_params=params(),
+        cost_estimate=pl.CostEstimate(flops=10**9, bytes_accessed=2**20, transcendentals=0),
+    )(weight, after)
+
+
+def call_join(received, bias, maps):
     return pl.pallas_call(
         join_kernel,
         out_shape=like((WIDTH, 8, 128), (256, 96), (64, 192), (16, 384)),
-        in_specs=[VMEM] * 3,
+        in_specs=[VMEM] * (2 + len(maps)),
         out_specs=(VMEM,) * 4,
         scratch_shapes=[
             pltpu.VMEM((WIDTH, 1024), BF),
             pltpu.VMEM((WIDTH, 8, 128), F32),
         ],
         compiler_params=params(),
-    )(received, weight, bias)
+    )(received, bias, *maps)
 
 
 def paired(shard, first):
@@ -453,10 +491,11 @@
 def local(section_in, conv_weight, conv_bias, join_weight, join_bias):
     x = section_in[0, 0, 0]
     far, near = call_cols(x)
-    padded, weights = call_prepare(x, conv_weight, far)
+    padded = call_prepare(x, far)
     strips = call_strips(paired(far, 1), paired(near, 0), padded)
-    settled = call_block(swapped(strips, "row"), conv_bias, weights)
-    out = call_join(swapped(settled, "branch"), join_weight, join_bias[None, :])
+    settled = call_block(swapped(strips, "row"), conv_bias, conv_weight)
+    maps = call_maps(join_weight, settled)
+    out = call_join(swapped(settled, "branch"), join_bias[None, :], maps)
     first = [out[0]]
     for g in GEO[1:]:
         pixel_major = out[g.b].reshape(g.strip, g.cols, g.channels)

time: 53.9 us -> 56.4 us (1.046)
  the two profiles are of different devices: /device:TPU:16 before, /device:TPU:1 now
where the time goes in v4:
time: 56.4 us; the launch traced here: 56.1 us
  starting transfers between devices  18.5 us (33%)
  blocking collectives  14.2 us (25%)
  waiting for transfers between devices  11.1 us (20%)
  Pallas kernels  10.6 us (19%)
  local copies, waits for them, and re-layouts  1.02 us (2%)
  between operations  0.75 us (1%)
    all_to_all x1, blocking collectives, swapped(): return lax.all_to_all(parts, axis, split_axis=0, concat_axis=0, tiled=True)  14.2 us
    all_to_all x1, waiting for transfers between devices, swapped(): return lax.all_to_all(parts, axis, split_axis=0, concat_axis=0, tiled=True)  10.5 us
    ppermute x2, starting transfers between devices, paired(): return lax.ppermute(shard, 'col', pairs)  10.3 us
    all_to_all x1, starting transfers between devices, swapped(): return lax.all_to_all(parts, axis, split_axis=0, concat_axis=0, tiled=True)  8.2 us
    pallas_call x1, Pallas kernels, call_block(): pl.pallas_call(block_kernel, out_shape=like((4, 384, 128))[0], in_specs=[...  5.52 us
    pallas_call x1, Pallas kernels, call_join(): pl.pallas_call(join_kernel, out_shape=like((WIDTH, 8, 128), (256, 96), (6...  2.66 us
  transfers between devices with their start and end apart: 3, of which 2 were waited for; matrix products, arithmetic and copies ran while one was open for 0% of the time, Pallas kernels for 2%

profile of v4, /device:TPU:1, one launch (start us, length us, event | category | flops | bytes accessed | tf_op | source)
XLA Modules:
  0.0 56.1 jit_solution(16320718623198650294)
XLA Ops:
  0.6 0.0 copy-start
  0.6 1.0 %copy-done = bf16[1,1,1,48,4096]{4,3,2,1,0:T(8,128)(2,1)S(1)} copy-done((bf16[1,1,1,48,4096]{4,3,2,1,0:T(8,128)(2,1)S(1)}, bf16[1,1,1,48,4096]{4,3,2,1,0:T(8,128)(2,1)}, u32[]{:S(2)}) %copy-start) | copy-done | bytes 393240
  1.6 0.5 shard_map.84
  2.1 10.2 %collective-permute-start = (bf16[48,128]{1,0:T(8,128)(2,1)S(1)}, bf16[48,128]{1,0:T(8,128)(2,1)S(1)}, u32[]{:S(2)}, u32[]{:S(2)}) collective-permute-start(bf16[48,128]{1,0:T(8,128)(2,1)S(1)} %get-tuple-element.42._), channel_id=1, source_target_pairs={{1,2},{2,1},{3,4},{4,3},{5,6},{6,5},{7,8},{8,7},{9,10},{10,9},{11,... | collective-permute-start | bytes 36872 | tf_op jit(solution)/shard_map/ppermute | solution.py:484
  12.3 0.1 collective-permute-start.1
  12.4 0.0 slice-start
  12.5 0.6 %shard_map.85 = (bf16[48,4224]{1,0:T(8,128)(2,1)S(1)}, bf16[96,1152]{1,0:T(8,128)(2,1)S(1)}, bf16[192,384]{1,0:T(8,128)(2,1)S(1)}, bf16[384,128]{1,0:T(8,128)(2,...) custom-call(bf16[48,4096]{1,0:T(8,128)(2,1)S(1)} %bitcast.13, ...), custom_call_target="tpu_custom_call" | custom-call | flops 1000000000 | bytes 1048576 | tf_op jit(solution)/shard_map/pallas_call | solution.py:405
  13.1 0.6 %collective-permute-done.far = bf16[48,128]{1,0:T(8,128)(2,1)S(1)} collective-permute-done((bf16[48,128]{1,0:T(8,128)(2,1)S(1)}, bf16[48,128]{1,0:T(8,128)(2,1)S(1)}, u32[]{:S(2)}, u32[]{:S(2)}) %collective-permute-start) | collective-permute-done | bytes 12320 | tf_op jit(solution)/shard_map/ppermute | solution.py:484
  13.7 0.0 collective-permute-done.1.near
  13.7 0.6 %shard_map.86 = bf16[4,624,128]{2,1,0:T(8,128)(2,1)S(1)} custom-call(bf16[48,128]{1,0:T(8,128)(2,1)S(1)} %collective-permute-done.far, bf16[48,128]{1,0:T(8,128)(2,1)S(1)} %collective-permute-done.1.near, bf16[48,4224]{1,0:T(8,128)(2,1)S(1)} %get-tuple-element.44.refs_0_, bf16[96,1152]{1,0:T(8,128)(2,1)S(1)} %get-tuple-element.45.refs_1_, ...), custom_call_target="tpu_custom_call" | custom-call | flops 10000000000 | bytes 16777216 | tf_op jit(solution)/shard_map/pallas_call | solution.py:421
  14.3 0.0 copy-start.1
  14.3 14.2 %all_to_all.10.strips = bf16[4,624,128]{2,1,0:T(8,128)(2,1)S(1)} all-to-all(bf16[4,624,128]{2,1,0:T(8,128)(2,1)S(1)} %shard_map.86), channel_id=1, replica_groups=mesh['branch'=4,'row'=4,'col'=16] {'row'}, dimensions={0} | all-to-all | bytes 1277952 | tf_op jit(solution)/shard_map/all_to_all | solution.py:488
  28.5 0.0 slice-done
  28.5 0.0 slice-done.1
  28.5 0.0 copy-done.1
  28.5 0.0 copy-start.3
  28.5 0.0 copy-start.2
  28.5 5.5 %shard_map.87._ = bf16[4,384,128]{2,1,0:T(8,128)(2,1)} custom-call(bf16[4,624,128]{2,1,0:T(8,128)(2,1)S(1)} %all_to_all.10.strips, f32[1,2,384]{2,1,0:T(2,128)S(1)} %copy-done.1, bf16[1,2,3,3,384,384]{5,4,3,2,1,0:T(8,128)(2,1)S(1)} %bitcast.11), custom_call_target="tpu_custom_call" | custom-call | tf_op jit(solution)/shard_map/pallas_call | solution.py:441
  34.1 8.2 %all-to-all-start.1 = ((bf16[4,384,128]{2,1,0:T(8,128)(2,1)}), bf16[4,384,128]{2,1,0:T(8,128)(2,1)S(1)}, u32[]{:S(2)}, u32[]{:S(2)}) async-start(bf16[4,384,128]{2,1,0:T(8,128)(2,1)} %shard_map.87._), calls=%async_computation.1 | async-start | bytes 786432 | tf_op jit(solution)/shard_map/all_to_all | solution.py:488
  42.3 0.0 copy-done.3
  42.3 0.0 copy-done.2
  42.3 0.7 %shard_map.88 = (bf16[48,96]{1,0:T(8,128)(2,1)S(1)}, bf16[48,192]{1,0:T(8,128)(2,1)S(1)}, bf16[48,384]{1,0:T(8,128)(2,1)S(1)}, bf16[96,48]{1,0:T(8,128)(2,1)S(1)...) custom-call(bf16[720,720]{1,0:T(8,128)(2,1)S(1)} %copy-done.2, ...), custom_call_target="tpu_custom_call" | custom-call | flops 1000000000 | bytes 1048576 | tf_op jit(solution)/shard_map/pallas_call | solution.py:455
  43.0 10.5 %all-to-all-done.1.zb = bf16[4,384,128]{2,1,0:T(8,128)(2,1)S(1)} async-done(((bf16[4,384,128]{2,1,0:T(8,128)(2,1)}), bf16[4,384,128]{2,1,0:T(8,128)(2,1)S(1)}, u32[]{:S(2)}, u32[]{:S(2)}) %all-to-all-start.1) | async-done | bytes 393248 | tf_op jit(solution)/shard_map/all_to_all | solution.py:488
  53.5 2.7 %shard_map.89 = (bf16[48,8,128]{2,1,0:T(8,128)(2,1)}, bf16[256,96]{1,0:T(8,128)(2,1)}, bf16[64,192]{1,0:T(8,128)(2,1)}, bf16[16,384]{1,0:T(8,128)(2,1)}) custom-call(bf16[4,384,128]{2,1,0:T(8,128)(2,1)S(1)} %all-to-all-done.1.zb, f32[1,720]{1,0:T(1,128)S(1)} %broadcast_in_dim.3.bias, bf16[48,96]{1,0:T(8,128)(2,1)S(1)} %get-tuple-element.55.refs_0_, ...), custom_call_target="tpu_custom_call" | custom-call | tf_op jit(solution)/shard_map/pallas_call | solution.py:466
  (3 shorter events, 0.0 us)
Async XLA Ops:
  0.6 1.0 %copy-start = (bf16[1,1,1,48,4096]{4,3,2,1,0:T(8,128)(2,1)S(1)}, bf16[1,1,1,48,4096]{4,3,2,1,0:T(8,128)(2,1)}, u32[]{:S(2)}) copy-start(bf16[1,1,1,48,4096]{4,3,2,1,0:T(8,128)(2,1)} %param.5) | copy-start | bytes 1179652
  2.1 11.6 %collective-permute-start = (bf16[48,128]{1,0:T(8,128)(2,1)S(1)}, bf16[48,128]{1,0:T(8,128)(2,1)S(1)}, u32[]{:S(2)}, u32[]{:S(2)}) collective-permute-start(bf16[48,128]{1,0:T(8,128)(2,1)S(1)} %get-tuple-element.42._), channel_id=1, source_target_pairs={{1,2},{2,1},{3,4},{4,3},{5,6},{6,5},{7,8},{8,7},{9,10},{10,9},{11,... | collective-permute-start | bytes 36872 | tf_op jit(solution)/shard_map/ppermute | solution.py:484
  12.3 1.4 %collective-permute-start.1 = (bf16[48,128]{1,0:T(8,128)(2,1)S(1)}, bf16[48,128]{1,0:T(8,128)(2,1)S(1)}, u32[]{:S(2)}, u32[]{:S(2)}) collective-permute-start(bf16[48,128]{1,0:T(8,128)(2,1)S(1)} %get-tuple-element.43), channel_id=1, source_target_pairs={{0,1},{1,0},{2,3},{3,2},{4,5},{5,4},{6,7},{7,6},{8,9},{9,8},{10,11... | collective-permute-start | bytes 36872 | tf_op jit(solution)/shard_map/ppermute | solution.py:484
  12.4 16.1 %slice-start = ((s8[5308416]{0:T(1024)(128)(4,1)}), s8[4194304]{0:T(1024)(128)(4,1)S(1)}, s32[]{:S(2)}) async-start(s8[5308416]{0:T(1024)(128)(4,1)} %bitcast.10), calls=%async_computation.2 | async-start | bytes 8388608
  13.7 14.8 %slice-start.1 = ((s8[5308416]{0:T(1024)(128)(4,1)}), s8[1114112]{0:T(1024)(128)(4,1)S(1)}, s32[]{:S(2)}) async-start(s8[5308416]{0:T(1024)(128)(4,1)} %bitcast.10), calls=%async_computation.3 | async-start | bytes 2228224
  14.3 14.2 %copy-start.1 = (f32[1,2,384]{2,1,0:T(2,128)S(1)}, f32[1,2,384]{2,1,0:T(2,128)}, u32[]{:S(2)}) copy-start(f32[1,2,384]{2,1,0:T(2,128)} %bias.1) | copy-start | bytes 9220
  28.5 13.8 %copy-start.3 = (f32[720]{0:T(1024)S(1)}, f32[720]{0:T(1024)}, u32[]{:S(2)}) copy-start(f32[720]{0:T(1024)} %param.9) | copy-start | bytes 8644
  28.5 13.8 %copy-start.2 = (bf16[720,720]{1,0:T(8,128)(2,1)S(1)}, bf16[720,720]{1,0:T(8,128)(2,1)}, u32[]{:S(2)}) copy-start(bf16[720,720]{1,0:T(8,128)(2,1)} %weight.3) | copy-start | bytes 3110404
  34.1 19.4 %all-to-all-start.1 = ((bf16[4,384,128]{2,1,0:T(8,128)(2,1)}), bf16[4,384,128]{2,1,0:T(8,128)(2,1)S(1)}, u32[]{:S(2)}, u32[]{:S(2)}) async-start(bf16[4,384,128]{2,1,0:T(8,128)(2,1)} %shard_map.87._), calls=%async_computation.1 | async-start | bytes 786432 | tf_op jit(solution)/shard_map/all_to_all | solution.py:488

commit v5 on v3

--- a/solution.py
+++ b/solution.py
@@ -8,7 +8,6 @@
 WIDTH = 48
 TH = 32
 TW = 128
-MARGIN = 128
 BF = jnp.bfloat16
 F32 = jnp.float32
 VMEM = pl.BlockSpec(memory_space=pltpu.VMEM)
@@ -31,19 +30,18 @@
         self.pitch = self.cols + 4
         self.padded = up128(self.rows * self.pitch)
         self.sides = 4 * self.rows
-        self.slot = up128(self.high * self.pitch + 2)
+        self.slot = up128(self.high * self.pitch)
         self.blocks = self.slot // 128
-        self.tile_h = (self.strip + 2) * self.pitch
-        self.tile_z = self.strip * self.pitch
-        self.n1 = up128(4 * self.tile_h)
-        self.n2 = up128(4 * self.tile_z)
-        self.width_h = up128(2 * MARGIN + self.n1)
+        self.wide = up128(4 * self.pitch)
+        self.lanes = self.high * self.wide
+        self.n1 = (self.strip + 2) * self.wide
+        self.n2 = self.strip * self.wide
         self.start = ((1 << b) - 1) * WIDTH
 
 
 GEO = [Geo(b) for b in range(4)]
 SLOT_ROWS = 624
-STEPS = (384, 640, 384, 256)
+STEPS = (640, 768, 512, 384)
 
 
 def place():
@@ -125,8 +123,8 @@
         for layer in range(2):
             for dy in range(3):
                 for dx in range(3):
-                    t = 3 * dy + dx
-                    wp[layer, :, c * t : c * (t + 1)] = weight[0, layer, dy, dx, 0:c, 0:c]
+                    tap = weight[0, layer, dy, dx, 0:c, 0:c]
+                    wp[layer, dy, :, c * dx : c * (dx + 1)] = tap
 
     per_branch(body)
 
@@ -168,7 +166,7 @@
         xf[...] = xp_all[g.b][...] + nn(stacked, places[g.b][...]).astype(BF)
         for k in range(4):
             for i, y, rows in runs(g, k):
-                at, lane, size = 1 + i * g.pitch, y * g.pitch, rows * g.pitch
+                at, lane, size = i * g.pitch, y * g.pitch, rows * g.pitch
                 slot[:, at : at + size] = xf[:, lane : lane + size]
             for m in range(g.blocks):
                 out[k, m * c : (m + 1) * c, :] = slot[:, 128 * m : 128 * (m + 1)]
@@ -178,10 +176,10 @@
 
 def inside(g, row_place, col_place):
     p = lax.broadcasted_iota(jnp.int32, (8, g.n1), 1).astype(F32)
-    tile = jnp.floor((p + 0.5) * (1.0 / g.tile_h))
-    rest = p - tile * g.tile_h
-    row = jnp.floor((rest + 0.5) * (1.0 / g.pitch))
-    x = rest - row * g.pitch
+    row = jnp.floor((p + 0.5) * (1.0 / g.wide))
+    rest = p - row * g.wide
+    tile = jnp.floor((rest + 0.5) * (1.0 / g.pitch))
+    x = rest - tile * g.pitch
     y = row - 1.0 + (row_place * g.strip).astype(F32)
     out = (
         ((tile == 0.0) & (y < 0.0))
@@ -194,40 +192,44 @@
 
 def block_kernel(strips, bias, *refs):
     wp_all, out = refs[:4], refs[4]
-    xs_all, col_all, hp_all, own_all = refs[5:9], refs[9:13], refs[13:17], refs[17:21]
-    z0, zt_all = refs[21], (None,) + refs[22:25]
+    xr_all, hr_all, z0, zt_all = refs[5:9], refs[9:13], refs[13], (None,) + refs[14:17]
     _, row_place, col_place = place()
 
     def body(g):
         c = g.channels
         cl = up128(c)
-        xs, hp, wp, col, own = xs_all[g.b], hp_all[g.b], wp_all[g.b], col_all[g.b], own_all[g.b]
-        for tile in range(4):
-            for m in range(g.blocks):
-                xs[tile, :, 128 * m : 128 * (m + 1)] = strips[tile, m * c : (m + 1) * c, :]
+        xr, hr, wp = xr_all[g.b], hr_all[g.b], wp_all[g.b]
+
+        def put(i, tile, source):
+            lane, to, left = i * g.pitch, i * g.wide + tile * g.pitch, g.pitch
+            while left:
+                m, at = divmod(lane, 128)
+                n = min(left, 128 - at)
+                if 0 <= source < 4:
+                    piece = strips[source, m * c : (m + 1) * c, at : at + n]
+                else:
+                    piece = jnp.zeros((c, n), BF)
+                xr[c : 2 * c, to : to + n] = piece
+                lane, to, left = lane + n, to + n, left - n
+
         for i in range(g.high):
-            lanes = slice(1 + i * g.pitch, 1 + (i + 1) * g.pitch)
             low = [k for k in range(4) if k * g.strip - 2 + i < 0]
             high = [k for k in range(4) if k * g.strip - 2 + i >= g.rows]
+            for tile in range(4):
+                put(i, tile, tile)
             if low:
 
                 @pl.when(row_place <= max(low))
-                def _(lanes=lanes):
-                    for tile in (3, 2, 1):
-                        xs[tile, :, lanes] = xs[tile - 1, :, lanes]
-                    xs[0, :, lanes] = jnp.zeros((c, g.pitch), BF)
+                def _(i=i):
+                    for tile in range(4):
+                        put(i, tile, tile - 1)
 
             if high:
 
                 @pl.when(row_place >= min(high))
-                def _(lanes=lanes):
-                    for tile in (0, 1, 2):
-                        xs[tile, :, lanes] = xs[tile + 1, :, lanes]
-                    xs[3, :, lanes] = jnp.zeros((c, g.pitch), BF)
-
-        for tile in range(4):
-            lane = 1 + 2 * g.pitch
-            own[:, tile * g.tile_z : (tile + 1) * g.tile_z] = xs[tile, :, lane : lane + g.tile_z]
+                def _(i=i):
+                    for tile in range(4):
+                        put(i, tile, tile + 1)
 
         mask = inside(g, row_place, col_place)
 
@@ -235,45 +237,42 @@
             wide = jnp.broadcast_to(bias[0, layer : layer + 1, :], (8, 8 * WIDTH))
             return wide.T[0:c, 0:1]
 
-        def conv(layer, view, size, n, finish):
-            for dy in range(3):
-                for dx in range(3):
-                    t = 3 * dy + dx
-                    for tile in range(4):
-                        col[c * t : c * (t + 1), tile * size : (tile + 1) * size] = view(
-                            tile, dy * g.pitch + dx
-                        )
+        def conv(layer, maps, size, n, finish):
+            maps[0:c, 1:size] = maps[c : 2 * c, 0 : size - 1]
+            maps[2 * c : 3 * c, 0 : size - 1] = maps[c : 2 * c, 1:size]
             step = STEPS[g.b]
             for at in range(0, n, step):
                 width = min(step, n - at)
-                finish(at, width, nn(wp[layer], col[:, at : at + width]))
+                total = None
+                for dy in range(3):
+                    lane = at + dy * g.wide
+                    term = nn(wp[layer, dy], maps[:, lane : lane + width])
+                    total = term if total is None else total + term
+                finish(at, width, total)
 
         bias0 = column(0)
 
         def finish_first(at, size, total):
             h = jnp.maximum(total + bias0, 0.0) * mask[:, at : at + size]
-            hp[:, MARGIN + at : MARGIN + at + size] = h.astype(BF)
-
-        conv(0, lambda tile, lane: xs[tile, :, lane : lane + g.tile_h], g.tile_h, g.n1, finish_first)
+            hr[c : 2 * c, at : at + size] = h.astype(BF)
+
+        conv(0, xr, g.lanes, g.n1, finish_first)
 
         bias1 = column(1)
 
         def finish_second(at, size, total):
-            z = jnp.maximum(total + bias1 + own[:, at : at + size].astype(F32), 0.0)
+            lane = 2 * g.wide + at
+            z = jnp.maximum(total + bias1 + xr[c : 2 * c, lane : lane + size].astype(F32), 0.0)
             if g.b == 0:
                 z0[:, at : at + size] = z.astype(BF)
             else:
                 zt_all[g.b][at : at + size, :] = z.T
 
-        def hidden(tile, lane):
-            lane += MARGIN + tile * g.tile_h - 1
-            return hp[:, lane : lane + g.tile_z]
-
-        conv(1, hidden, g.tile_z, g.n2, finish_second)
+        conv(1, hr, g.n1, g.n2, finish_second)
 
         for tile in range(4):
             for i in range(g.strip):
-                at = tile * g.tile_z + i * g.pitch + 2
+                at = i * g.wide + tile * g.pitch + 2
                 if g.b == 0:
                     out[tile, i * WIDTH : (i + 1) * WIDTH, :] = z0[:, at : at + g.cols]
                     continue
@@ -377,7 +376,7 @@
 
 def call_prepare(x, weight, after):
     shapes = [(g.channels, g.padded) for g in GEO]
-    shapes += [(2, g.channels, 9 * g.channels) for g in GEO]
+    shapes += [(2, 3, g.channels, 3 * g.channels) for g in GEO]
     shapes += [(g.sides, g.padded) for g in GEO]
     shapes += [(g.channels, g.channels) for g in GEO[1:]]
     made = pl.pallas_call(
@@ -408,10 +407,8 @@
 
 
 def call_block(strips, bias, weights):
-    scratch = [pltpu.VMEM((4, g.channels, g.slot), BF) for g in GEO]
-    scratch += [pltpu.VMEM((9 * g.channels, g.n1), BF) for g in GEO]
-    scratch += [pltpu.VMEM((g.channels, g.width_h), BF) for g in GEO]
-    scratch += [pltpu.VMEM((g.channels, g.n2), BF) for g in GEO]
+    scratch = [pltpu.VMEM((3 * g.channels, g.lanes), BF) for g in GEO]
+    scratch += [pltpu.VMEM((3 * g.channels, g.n1), BF) for g in GEO]
     scratch += [pltpu.VMEM((WIDTH, GEO[0].n2), BF)]
     scratch += [pltpu.VMEM((g.n2, g.channels), F32) for g in GEO[1:]]
     return pl.pallas_call(

time: 53.9 us -> 53.2 us (0.987)
  Pallas kernels: 9.49 us -> 8.5 us
    pallas_call x1, Pallas kernels: 5 us -> 4.02 us  [call_block(): pl.pallas_call(block_kernel, out_shape=like((4, 384, 128))[0], in_specs=[...]
where the time goes in v5:
time: 53.2 us; the launch traced here: 52.9 us
  blocking collectives  15 us (28%)
  starting transfers between devices  14.6 us (27%)
  waiting for transfers between devices  10.6 us (20%)
  Pallas kernels  8.5 us (16%)
  local copies, waits for them, and re-layouts  3.51 us (7%)
  between operations  0.7 us (1%)
    all_to_all x1, blocking collectives, swapped(): return lax.all_to_all(parts, axis, split_axis=0, concat_axis=0, tiled=True)  15 us
    all_to_all x1, waiting for transfers between devices, swapped(): return lax.all_to_all(parts, axis, split_axis=0, concat_axis=0, tiled=True)  10.6 us
    ppermute x2, starting transfers between devices, paired(): return lax.ppermute(shard, 'col', pairs)  9.3 us
    all_to_all x1, starting transfers between devices, swapped(): return lax.all_to_all(parts, axis, split_axis=0, concat_axis=0, tiled=True)  5.35 us
    pallas_call x1, Pallas kernels, call_block(): pl.pallas_call(block_kernel, out_shape=like((4, 384, 128))[0], in_specs=[...  4.02 us
    unnamed x10, local copies, waits for them, and re-layouts  3.51 us
    pallas_call x1, Pallas kernels, call_join(): pl.pallas_call(join_kernel, out_shape=like((WIDTH, 8, 128), (256, 96), (6...  2.7 us
  transfers between devices with their start and end apart: 3, of which 1 were waited for; matrix products, arithmetic and copies ran while one was open for 0% of the time, Pallas kernels for 1%

profile of v5, /device:TPU:16, one launch (start us, length us, event | category | flops | bytes accessed | tf_op | source)
XLA Modules:
  0.0 52.9 jit_solution(7415825306354051444)
XLA Ops:
  0.6 0.0 copy-start.1
  0.6 1.0 %copy-done.1 = bf16[1,1,1,48,4096]{4,3,2,1,0:T(8,128)(2,1)S(1)} copy-done((bf16[1,1,1,48,4096]{4,3,2,1,0:T(8,128)(2,1)S(1)}, bf16[1,1,1,48,4096]{4,3,2,1,0:T(8,128)(2,1)}, u32[]{:S(2)}) %copy-start.1) | copy-done | bytes 393240
  1.6 0.5 shard_map.84
  2.1 8.4 %collective-permute-start = (bf16[48,128]{1,0:T(8,128)(2,1)S(1)}, bf16[48,128]{1,0:T(8,128)(2,1)S(1)}, u32[]{:S(2)}, u32[]{:S(2)}) collective-permute-start(bf16[48,128]{1,0:T(8,128)(2,1)S(1)} %get-tuple-element.25._), channel_id=1, source_target_pairs={{1,2},{2,1},{3,4},{4,3},{5,6},{6,5},{7,8},{8,7},{9,10},{10,9},{11,... | collective-permute-start | bytes 36872 | tf_op jit(solution)/shard_map/ppermute | solution.py:443
  10.6 0.9 %collective-permute-start.1 = (bf16[48,128]{1,0:T(8,128)(2,1)S(1)}, bf16[48,128]{1,0:T(8,128)(2,1)S(1)}, u32[]{:S(2)}, u32[]{:S(2)}) collective-permute-start(bf16[48,128]{1,0:T(8,128)(2,1)S(1)} %get-tuple-element.26), channel_id=1, source_target_pairs={{0,1},{1,0},{2,3},{3,2},{4,5},{5,4},{6,7},{7,6},{8,9},{9,8},{10,11... | collective-permute-start | bytes 36872 | tf_op jit(solution)/shard_map/ppermute | solution.py:443
  11.4 0.0 copy-start
  11.4 2.5 %copy-done = bf16[1,2,3,3,384,384]{5,4,3,2,1,0:T(8,128)(2,1)S(1)} copy-done((bf16[1,2,3,3,384,384]{5,4,3,2,1,0:T(8,128)(2,1)S(1)}, bf16[1,2,3,3,384,384]{5,4,3,2,1,0:T(8,128)(2,1)}, u32[]{:S(2)}) %copy-start) | copy-done | bytes 5308440
  13.9 0.7 %shard_map.85 = (bf16[48,4224]{1,0:T(8,128)(2,1)S(1)}, bf16[96,1152]{1,0:T(8,128)(2,1)S(1)}, bf16[192,384]{1,0:T(8,128)(2,1)S(1)}, bf16[384,128]{1,0:T(8,128)(2,...) custom-call(bf16[48,4096]{1,0:T(8,128)(2,1)S(1)} %bitcast.11, ...), custom_call_target="tpu_custom_call" | custom-call | flops 1000000000 | bytes 12582912 | tf_op jit(solution)/shard_map/pallas_call | solution.py:382
  14.6 0.0 collective-permute-done.far
  14.6 0.0 collective-permute-done.1.near
  14.6 0.0 copy-start.3
  14.7 0.6 %shard_map.86 = bf16[4,624,128]{2,1,0:T(8,128)(2,1)S(1)} custom-call(bf16[48,128]{1,0:T(8,128)(2,1)S(1)} %collective-permute-done.far, bf16[48,128]{1,0:T(8,128)(2,1)S(1)} %collective-permute-done.1.near, bf16[48,4224]{1,0:T(8,128)(2,1)S(1)} %get-tuple-element.27.refs_0_, bf16[96,1152]{1,0:T(8,128)(2,1)S(1)} %get-tuple-element.28.refs_1_, ...), custom_call_target="tpu_custom_call" | custom-call | tf_op jit(solution)/shard_map/pallas_call | solution.py:399
  15.3 15.0 %all_to_all.10.strips = bf16[4,624,128]{2,1,0:T(8,128)(2,1)S(1)} all-to-all(bf16[4,624,128]{2,1,0:T(8,128)(2,1)S(1)} %shard_map.86), channel_id=1, replica_groups=mesh['branch'=4,'row'=4,'col'=16] {'row'}, dimensions={0} | all-to-all | bytes 1277952 | tf_op jit(solution)/shard_map/all_to_all | solution.py:447
  30.3 0.0 copy-done.3
  30.3 0.0 copy-start.4
  30.3 0.0 copy-start.2
  30.3 4.0 %shard_map.87 = bf16[4,384,128]{2,1,0:T(8,128)(2,1)} custom-call(bf16[4,624,128]{2,1,0:T(8,128)(2,1)S(1)} %all_to_all.10.strips, f32[1,2,384]{2,1,0:T(2,128)S(1)} %copy-done.3, bf16[2,3,48,144]{3,2,1,0:T(8,128)(2,1)S(1)} %get-tuple-element.38.refs_0_, bf16[2,3,96,288]{3,2,1,0:T(8,128)(2,1)S(1)} %get-tuple-element.39.refs_1_, ...), custom_call_target="tpu_custom_call" | custom-call | tf_op jit(solution)/shard_map/pallas_call | solution.py:414
  34.3 5.3 %all-to-all-start.1 = ((bf16[4,384,128]{2,1,0:T(8,128)(2,1)}), bf16[4,384,128]{2,1,0:T(8,128)(2,1)S(1)}, u32[]{:S(2)}, u32[]{:S(2)}) async-start(bf16[4,384,128]{2,1,0:T(8,128)(2,1)} %shard_map.87), calls=%async_computation.1 | async-start | bytes 786432 | tf_op jit(solution)/shard_map/all_to_all | solution.py:447
  39.6 0.0 copy-done.4
  39.6 10.6 %all-to-all-done.1.zb = bf16[4,384,128]{2,1,0:T(8,128)(2,1)S(1)} async-done(((bf16[4,384,128]{2,1,0:T(8,128)(2,1)}), bf16[4,384,128]{2,1,0:T(8,128)(2,1)S(1)}, u32[]{:S(2)}, u32[]{:S(2)}) %all-to-all-start.1) | async-done | bytes 393248 | tf_op jit(solution)/shard_map/all_to_all | solution.py:447
  50.2 0.0 copy-done.2
  50.2 2.7 %shard_map.88 = (bf16[48,8,128]{2,1,0:T(8,128)(2,1)}, bf16[256,96]{1,0:T(8,128)(2,1)}, bf16[64,192]{1,0:T(8,128)(2,1)}, bf16[16,384]{1,0:T(8,128)(2,1)}) custom-call(bf16[4,384,128]{2,1,0:T(8,128)(2,1)S(1)} %all-to-all-done.1.zb, bf16[720,720]{1,0:T(8,128)(2,1)S(1)} %copy-done.2, f32[1,720]{1,0:T(1,128)S(1)} %broadcast_in_dim.3.bias), custom_call_target="tpu_custom_call" | custom-call | tf_op jit(solution)/shard_map/pallas_call | solution.py:425
  (1 shorter events, 0.0 us)
Async XLA Ops:
  0.6 1.0 %copy-start.1 = (bf16[1,1,1,48,4096]{4,3,2,1,0:T(8,128)(2,1)S(1)}, bf16[1,1,1,48,4096]{4,3,2,1,0:T(8,128)(2,1)}, u32[]{:S(2)}) copy-start(bf16[1,1,1,48,4096]{4,3,2,1,0:T(8,128)(2,1)} %param.5) | copy-start | bytes 1179652
  2.1 12.5 %collective-permute-start = (bf16[48,128]{1,0:T(8,128)(2,1)S(1)}, bf16[48,128]{1,0:T(8,128)(2,1)S(1)}, u32[]{:S(2)}, u32[]{:S(2)}) collective-permute-start(bf16[48,128]{1,0:T(8,128)(2,1)S(1)} %get-tuple-element.25._), channel_id=1, source_target_pairs={{1,2},{2,1},{3,4},{4,3},{5,6},{6,5},{7,8},{8,7},{9,10},{10,9},{11,... | collective-permute-start | bytes 36872 | tf_op jit(solution)/shard_map/ppermute | solution.py:443
  10.6 4.1 %collective-permute-start.1 = (bf16[48,128]{1,0:T(8,128)(2,1)S(1)}, bf16[48,128]{1,0:T(8,128)(2,1)S(1)}, u32[]{:S(2)}, u32[]{:S(2)}) collective-permute-start(bf16[48,128]{1,0:T(8,128)(2,1)S(1)} %get-tuple-element.26), channel_id=1, source_target_pairs={{0,1},{1,0},{2,3},{3,2},{4,5},{5,4},{6,7},{7,6},{8,9},{9,8},{10,11... | collective-permute-start | bytes 36872 | tf_op jit(solution)/shard_map/ppermute | solution.py:443
  11.4 2.5 %copy-start = (bf16[1,2,3,3,384,384]{5,4,3,2,1,0:T(8,128)(2,1)S(1)}, bf16[1,2,3,3,384,384]{5,4,3,2,1,0:T(8,128)(2,1)}, u32[]{:S(2)}) copy-start(bf16[1,2,3,3,384,384]{5,4,3,2,1,0:T(8,128)(2,1)} %weight.2) | copy-start | bytes 15925252
  14.6 15.6 %copy-start.3 = (f32[1,2,384]{2,1,0:T(2,128)S(1)}, f32[1,2,384]{2,1,0:T(2,128)}, u32[]{:S(2)}) copy-start(f32[1,2,384]{2,1,0:T(2,128)} %bias.1) | copy-start | bytes 9220
  30.3 9.4 %copy-start.4 = (f32[720]{0:T(1024)S(1)}, f32[720]{0:T(1024)}, u32[]{:S(2)}) copy-start(f32[720]{0:T(1024)} %param.9) | copy-start | bytes 8644
  30.3 20.0 %copy-start.2 = (bf16[720,720]{1,0:T(8,128)(2,1)S(1)}, bf16[720,720]{1,0:T(8,128)(2,1)}, u32[]{:S(2)}) copy-start(bf16[720,720]{1,0:T(8,128)(2,1)} %weight.3) | copy-start | bytes 3110404
  34.3 15.9 %all-to-all-start.1 = ((bf16[4,384,128]{2,1,0:T(8,128)(2,1)}), bf16[4,384,128]{2,1,0:T(8,128)(2,1)S(1)}, u32[]{:S(2)}, u32[]{:S(2)}) async-start(bf16[4,384,128]{2,1,0:T(8,128)(2,1)} %shard_map.87), calls=%async_computation.1 | async-start | bytes 786432 | tf_op jit(solution)/shard_map/all_to_all | solution.py:447

commit v6 on v5

--- a/solution.py
+++ b/solution.py
@@ -102,28 +102,45 @@
     return (k == spot).astype(F32).astype(BF)
 
 
-def prepare_kernel(x, weight, _, *refs):
+def prepare_kernel(x_hbm, weight, _, *refs):
     xp_all, wp_all, places, orders = refs[:4], refs[4:8], refs[8:12], (None,) + refs[12:15]
+    wbuf, sems, x, x_sem = refs[18:]
     st_all = (x,) + refs[15:18]
+    copy = pltpu.make_async_copy(x_hbm, x, x_sem)
+    copy.start()
 
     def body(g):
         c = g.channels
         st, xp, wp = st_all[g.b], xp_all[g.b], wp_all[g.b]
+        cl = up128(c)
+
+        def fetch(layer):
+            return pltpu.make_async_copy(
+                weight.at[0, layer, :, :, 0:c, 0:cl],
+                wbuf.at[layer, :, :, 0:c, 0:cl],
+                sems.at[layer],
+            )
+
+        fetch(0).start()
+        fetch(1).start()
         places[g.b][...] = side_places(g)
         if g.b:
             order = channel_order(g)
             orders[g.b][...] = order
+        xp[...] = jnp.zeros_like(xp)
+        copy.wait()
+        if g.b:
             for q in range(g.parts):
                 st[q * WIDTH : (q + 1) * WIDTH, :] = x[:, q * g.pixels : (q + 1) * g.pixels]
             st[...] = nn(order, st[...]).astype(BF)
-        xp[...] = jnp.zeros_like(xp)
         for y in range(g.rows):
             to = y * g.pitch + 2
             xp[:, to : to + g.cols] = st[:, y * g.cols : (y + 1) * g.cols]
         for layer in range(2):
+            fetch(layer).wait()
             for dy in range(3):
                 for dx in range(3):
-                    tap = weight[0, layer, dy, dx, 0:c, 0:c]
+                    tap = wbuf[layer, dy, dx, 0:c, 0:c]
                     wp[layer, dy, :, c * dx : c * (dx + 1)] = tap
 
     per_branch(body)
@@ -326,16 +343,25 @@
         jnp.concatenate([zb[3, 0:16, :], zb[3, 16:32, :], zb[3, 32:48, :]], axis=1),
     ]
 
-    def block(j, i):
-        gj, gi = GEO[j], GEO[i]
-        return weight[gj.start : gj.start + gj.channels, gi.start : gi.start + gi.channels]
-
-    total = None
-    for i in (1, 2, 3):
-        term = nn(nt(block(0, i), z[i]).astype(BF), repeat_map_t(0, i))
-        total = term if total is None else total + term
+    def block(j, i, last=None):
+        first, end = GEO[j], GEO[j if last is None else last]
+        gi = GEO[i]
+        rows = slice(first.start, end.start + end.channels)
+        return weight[rows, gi.start : gi.start + gi.channels]
+
+    def tn(a, b):
+        return lax.dot_general(a, b, (((0,), (0,)), ((), ())), preferred_element_type=F32)
+
+    size = [g.pixels // 4 for g in GEO]
+    terms = {i: nt(z[i], block(0, i, i - 1)).astype(BF) for i in (1, 2, 3)}
+    shrink0 = jnp.concatenate([repeat_map_t(0, i) for i in (1, 2, 3)], axis=0)
+    shrink1 = jnp.concatenate([repeat_map_t(1, i) for i in (2, 3)], axis=0)
+    sums = {0: nt(shrink0, z[0]), 1: nn(shrink1, z[1]), 2: nn(repeat_map_t(2, 3), z[2])}
+
+    stacked = jnp.concatenate([terms[i][:, 0:WIDTH] for i in (1, 2, 3)], axis=0)
     wide = jnp.broadcast_to(bias[:, 0:WIDTH], (8, WIDTH))
-    total = jnp.maximum(total + z[0].astype(F32) + wide.T[:, 0:1], 0.0)
+    total = tn(stacked, shrink0) + z[0].astype(F32) + wide.T[:, 0:1]
+    total = jnp.maximum(total, 0.0)
     for y in range(8):
         s0[:, y, :] = total[:, 128 * y : 128 * (y + 1)]
     out0[...] = s0[...].astype(BF)
@@ -343,15 +369,13 @@
     for j, out in ((1, out1), (2, out2), (3, out3)):
         g = GEO[j]
         total = z[j].astype(F32) + bias[:, g.start : g.start + g.channels]
-        for i in range(4):
-            if i == j:
-                continue
-            if i < j:
-                sums = (nt if i == 0 else nn)(repeat_map_t(i, j), z[i])
-                mean = (sums * (0.25 ** (j - i))).astype(BF)
-                total = total + nt(mean, block(j, i)).astype(BF).astype(F32)
-            else:
-                total = total + nn(repeat_map(j, i), nt(z[i], block(j, i)).astype(BF))
+        for i in range(j):
+            first = sum(size[i + 1 : j])
+            mean = (sums[i][first : first + size[j], :] * (0.25 ** (j - i))).astype(BF)
+            total = total + nt(mean, block(j, i)).astype(BF).astype(F32)
+        for i in range(j + 1, 4):
+            term = terms[i][:, g.start : g.start + g.channels]
+            total = total + nn(repeat_map(j, i), term)
         out[...] = jnp.maximum(total, 0.0).astype(BF)
 
 
@@ -382,10 +406,12 @@
     made = pl.pallas_call(
         prepare_kernel,
         out_shape=like(*shapes),
-        in_specs=[VMEM, VMEM, pl.BlockSpec(memory_space=pl.ANY)],
+        in_specs=[pl.BlockSpec(memory_space=pltpu.HBM)] * 2 + [pl.BlockSpec(memory_space=pl.ANY)],
         out_specs=(VMEM,) * len(shapes),
-        scratch_shapes=[pltpu.VMEM((g.channels, g.pixels), BF) for g in GEO[1:]],
-        compiler_params=params(),
+        scratch_shapes=[pltpu.VMEM((g.channels, g.pixels), BF) for g in GEO[1:]]
+        + [pltpu.VMEM((2, 3, 3, 384, 384), BF), pltpu.SemaphoreType.DMA((2,))]
+        + [pltpu.VMEM((WIDTH, TH * TW), BF), pltpu.SemaphoreType.DMA],
+        compiler_params=params(42),
         cost_estimate=pl.CostEstimate(flops=10**9, bytes_accessed=12 * 2**20, transcendentals=0),
     )(x, weight, after)
     return made[:4] + made[8:], made[4:8]

time: 53.2 us -> 52.9 us (level)
  local copies, waits for them, and re-layouts: 3.51 us -> 2 us
  starting transfers between devices: 14.6 us -> 16.1 us
    unnamed x10, local copies, waits for them, and re-layouts: 3.51 us -> 2 us
    all_to_all x1, starting transfers between devices: 5.35 us -> 6.77 us  [swapped(): return lax.all_to_all(parts, axis, split_axis=0, concat_axis=0, tiled=True)]
    pallas_call x1, Pallas kernels: 2.7 us -> 1.71 us  [call_join(): pl.pallas_call(join_kernel, out_shape=like((WIDTH, 8, 128), (256, 96), (6...]
    pallas_call x1, Pallas kernels: 0.68 us -> 1.38 us  [call_prepare(): pl.pallas_call(prepare_kernel, out_shape=like(*shapes), in_specs=[pl.Bloc...]
  transfers between devices with their start and end apart: 3 -> 3, of which waited for: 1 -> 1; matrix products, arithmetic and copies ran while one was open for 0% -> 0% of each run, Pallas kernels for 1% -> 3%
where the time goes in v6:
time: 52.9 us; the launch traced here: 52.6 us
  starting transfers between devices  16.1 us (30%)
  blocking collectives  15 us (28%)
  waiting for transfers between devices  10.6 us (20%)
  Pallas kernels  8.21 us (16%)
  local copies, waits for them, and re-layouts  2 us (4%)
  between operations  0.7 us (1%)
    all_to_all x1, blocking collectives, swapped(): return lax.all_to_all(parts, axis, split_axis=0, concat_axis=0, tiled=True)  15 us
    all_to_all x1, waiting for transfers between devices, swapped(): return lax.all_to_all(parts, axis, split_axis=0, concat_axis=0, tiled=True)  10.6 us
    ppermute x2, starting transfers between devices, paired(): return lax.ppermute(shard, 'col', pairs)  9.3 us
    all_to_all x1, starting transfers between devices, swapped(): return lax.all_to_all(parts, axis, split_axis=0, concat_axis=0, tiled=True)  6.77 us
    pallas_call x1, Pallas kernels, call_block(): pl.pallas_call(block_kernel, out_shape=like((4, 384, 128))[0], in_specs=[...  4.02 us
    unnamed x10, local copies, waits for them, and re-layouts  2 us
    pallas_call x1, Pallas kernels, call_join(): pl.pallas_call(join_kernel, out_shape=like((WIDTH, 8, 128), (256, 96), (6...  1.71 us
    pallas_call x1, Pallas kernels, call_prepare(): pl.pallas_call(prepare_kernel, out_shape=like(*shapes), in_specs=[pl.Bloc...  1.38 us
  transfers between devices with their start and end apart: 3, of which 1 were waited for; matrix products, arithmetic and copies ran while one was open for 0% of the time, Pallas kernels for 3%

profile of v6, /device:TPU:16, one launch (start us, length us, event | category | flops | bytes accessed | tf_op | source)
XLA Modules:
  0.0 52.6 jit_solution(8834234120515008322)
XLA Ops:
  0.6 0.0 copy-start
  0.6 1.0 %copy-done = bf16[1,1,1,48,4096]{4,3,2,1,0:T(8,128)(2,1)S(1)} copy-done((bf16[1,1,1,48,4096]{4,3,2,1,0:T(8,128)(2,1)S(1)}, bf16[1,1,1,48,4096]{4,3,2,1,0:T(8,128)(2,1)}, u32[]{:S(2)}) %copy-start) | copy-done | bytes 393240
  1.6 0.5 shard_map.84
  2.1 8.4 %collective-permute-start = (bf16[48,128]{1,0:T(8,128)(2,1)S(1)}, bf16[48,128]{1,0:T(8,128)(2,1)S(1)}, u32[]{:S(2)}, u32[]{:S(2)}) collective-permute-start(bf16[48,128]{1,0:T(8,128)(2,1)S(1)} %get-tuple-element.25._), channel_id=1, source_target_pairs={{1,2},{2,1},{3,4},{4,3},{5,6},{6,5},{7,8},{8,7},{9,10},{10,9},{11,... | collective-permute-start | bytes 36872 | tf_op jit(solution)/shard_map/ppermute | solution.py:469
  10.6 0.9 %collective-permute-start.1 = (bf16[48,128]{1,0:T(8,128)(2,1)S(1)}, bf16[48,128]{1,0:T(8,128)(2,1)S(1)}, u32[]{:S(2)}, u32[]{:S(2)}) collective-permute-start(bf16[48,128]{1,0:T(8,128)(2,1)S(1)} %get-tuple-element.26), channel_id=1, source_target_pairs={{0,1},{1,0},{2,3},{3,2},{4,5},{5,4},{6,7},{7,6},{8,9},{9,8},{10,11... | collective-permute-start | bytes 36872 | tf_op jit(solution)/shard_map/ppermute | solution.py:469
  11.4 0.0 copy-start.1
  11.4 1.0 %copy-done.1 = bf16[1,1,1,48,4096]{4,3,2,1,0:T(8,128)(2,1)S(1)} copy-done((bf16[1,1,1,48,4096]{4,3,2,1,0:T(8,128)(2,1)S(1)}, bf16[1,1,1,48,4096]{4,3,2,1,0:T(8,128)(2,1)}, u32[]{:S(2)}) %copy-start.1) | copy-done | bytes 393240
  12.4 1.4 %shard_map.85 = (bf16[48,4224]{1,0:T(8,128)(2,1)S(1)}, bf16[96,1152]{1,0:T(8,128)(2,1)S(1)}, bf16[192,384]{1,0:T(8,128)(2,1)S(1)}, bf16[384,128]{1,0:T(8,128)(2,...) custom-call(bf16[48,4096]{1,0:T(8,128)(2,1)S(1)} %bitcast.11, ...), custom_call_target="tpu_custom_call" | custom-call | flops 1000000000 | bytes 12582912 | tf_op jit(solution)/shard_map/pallas_call | solution.py:406
  13.8 0.0 collective-permute-done.far
  13.8 0.0 collective-permute-done.1.near
  13.8 0.0 copy-start.3
  13.8 0.6 %shard_map.86 = bf16[4,624,128]{2,1,0:T(8,128)(2,1)S(1)} custom-call(bf16[48,128]{1,0:T(8,128)(2,1)S(1)} %collective-permute-done.far, bf16[48,128]{1,0:T(8,128)(2,1)S(1)} %collective-permute-done.1.near, bf16[48,4224]{1,0:T(8,128)(2,1)S(1)} %get-tuple-element.27.refs_0_, bf16[96,1152]{1,0:T(8,128)(2,1)S(1)} %get-tuple-element.28.refs_1_, ...), custom_call_target="tpu_custom_call" | custom-call | tf_op jit(solution)/shard_map/pallas_call | solution.py:425
  14.5 15.0 %all_to_all.10.strips = bf16[4,624,128]{2,1,0:T(8,128)(2,1)S(1)} all-to-all(bf16[4,624,128]{2,1,0:T(8,128)(2,1)S(1)} %shard_map.86), channel_id=1, replica_groups=mesh['branch'=4,'row'=4,'col'=16] {'row'}, dimensions={0} | all-to-all | bytes 1277952 | tf_op jit(solution)/shard_map/all_to_all | solution.py:473
  29.5 0.0 copy-done.3
  29.5 0.0 copy-start.4
  29.5 0.0 copy-start.2
  29.5 4.0 %shard_map.87 = bf16[4,384,128]{2,1,0:T(8,128)(2,1)} custom-call(bf16[4,624,128]{2,1,0:T(8,128)(2,1)S(1)} %all_to_all.10.strips, f32[1,2,384]{2,1,0:T(2,128)S(1)} %copy-done.3, bf16[2,3,48,144]{3,2,1,0:T(8,128)(2,1)S(1)} %get-tuple-element.38.refs_0_, bf16[2,3,96,288]{3,2,1,0:T(8,128)(2,1)S(1)} %get-tuple-element.39.refs_1_, ...), custom_call_target="tpu_custom_call" | custom-call | tf_op jit(solution)/shard_map/pallas_call | solution.py:440
  33.5 6.8 %all-to-all-start.1 = ((bf16[4,384,128]{2,1,0:T(8,128)(2,1)}), bf16[4,384,128]{2,1,0:T(8,128)(2,1)S(1)}, u32[]{:S(2)}, u32[]{:S(2)}) async-start(bf16[4,384,128]{2,1,0:T(8,128)(2,1)} %shard_map.87), calls=%async_computation.1 | async-start | bytes 786432 | tf_op jit(solution)/shard_map/all_to_all | solution.py:473
  40.3 0.0 copy-done.4
  40.3 10.6 %all-to-all-done.1.zb = bf16[4,384,128]{2,1,0:T(8,128)(2,1)S(1)} async-done(((bf16[4,384,128]{2,1,0:T(8,128)(2,1)}), bf16[4,384,128]{2,1,0:T(8,128)(2,1)S(1)}, u32[]{:S(2)}, u32[]{:S(2)}) %all-to-all-start.1) | async-done | bytes 393248 | tf_op jit(solution)/shard_map/all_to_all | solution.py:473
  50.9 0.0 copy-done.2
  50.9 1.7 %shard_map.88 = (bf16[48,8,128]{2,1,0:T(8,128)(2,1)}, bf16[256,96]{1,0:T(8,128)(2,1)}, bf16[64,192]{1,0:T(8,128)(2,1)}, bf16[16,384]{1,0:T(8,128)(2,1)}) custom-call(bf16[4,384,128]{2,1,0:T(8,128)(2,1)S(1)} %all-to-all-done.1.zb, bf16[720,720]{1,0:T(8,128)(2,1)S(1)} %copy-done.2, f32[1,720]{1,0:T(1,128)S(1)} %broadcast_in_dim.3.bias), custom_call_target="tpu_custom_call" | custom-call | tf_op jit(solution)/shard_map/pallas_call | solution.py:451
  (1 shorter events, 0.0 us)
Async XLA Ops:
  0.6 1.0 %copy-start = (bf16[1,1,1,48,4096]{4,3,2,1,0:T(8,128)(2,1)S(1)}, bf16[1,1,1,48,4096]{4,3,2,1,0:T(8,128)(2,1)}, u32[]{:S(2)}) copy-start(bf16[1,1,1,48,4096]{4,3,2,1,0:T(8,128)(2,1)} %param.5) | copy-start | bytes 1179652
  2.1 11.7 %collective-permute-start = (bf16[48,128]{1,0:T(8,128)(2,1)S(1)}, bf16[48,128]{1,0:T(8,128)(2,1)S(1)}, u32[]{:S(2)}, u32[]{:S(2)}) collective-permute-start(bf16[48,128]{1,0:T(8,128)(2,1)S(1)} %get-tuple-element.25._), channel_id=1, source_target_pairs={{1,2},{2,1},{3,4},{4,3},{5,6},{6,5},{7,8},{8,7},{9,10},{10,9},{11,... | collective-permute-start | bytes 36872 | tf_op jit(solution)/shard_map/ppermute | solution.py:469
  10.6 3.3 %collective-permute-start.1 = (bf16[48,128]{1,0:T(8,128)(2,1)S(1)}, bf16[48,128]{1,0:T(8,128)(2,1)S(1)}, u32[]{:S(2)}, u32[]{:S(2)}) collective-permute-start(bf16[48,128]{1,0:T(8,128)(2,1)S(1)} %get-tuple-element.26), channel_id=1, source_target_pairs={{0,1},{1,0},{2,3},{3,2},{4,5},{5,4},{6,7},{7,6},{8,9},{9,8},{10,11... | collective-permute-start | bytes 36872 | tf_op jit(solution)/shard_map/ppermute | solution.py:469
  11.4 1.0 %copy-start.1 = (bf16[1,1,1,48,4096]{4,3,2,1,0:T(8,128)(2,1)S(1)}, bf16[1,1,1,48,4096]{4,3,2,1,0:T(8,128)(2,1)}, u32[]{:S(2)}) copy-start(bf16[1,1,1,48,4096]{4,3,2,1,0:T(8,128)(2,1)} %param.5) | copy-start | bytes 1179652
  13.8 15.6 %copy-start.3 = (f32[1,2,384]{2,1,0:T(2,128)S(1)}, f32[1,2,384]{2,1,0:T(2,128)}, u32[]{:S(2)}) copy-start(f32[1,2,384]{2,1,0:T(2,128)} %bias.1) | copy-start | bytes 9220
  29.5 10.8 %copy-start.4 = (f32[720]{0:T(1024)S(1)}, f32[720]{0:T(1024)}, u32[]{:S(2)}) copy-start(f32[720]{0:T(1024)} %param.9) | copy-start | bytes 8644
  29.5 21.4 %copy-start.2 = (bf16[720,720]{1,0:T(8,128)(2,1)S(1)}, bf16[720,720]{1,0:T(8,128)(2,1)}, u32[]{:S(2)}) copy-start(bf16[720,720]{1,0:T(8,128)(2,1)} %weight.3) | copy-start | bytes 3110404
  33.5 17.4 %all-to-all-start.1 = ((bf16[4,384,128]{2,1,0:T(8,128)(2,1)}), bf16[4,384,128]{2,1,0:T(8,128)(2,1)S(1)}, u32[]{:S(2)}, u32[]{:S(2)}) async-start(bf16[4,384,128]{2,1,0:T(8,128)(2,1)} %shard_map.87), calls=%async_computation.1 | async-start | bytes 786432 | tf_op jit(solution)/shard_map/all_to_all | solution.py:473

commit v7 on v6

--- a/solution.py
+++ b/solution.py
@@ -41,6 +41,7 @@
 
 GEO = [Geo(b) for b in range(4)]
 SLOT_ROWS = 624
+PREPARE_MIB = 42
 STEPS = (640, 768, 512, 384)
 
 
@@ -121,8 +122,17 @@
                 sems.at[layer],
             )
 
-        fetch(0).start()
-        fetch(1).start()
+        def fetch_tap(n):
+            layer, dy, dx = n // 9, n // 3 % 3, n % 3
+            return pltpu.make_async_copy(
+                weight.at[0, layer, dy, dx],
+                wp.at[layer, dy, :, c * dx : c * (dx + 1)],
+                sems.at[n],
+            )
+
+        fetches = [fetch_tap(n) for n in range(18)] if g.b == 3 else [fetch(0), fetch(1)]
+        for each in fetches:
+            each.start()
         places[g.b][...] = side_places(g)
         if g.b:
             order = channel_order(g)
@@ -136,8 +146,9 @@
         for y in range(g.rows):
             to = y * g.pitch + 2
             xp[:, to : to + g.cols] = st[:, y * g.cols : (y + 1) * g.cols]
-        for layer in range(2):
-            fetch(layer).wait()
+        for each in fetches:
+            each.wait()
+        for layer in range(2 if g.b < 3 else 0):
             for dy in range(3):
                 for dx in range(3):
                     tap = wbuf[layer, dy, dx, 0:c, 0:c]
@@ -257,14 +268,18 @@
         def conv(layer, maps, size, n, finish):
             maps[0:c, 1:size] = maps[c : 2 * c, 0 : size - 1]
             maps[2 * c : 3 * c, 0 : size - 1] = maps[c : 2 * c, 1:size]
+            thirds = [slice(0, 3 * c)]
+            if g.b == 3:
+                thirds = [slice(c * third, c * (third + 1)) for third in (1, 0, 2)]
             step = STEPS[g.b]
             for at in range(0, n, step):
                 width = min(step, n - at)
                 total = None
-                for dy in range(3):
-                    lane = at + dy * g.wide
-                    term = nn(wp[layer, dy], maps[:, lane : lane + width])
-                    total = term if total is None else total + term
+                for part in thirds:
+                    for dy in range(3):
+                        lane = at + dy * g.wide
+                        term = nn(wp[layer, dy, :, part], maps[part, lane : lane + width])
+                        total = term if total is None else total + term
                 finish(at, width, total)
 
         bias0 = column(0)
@@ -409,9 +424,9 @@
         in_specs=[pl.BlockSpec(memory_space=pltpu.HBM)] * 2 + [pl.BlockSpec(memory_space=pl.ANY)],
         out_specs=(VMEM,) * len(shapes),
         scratch_shapes=[pltpu.VMEM((g.channels, g.pixels), BF) for g in GEO[1:]]
-        + [pltpu.VMEM((2, 3, 3, 384, 384), BF), pltpu.SemaphoreType.DMA((2,))]
+        + [pltpu.VMEM((2, 3, 3, 192, 256), BF), pltpu.SemaphoreType.DMA((18,))]
         + [pltpu.VMEM((WIDTH, TH * TW), BF), pltpu.SemaphoreType.DMA],
-        compiler_params=params(42),
+        compiler_params=params(PREPARE_MIB),
         cost_estimate=pl.CostEstimate(flops=10**9, bytes_accessed=12 * 2**20, transcendentals=0),
     )(x, weight, after)
     return made[:4] + made[8:], made[4:8]

time: 52.9 us -> 52.7 us (level)
  no operation moved by 1% of the time
where the time goes in v7:
time: 52.7 us; the launch traced here: 52.4 us
  starting transfers between devices  15.8 us (30%)
  blocking collectives  15 us (28%)
  waiting for transfers between devices  10.6 us (20%)
  Pallas kernels  8.34 us (16%)
  local copies, waits for them, and re-layouts  2 us (4%)
  between operations  0.7 us (1%)
    all_to_all x1, blocking collectives, swapped(): return lax.all_to_all(parts, axis, split_axis=0, concat_axis=0, tiled=True)  15 us
    all_to_all x1, waiting for transfers between devices, swapped(): return lax.all_to_all(parts, axis, split_axis=0, concat_axis=0, tiled=True)  10.6 us
    ppermute x2, starting transfers between devices, paired(): return lax.ppermute(shard, 'col', pairs)  9.3 us
    all_to_all x1, starting transfers between devices, swapped(): return lax.all_to_all(parts, axis, split_axis=0, concat_axis=0, tiled=True)  6.49 us
    pallas_call x1, Pallas kernels, call_block(): pl.pallas_call(block_kernel, out_shape=like((4, 384, 128))[0], in_specs=[...  4.02 us
    unnamed x10, local copies, waits for them, and re-layouts  2 us
    pallas_call x1, Pallas kernels, call_join(): pl.pallas_call(join_kernel, out_shape=like((WIDTH, 8, 128), (256, 96), (6...  1.71 us
    pallas_call x1, Pallas kernels, call_prepare(): pl.pallas_call(prepare_kernel, out_shape=like(*shapes), in_specs=[pl.Bloc...  1.5 us
  transfers between devices with their start and end apart: 3, of which 1 were waited for; matrix products, arithmetic and copies ran while one was open for 0% of the time, Pallas kernels for 3%

profile of v7, /device:TPU:16, one launch (start us, length us, event | category | flops | bytes accessed | tf_op | source)
XLA Modules:
  0.0 52.4 jit_solution(3449674909790830995)
XLA Ops:
  0.6 0.0 copy-start
  0.6 1.0 %copy-done = bf16[1,1,1,48,4096]{4,3,2,1,0:T(8,128)(2,1)S(1)} copy-done((bf16[1,1,1,48,4096]{4,3,2,1,0:T(8,128)(2,1)S(1)}, bf16[1,1,1,48,4096]{4,3,2,1,0:T(8,128)(2,1)}, u32[]{:S(2)}) %copy-start) | copy-done | bytes 393240
  1.6 0.5 shard_map.84
  2.1 8.4 %collective-permute-start = (bf16[48,128]{1,0:T(8,128)(2,1)S(1)}, bf16[48,128]{1,0:T(8,128)(2,1)S(1)}, u32[]{:S(2)}, u32[]{:S(2)}) collective-permute-start(bf16[48,128]{1,0:T(8,128)(2,1)S(1)} %get-tuple-element.25._), channel_id=1, source_target_pairs={{1,2},{2,1},{3,4},{4,3},{5,6},{6,5},{7,8},{8,7},{9,10},{10,9},{11,... | collective-permute-start | bytes 36872 | tf_op jit(solution)/shard_map/ppermute | solution.py:484
  10.6 0.9 %collective-permute-start.1 = (bf16[48,128]{1,0:T(8,128)(2,1)S(1)}, bf16[48,128]{1,0:T(8,128)(2,1)S(1)}, u32[]{:S(2)}, u32[]{:S(2)}) collective-permute-start(bf16[48,128]{1,0:T(8,128)(2,1)S(1)} %get-tuple-element.26), channel_id=1, source_target_pairs={{0,1},{1,0},{2,3},{3,2},{4,5},{5,4},{6,7},{7,6},{8,9},{9,8},{10,11... | collective-permute-start | bytes 36872 | tf_op jit(solution)/shard_map/ppermute | solution.py:484
  11.4 0.0 copy-start.1
  11.4 1.0 %copy-done.1 = bf16[1,1,1,48,4096]{4,3,2,1,0:T(8,128)(2,1)S(1)} copy-done((bf16[1,1,1,48,4096]{4,3,2,1,0:T(8,128)(2,1)S(1)}, bf16[1,1,1,48,4096]{4,3,2,1,0:T(8,128)(2,1)}, u32[]{:S(2)}) %copy-start.1) | copy-done | bytes 393240
  12.4 1.5 %shard_map.85 = (bf16[48,4224]{1,0:T(8,128)(2,1)S(1)}, bf16[96,1152]{1,0:T(8,128)(2,1)S(1)}, bf16[192,384]{1,0:T(8,128)(2,1)S(1)}, bf16[384,128]{1,0:T(8,128)(2,...) custom-call(bf16[48,4096]{1,0:T(8,128)(2,1)S(1)} %bitcast.11, ...), custom_call_target="tpu_custom_call" | custom-call | flops 1000000000 | bytes 12582912 | tf_op jit(solution)/shard_map/pallas_call | solution.py:421
  13.9 0.0 collective-permute-done.far
  13.9 0.0 collective-permute-done.1.near
  14.0 0.0 copy-start.3
  14.0 0.6 %shard_map.86 = bf16[4,624,128]{2,1,0:T(8,128)(2,1)S(1)} custom-call(bf16[48,128]{1,0:T(8,128)(2,1)S(1)} %collective-permute-done.far, bf16[48,128]{1,0:T(8,128)(2,1)S(1)} %collective-permute-done.1.near, bf16[48,4224]{1,0:T(8,128)(2,1)S(1)} %get-tuple-element.27.refs_0_, bf16[96,1152]{1,0:T(8,128)(2,1)S(1)} %get-tuple-element.28.refs_1_, ...), custom_call_target="tpu_custom_call" | custom-call | tf_op jit(solution)/shard_map/pallas_call | solution.py:440
  14.6 15.0 %all_to_all.10.strips = bf16[4,624,128]{2,1,0:T(8,128)(2,1)S(1)} all-to-all(bf16[4,624,128]{2,1,0:T(8,128)(2,1)S(1)} %shard_map.86), channel_id=1, replica_groups=mesh['branch'=4,'row'=4,'col'=16] {'row'}, dimensions={0} | all-to-all | bytes 1277952 | tf_op jit(solution)/shard_map/all_to_all | solution.py:488
  29.6 0.0 copy-done.3
  29.6 0.0 copy-start.4
  29.6 0.0 copy-start.2
  29.6 4.0 %shard_map.87 = bf16[4,384,128]{2,1,0:T(8,128)(2,1)} custom-call(bf16[4,624,128]{2,1,0:T(8,128)(2,1)S(1)} %all_to_all.10.strips, f32[1,2,384]{2,1,0:T(2,128)S(1)} %copy-done.3, bf16[2,3,48,144]{3,2,1,0:T(8,128)(2,1)S(1)} %get-tuple-element.38.refs_0_, bf16[2,3,96,288]{3,2,1,0:T(8,128)(2,1)S(1)} %get-tuple-element.39.refs_1_, ...), custom_call_target="tpu_custom_call" | custom-call | tf_op jit(solution)/shard_map/pallas_call | solution.py:455
  33.6 6.5 %all-to-all-start.1 = ((bf16[4,384,128]{2,1,0:T(8,128)(2,1)}), bf16[4,384,128]{2,1,0:T(8,128)(2,1)S(1)}, u32[]{:S(2)}, u32[]{:S(2)}) async-start(bf16[4,384,128]{2,1,0:T(8,128)(2,1)} %shard_map.87), calls=%async_computation.1 | async-start | bytes 786432 | tf_op jit(solution)/shard_map/all_to_all | solution.py:488
  40.1 0.0 copy-done.4
  40.1 10.6 %all-to-all-done.1.zb = bf16[4,384,128]{2,1,0:T(8,128)(2,1)S(1)} async-done(((bf16[4,384,128]{2,1,0:T(8,128)(2,1)}), bf16[4,384,128]{2,1,0:T(8,128)(2,1)S(1)}, u32[]{:S(2)}, u32[]{:S(2)}) %all-to-all-start.1) | async-done | bytes 393248 | tf_op jit(solution)/shard_map/all_to_all | solution.py:488
  50.7 0.0 copy-done.2
  50.7 1.7 %shard_map.88 = (bf16[48,8,128]{2,1,0:T(8,128)(2,1)}, bf16[256,96]{1,0:T(8,128)(2,1)}, bf16[64,192]{1,0:T(8,128)(2,1)}, bf16[16,384]{1,0:T(8,128)(2,1)}) custom-call(bf16[4,384,128]{2,1,0:T(8,128)(2,1)S(1)} %all-to-all-done.1.zb, bf16[720,720]{1,0:T(8,128)(2,1)S(1)} %copy-done.2, f32[1,720]{1,0:T(1,128)S(1)} %broadcast_in_dim.3.bias), custom_call_target="tpu_custom_call" | custom-call | tf_op jit(solution)/shard_map/pallas_call | solution.py:466
  (1 shorter events, 0.0 us)
Async XLA Ops:
  0.6 1.0 %copy-start = (bf16[1,1,1,48,4096]{4,3,2,1,0:T(8,128)(2,1)S(1)}, bf16[1,1,1,48,4096]{4,3,2,1,0:T(8,128)(2,1)}, u32[]{:S(2)}) copy-start(bf16[1,1,1,48,4096]{4,3,2,1,0:T(8,128)(2,1)} %param.5) | copy-start | bytes 1179652
  2.1 11.8 %collective-permute-start = (bf16[48,128]{1,0:T(8,128)(2,1)S(1)}, bf16[48,128]{1,0:T(8,128)(2,1)S(1)}, u32[]{:S(2)}, u32[]{:S(2)}) collective-permute-start(bf16[48,128]{1,0:T(8,128)(2,1)S(1)} %get-tuple-element.25._), channel_id=1, source_target_pairs={{1,2},{2,1},{3,4},{4,3},{5,6},{6,5},{7,8},{8,7},{9,10},{10,9},{11,... | collective-permute-start | bytes 36872 | tf_op jit(solution)/shard_map/ppermute | solution.py:484
  10.6 3.4 %collective-permute-start.1 = (bf16[48,128]{1,0:T(8,128)(2,1)S(1)}, bf16[48,128]{1,0:T(8,128)(2,1)S(1)}, u32[]{:S(2)}, u32[]{:S(2)}) collective-permute-start(bf16[48,128]{1,0:T(8,128)(2,1)S(1)} %get-tuple-element.26), channel_id=1, source_target_pairs={{0,1},{1,0},{2,3},{3,2},{4,5},{5,4},{6,7},{7,6},{8,9},{9,8},{10,11... | collective-permute-start | bytes 36872 | tf_op jit(solution)/shard_map/ppermute | solution.py:484
  11.4 1.0 %copy-start.1 = (bf16[1,1,1,48,4096]{4,3,2,1,0:T(8,128)(2,1)S(1)}, bf16[1,1,1,48,4096]{4,3,2,1,0:T(8,128)(2,1)}, u32[]{:S(2)}) copy-start(bf16[1,1,1,48,4096]{4,3,2,1,0:T(8,128)(2,1)} %param.5) | copy-start | bytes 1179652
  14.0 15.6 %copy-start.3 = (f32[1,2,384]{2,1,0:T(2,128)S(1)}, f32[1,2,384]{2,1,0:T(2,128)}, u32[]{:S(2)}) copy-start(f32[1,2,384]{2,1,0:T(2,128)} %bias.1) | copy-start | bytes 9220
  29.6 10.5 %copy-start.4 = (f32[720]{0:T(1024)S(1)}, f32[720]{0:T(1024)}, u32[]{:S(2)}) copy-start(f32[720]{0:T(1024)} %param.9) | copy-start | bytes 8644
  29.6 21.1 %copy-start.2 = (bf16[720,720]{1,0:T(8,128)(2,1)S(1)}, bf16[720,720]{1,0:T(8,128)(2,1)}, u32[]{:S(2)}) copy-start(bf16[720,720]{1,0:T(8,128)(2,1)} %weight.3) | copy-start | bytes 3110404
  33.6 17.1 %all-to-all-start.1 = ((bf16[4,384,128]{2,1,0:T(8,128)(2,1)}), bf16[4,384,128]{2,1,0:T(8,128)(2,1)S(1)}, u32[]{:S(2)}, u32[]{:S(2)}) async-start(bf16[4,384,128]{2,1,0:T(8,128)(2,1)} %shard_map.87), calls=%async_computation.1 | async-start | bytes 786432 | tf_op jit(solution)/shard_map/all_to_all | solution.py:488

commit v8 on v7

--- a/solution.py
+++ b/solution.py
@@ -58,7 +58,7 @@
             body(g)
 
 
-def cols_kernel(x, far, near, west, east):
+def cols_kernel(x, far, near, kept, west, east):
     def body(g):
         for q in range(g.parts):
             for y in range(g.rows):
@@ -69,6 +69,7 @@
                 east[:, at : at + 2] = x[:, last : last + 2]
 
     per_branch(body)
+    kept[...] = x[...]
     odd = place()[2] % 2
 
     @pl.when(odd == 0)
@@ -103,12 +104,9 @@
     return (k == spot).astype(F32).astype(BF)
 
 
-def prepare_kernel(x_hbm, weight, _, *refs):
+def prepare_kernel(x, weight, *refs):
     xp_all, wp_all, places, orders = refs[:4], refs[4:8], refs[8:12], (None,) + refs[12:15]
-    wbuf, sems, x, x_sem = refs[18:]
-    st_all = (x,) + refs[15:18]
-    copy = pltpu.make_async_copy(x_hbm, x, x_sem)
-    copy.start()
+    st_all, wbuf, sems = (x,) + refs[15:18], refs[18], refs[19]
 
     def body(g):
         c = g.channels
@@ -138,7 +136,6 @@
             order = channel_order(g)
             orders[g.b][...] = order
         xp[...] = jnp.zeros_like(xp)
-        copy.wait()
         if g.b:
             for q in range(g.parts):
                 st[q * WIDTH : (q + 1) * WIDTH, :] = x[:, q * g.pixels : (q + 1) * g.pixels]
@@ -405,15 +402,15 @@
 def call_cols(x):
     return pl.pallas_call(
         cols_kernel,
-        out_shape=like((WIDTH, 128), (WIDTH, 128)),
+        out_shape=like((WIDTH, 128), (WIDTH, 128), (WIDTH, TH * TW)),
         in_specs=[VMEM],
-        out_specs=(VMEM, VMEM),
+        out_specs=(VMEM,) * 3,
         scratch_shapes=[pltpu.VMEM((WIDTH, 128), BF)] * 2,
         compiler_params=params(),
     )(x)
 
 
-def call_prepare(x, weight, after):
+def call_prepare(x, weight):
     shapes = [(g.channels, g.padded) for g in GEO]
     shapes += [(2, 3, g.channels, 3 * g.channels) for g in GEO]
     shapes += [(g.sides, g.padded) for g in GEO]
@@ -421,14 +418,13 @@
     made = pl.pallas_call(
         prepare_kernel,
         out_shape=like(*shapes),
-        in_specs=[pl.BlockSpec(memory_space=pltpu.HBM)] * 2 + [pl.BlockSpec(memory_space=pl.ANY)],
+        in_specs=[VMEM, pl.BlockSpec(memory_space=pltpu.HBM)],
         out_specs=(VMEM,) * len(shapes),
         scratch_shapes=[pltpu.VMEM((g.channels, g.pixels), BF) for g in GEO[1:]]
-        + [pltpu.VMEM((2, 3, 3, 192, 256), BF), pltpu.SemaphoreType.DMA((18,))]
-        + [pltpu.VMEM((WIDTH, TH * TW), BF), pltpu.SemaphoreType.DMA],
+        + [pltpu.VMEM((2, 3, 3, 192, 256), BF), pltpu.SemaphoreType.DMA((18,))],
         compiler_params=params(PREPARE_MIB),
         cost_estimate=pl.CostEstimate(flops=10**9, bytes_accessed=12 * 2**20, transcendentals=0),
-    )(x, weight, after)
+    )(x, weight)
     return made[:4] + made[8:], made[4:8]
 
 
@@ -490,8 +486,8 @@
 
 def local(section_in, conv_weight, conv_bias, join_weight, join_bias):
     x = section_in[0, 0, 0]
-    far, near = call_cols(x)
-    padded, weights = call_prepare(x, conv_weight, far)
+    far, near, kept = call_cols(x)
+    padded, weights = call_prepare(kept, conv_weight)
     strips = call_strips(paired(far, 1), paired(near, 0), padded)
     settled = call_block(swapped(strips, "row"), conv_bias, weights)
     out = call_join(swapped(settled, "branch"), join_weight, join_bias[None, :])

time: 52.7 us -> 51.4 us (0.975)
  local copies, waits for them, and re-layouts: 2 us -> 1.01 us
    unnamed x10 -> x8, local copies, waits for them, and re-layouts: 2 us -> 1 us
  transfers between devices with their start and end apart: 3 -> 3, of which waited for: 1 -> 1; matrix products, arithmetic and copies ran while one was open for 0% -> 0% of each run, Pallas kernels for 3% -> 2%
where the time goes in v8:
time: 51.4 us; the launch traced here: 51.1 us
  starting transfers between devices  16 us (31%)
  blocking collectives  15 us (29%)
  waiting for transfers between devices  10.3 us (20%)
  Pallas kernels  8.15 us (16%)
  local copies, waits for them, and re-layouts  1.01 us (2%)
  between operations  0.7 us (1%)
    all_to_all x1, blocking collectives, swapped(): return lax.all_to_all(parts, axis, split_axis=0, concat_axis=0, tiled=True)  15 us
    all_to_all x1, waiting for transfers between devices, swapped(): return lax.all_to_all(parts, axis, split_axis=0, concat_axis=0, tiled=True)  10.3 us
    ppermute x2, starting transfers between devices, paired(): return lax.ppermute(shard, 'col', pairs)  9.3 us
    all_to_all x1, starting transfers between devices, swapped(): return lax.all_to_all(parts, axis, split_axis=0, concat_axis=0, tiled=True)  6.68 us
    pallas_call x1, Pallas kernels, call_block(): pl.pallas_call(block_kernel, out_shape=like((4, 384, 128))[0], in_specs=[...  4.05 us
    pallas_call x1, Pallas kernels, call_join(): pl.pallas_call(join_kernel, out_shape=like((WIDTH, 8, 128), (256, 96), (6...  1.71 us
    pallas_call x1, Pallas kernels, call_prepare(): pl.pallas_call(prepare_kernel, out_shape=like(*shapes), in_specs=[VMEM, p...  1.26 us
  transfers between devices with their start and end apart: 3, of which 1 were waited for; matrix products, arithmetic and copies ran while one was open for 0% of the time, Pallas kernels for 2%

profile of v8, /device:TPU:16, one launch (start us, length us, event | category | flops | bytes accessed | tf_op | source)
XLA Modules:
  0.0 51.1 jit_solution(4227668069695253972)
XLA Ops:
  0.6 0.0 copy-start.1
  0.6 1.0 %copy-done.1 = bf16[1,1,1,48,4096]{4,3,2,1,0:T(8,128)(2,1)S(1)} copy-done((bf16[1,1,1,48,4096]{4,3,2,1,0:T(8,128)(2,1)S(1)}, bf16[1,1,1,48,4096]{4,3,2,1,0:T(8,128)(2,1)}, u32[]{:S(2)}) %copy-start.1) | copy-done | bytes 393240
  1.6 0.5 shard_map.84
  2.1 8.4 %collective-permute-start = (bf16[48,128]{1,0:T(8,128)(2,1)S(1)}, bf16[48,128]{1,0:T(8,128)(2,1)S(1)}, u32[]{:S(2)}, u32[]{:S(2)}) collective-permute-start(bf16[48,128]{1,0:T(8,128)(2,1)S(1)} %get-tuple-element.26), channel_id=1, source_target_pairs={{1,2},{2,1},{3,4},{4,3},{5,6},{6,5},{7,8},{8,7},{9,10},{10,9},{11,... | collective-permute-start | bytes 36872 | tf_op jit(solution)/shard_map/ppermute | solution.py:480
  10.6 0.9 %collective-permute-start.1 = (bf16[48,128]{1,0:T(8,128)(2,1)S(1)}, bf16[48,128]{1,0:T(8,128)(2,1)S(1)}, u32[]{:S(2)}, u32[]{:S(2)}) collective-permute-start(bf16[48,128]{1,0:T(8,128)(2,1)S(1)} %get-tuple-element.27), channel_id=1, source_target_pairs={{0,1},{1,0},{2,3},{3,2},{4,5},{5,4},{6,7},{7,6},{8,9},{9,8},{10,11... | collective-permute-start | bytes 36872 | tf_op jit(solution)/shard_map/ppermute | solution.py:480
  11.4 1.3 %shard_map.85 = (bf16[48,4224]{1,0:T(8,128)(2,1)S(1)}, bf16[96,1152]{1,0:T(8,128)(2,1)S(1)}, bf16[192,384]{1,0:T(8,128)(2,1)S(1)}, bf16[384,128]{1,0:T(8,128)(2,...) custom-call(bf16[48,4096]{1,0:T(8,128)(2,1)S(1)} %get-tuple-element., ...), custom_call_target="tpu_custom_call" | custom-call | flops 1000000000 | bytes 12582912 | tf_op jit(solution)/shard_map/pallas_call | solution.py:418
  12.7 0.0 collective-permute-done.far
  12.7 0.0 collective-permute-done.1.near
  12.7 0.0 copy-start.2
  12.8 0.6 %shard_map.86 = bf16[4,624,128]{2,1,0:T(8,128)(2,1)S(1)} custom-call(bf16[48,128]{1,0:T(8,128)(2,1)S(1)} %collective-permute-done.far, bf16[48,128]{1,0:T(8,128)(2,1)S(1)} %collective-permute-done.1.near, bf16[48,4224]{1,0:T(8,128)(2,1)S(1)} %get-tuple-element.29.refs_0_, bf16[96,1152]{1,0:T(8,128)(2,1)S(1)} %get-tuple-element.30.refs_1_, ...), custom_call_target="tpu_custom_call" | custom-call | tf_op jit(solution)/shard_map/pallas_call | solution.py:436
  13.4 15.0 %all_to_all.10.strips = bf16[4,624,128]{2,1,0:T(8,128)(2,1)S(1)} all-to-all(bf16[4,624,128]{2,1,0:T(8,128)(2,1)S(1)} %shard_map.86), channel_id=1, replica_groups=mesh['branch'=4,'row'=4,'col'=16] {'row'}, dimensions={0} | all-to-all | bytes 1277952 | tf_op jit(solution)/shard_map/all_to_all | solution.py:484
  28.4 0.0 copy-done.2
  28.4 0.0 copy-start.3
  28.4 0.0 copy-start
  28.4 4.1 %shard_map.87 = bf16[4,384,128]{2,1,0:T(8,128)(2,1)} custom-call(bf16[4,624,128]{2,1,0:T(8,128)(2,1)S(1)} %all_to_all.10.strips, f32[1,2,384]{2,1,0:T(2,128)S(1)} %copy-done.2, bf16[2,3,48,144]{3,2,1,0:T(8,128)(2,1)S(1)} %get-tuple-element.40.refs_0_, bf16[2,3,96,288]{3,2,1,0:T(8,128)(2,1)S(1)} %get-tuple-element.41.refs_1_, ...), custom_call_target="tpu_custom_call" | custom-call | tf_op jit(solution)/shard_map/pallas_call | solution.py:451
  32.4 6.7 %all-to-all-start.1 = ((bf16[4,384,128]{2,1,0:T(8,128)(2,1)}), bf16[4,384,128]{2,1,0:T(8,128)(2,1)S(1)}, u32[]{:S(2)}, u32[]{:S(2)}) async-start(bf16[4,384,128]{2,1,0:T(8,128)(2,1)} %shard_map.87), calls=%async_computation.1 | async-start | bytes 786432 | tf_op jit(solution)/shard_map/all_to_all | solution.py:484
  39.1 0.0 copy-done.3
  39.1 10.3 %all-to-all-done.1.zb = bf16[4,384,128]{2,1,0:T(8,128)(2,1)S(1)} async-done(((bf16[4,384,128]{2,1,0:T(8,128)(2,1)}), bf16[4,384,128]{2,1,0:T(8,128)(2,1)S(1)}, u32[]{:S(2)}, u32[]{:S(2)}) %all-to-all-start.1) | async-done | bytes 393248 | tf_op jit(solution)/shard_map/all_to_all | solution.py:484
  49.4 0.0 copy-done
  49.4 1.7 %shard_map.88 = (bf16[48,8,128]{2,1,0:T(8,128)(2,1)}, bf16[256,96]{1,0:T(8,128)(2,1)}, bf16[64,192]{1,0:T(8,128)(2,1)}, bf16[16,384]{1,0:T(8,128)(2,1)}) custom-call(bf16[4,384,128]{2,1,0:T(8,128)(2,1)S(1)} %all-to-all-done.1.zb, bf16[720,720]{1,0:T(8,128)(2,1)S(1)} %copy-done, f32[1,720]{1,0:T(1,128)S(1)} %broadcast_in_dim.3.bias), custom_call_target="tpu_custom_call" | custom-call | tf_op jit(solution)/shard_map/pallas_call | solution.py:462
  (1 shorter events, 0.0 us)
Async XLA Ops:
  0.6 1.0 %copy-start.1 = (bf16[1,1,1,48,4096]{4,3,2,1,0:T(8,128)(2,1)S(1)}, bf16[1,1,1,48,4096]{4,3,2,1,0:T(8,128)(2,1)}, u32[]{:S(2)}) copy-start(bf16[1,1,1,48,4096]{4,3,2,1,0:T(8,128)(2,1)} %param.5) | copy-start | bytes 1179652
  2.1 10.6 %collective-permute-start = (bf16[48,128]{1,0:T(8,128)(2,1)S(1)}, bf16[48,128]{1,0:T(8,128)(2,1)S(1)}, u32[]{:S(2)}, u32[]{:S(2)}) collective-permute-start(bf16[48,128]{1,0:T(8,128)(2,1)S(1)} %get-tuple-element.26), channel_id=1, source_target_pairs={{1,2},{2,1},{3,4},{4,3},{5,6},{6,5},{7,8},{8,7},{9,10},{10,9},{11,... | collective-permute-start | bytes 36872 | tf_op jit(solution)/shard_map/ppermute | solution.py:480
  10.6 2.2 %collective-permute-start.1 = (bf16[48,128]{1,0:T(8,128)(2,1)S(1)}, bf16[48,128]{1,0:T(8,128)(2,1)S(1)}, u32[]{:S(2)}, u32[]{:S(2)}) collective-permute-start(bf16[48,128]{1,0:T(8,128)(2,1)S(1)} %get-tuple-element.27), channel_id=1, source_target_pairs={{0,1},{1,0},{2,3},{3,2},{4,5},{5,4},{6,7},{7,6},{8,9},{9,8},{10,11... | collective-permute-start | bytes 36872 | tf_op jit(solution)/shard_map/ppermute | solution.py:480
  12.7 15.6 %copy-start.2 = (f32[1,2,384]{2,1,0:T(2,128)S(1)}, f32[1,2,384]{2,1,0:T(2,128)}, u32[]{:S(2)}) copy-start(f32[1,2,384]{2,1,0:T(2,128)} %bias.1) | copy-start | bytes 9220
  28.4 10.7 %copy-start.3 = (f32[720]{0:T(1024)S(1)}, f32[720]{0:T(1024)}, u32[]{:S(2)}) copy-start(f32[720]{0:T(1024)} %param.9) | copy-start | bytes 8644
  28.4 21.0 %copy-start = (bf16[720,720]{1,0:T(8,128)(2,1)S(1)}, bf16[720,720]{1,0:T(8,128)(2,1)}, u32[]{:S(2)}) copy-start(bf16[720,720]{1,0:T(8,128)(2,1)} %weight.3) | copy-start | bytes 3110404
  32.4 17.0 %all-to-all-start.1 = ((bf16[4,384,128]{2,1,0:T(8,128)(2,1)}), bf16[4,384,128]{2,1,0:T(8,128)(2,1)S(1)}, u32[]{:S(2)}, u32[]{:S(2)}) async-start(bf16[4,384,128]{2,1,0:T(8,128)(2,1)} %shard_map.87), calls=%async_computation.1 | async-start | bytes 786432 | tf_op jit(solution)/shard_map/all_to_all | solution.py:484

commit v9 on v8

--- a/solution.py
+++ b/solution.py
@@ -42,7 +42,7 @@
 GEO = [Geo(b) for b in range(4)]
 SLOT_ROWS = 624
 PREPARE_MIB = 42
-STEPS = (640, 768, 512, 384)
+STEPS = (640, 768, 512, 256)
 
 
 def place():

time: 51.4 us -> 51.4 us (level)
  no operation moved by 1% of the time
where the time goes in v9:
time: 51.4 us; the launch traced here: 51.1 us
  starting transfers between devices  16 us (31%)
  blocking collectives  15 us (29%)
  waiting for transfers between devices  10.3 us (20%)
  Pallas kernels  8.15 us (16%)
  local copies, waits for them, and re-layouts  1.01 us (2%)
  between operations  0.7 us (1%)
    all_to_all x1, blocking collectives, swapped(): return lax.all_to_all(parts, axis, split_axis=0, concat_axis=0, tiled=True)  15 us
    all_to_all x1, waiting for transfers between devices, swapped(): return lax.all_to_all(parts, axis, split_axis=0, concat_axis=0, tiled=True)  10.3 us
    ppermute x2, starting transfers between devices, paired(): return lax.ppermute(shard, 'col', pairs)  9.3 us
    all_to_all x1, starting transfers between devices, swapped(): return lax.all_to_all(parts, axis, split_axis=0, concat_axis=0, tiled=True)  6.67 us
    pallas_call x1, Pallas kernels, call_block(): pl.pallas_call(block_kernel, out_shape=like((4, 384, 128))[0], in_specs=[...  4.05 us
    pallas_call x1, Pallas kernels, call_join(): pl.pallas_call(join_kernel, out_shape=like((WIDTH, 8, 128), (256, 96), (6...  1.71 us
    pallas_call x1, Pallas kernels, call_prepare(): pl.pallas_call(prepare_kernel, out_shape=like(*shapes), in_specs=[VMEM, p...  1.26 us
  transfers between devices with their start and end apart: 3, of which 1 were waited for; matrix products, arithmetic and copies ran while one was open for 0% of the time, Pallas kernels for 2%

profile of v9, /device:TPU:16, one launch (start us, length us, event | category | flops | bytes accessed | tf_op | source)
XLA Modules:
  0.0 51.1 jit_solution(9042653652324177592)
XLA Ops:
  0.6 0.0 copy-start.1
  0.6 1.0 %copy-done.1 = bf16[1,1,1,48,4096]{4,3,2,1,0:T(8,128)(2,1)S(1)} copy-done((bf16[1,1,1,48,4096]{4,3,2,1,0:T(8,128)(2,1)S(1)}, bf16[1,1,1,48,4096]{4,3,2,1,0:T(8,128)(2,1)}, u32[]{:S(2)}) %copy-start.1) | copy-done | bytes 393240
  1.6 0.5 shard_map.84
  2.1 8.4 %collective-permute-start = (bf16[48,128]{1,0:T(8,128)(2,1)S(1)}, bf16[48,128]{1,0:T(8,128)(2,1)S(1)}, u32[]{:S(2)}, u32[]{:S(2)}) collective-permute-start(bf16[48,128]{1,0:T(8,128)(2,1)S(1)} %get-tuple-element.26), channel_id=1, source_target_pairs={{1,2},{2,1},{3,4},{4,3},{5,6},{6,5},{7,8},{8,7},{9,10},{10,9},{11,... | collective-permute-start | bytes 36872 | tf_op jit(solution)/shard_map/ppermute | solution.py:480
  10.6 0.9 %collective-permute-start.1 = (bf16[48,128]{1,0:T(8,128)(2,1)S(1)}, bf16[48,128]{1,0:T(8,128)(2,1)S(1)}, u32[]{:S(2)}, u32[]{:S(2)}) collective-permute-start(bf16[48,128]{1,0:T(8,128)(2,1)S(1)} %get-tuple-element.27), channel_id=1, source_target_pairs={{0,1},{1,0},{2,3},{3,2},{4,5},{5,4},{6,7},{7,6},{8,9},{9,8},{10,11... | collective-permute-start | bytes 36872 | tf_op jit(solution)/shard_map/ppermute | solution.py:480
  11.4 1.3 %shard_map.85 = (bf16[48,4224]{1,0:T(8,128)(2,1)S(1)}, bf16[96,1152]{1,0:T(8,128)(2,1)S(1)}, bf16[192,384]{1,0:T(8,128)(2,1)S(1)}, bf16[384,128]{1,0:T(8,128)(2,...) custom-call(bf16[48,4096]{1,0:T(8,128)(2,1)S(1)} %get-tuple-element., ...), custom_call_target="tpu_custom_call" | custom-call | flops 1000000000 | bytes 12582912 | tf_op jit(solution)/shard_map/pallas_call | solution.py:418
  12.7 0.0 collective-permute-done.far
  12.7 0.0 collective-permute-done.1.near
  12.7 0.0 copy-start.2
  12.8 0.6 %shard_map.86 = bf16[4,624,128]{2,1,0:T(8,128)(2,1)S(1)} custom-call(bf16[48,128]{1,0:T(8,128)(2,1)S(1)} %collective-permute-done.far, bf16[48,128]{1,0:T(8,128)(2,1)S(1)} %collective-permute-done.1.near, bf16[48,4224]{1,0:T(8,128)(2,1)S(1)} %get-tuple-element.29.refs_0_, bf16[96,1152]{1,0:T(8,128)(2,1)S(1)} %get-tuple-element.30.refs_1_, ...), custom_call_target="tpu_custom_call" | custom-call | tf_op jit(solution)/shard_map/pallas_call | solution.py:436
  13.4 15.0 %all_to_all.10.strips = bf16[4,624,128]{2,1,0:T(8,128)(2,1)S(1)} all-to-all(bf16[4,624,128]{2,1,0:T(8,128)(2,1)S(1)} %shard_map.86), channel_id=1, replica_groups=mesh['branch'=4,'row'=4,'col'=16] {'row'}, dimensions={0} | all-to-all | bytes 1277952 | tf_op jit(solution)/shard_map/all_to_all | solution.py:484
  28.4 0.0 copy-done.2
  28.4 0.0 copy-start.3
  28.4 0.0 copy-start
  28.4 4.1 %shard_map.87 = bf16[4,384,128]{2,1,0:T(8,128)(2,1)} custom-call(bf16[4,624,128]{2,1,0:T(8,128)(2,1)S(1)} %all_to_all.10.strips, f32[1,2,384]{2,1,0:T(2,128)S(1)} %copy-done.2, bf16[2,3,48,144]{3,2,1,0:T(8,128)(2,1)S(1)} %get-tuple-element.40.refs_0_, bf16[2,3,96,288]{3,2,1,0:T(8,128)(2,1)S(1)} %get-tuple-element.41.refs_1_, ...), custom_call_target="tpu_custom_call" | custom-call | tf_op jit(solution)/shard_map/pallas_call | solution.py:451
  32.4 6.7 %all-to-all-start.1 = ((bf16[4,384,128]{2,1,0:T(8,128)(2,1)}), bf16[4,384,128]{2,1,0:T(8,128)(2,1)S(1)}, u32[]{:S(2)}, u32[]{:S(2)}) async-start(bf16[4,384,128]{2,1,0:T(8,128)(2,1)} %shard_map.87), calls=%async_computation.1 | async-start | bytes 786432 | tf_op jit(solution)/shard_map/all_to_all | solution.py:484
  39.1 0.0 copy-done.3
  39.1 10.3 %all-to-all-done.1.zb = bf16[4,384,128]{2,1,0:T(8,128)(2,1)S(1)} async-done(((bf16[4,384,128]{2,1,0:T(8,128)(2,1)}), bf16[4,384,128]{2,1,0:T(8,128)(2,1)S(1)}, u32[]{:S(2)}, u32[]{:S(2)}) %all-to-all-start.1) | async-done | bytes 393248 | tf_op jit(solution)/shard_map/all_to_all | solution.py:484
  49.4 0.0 copy-done
  49.4 1.7 %shard_map.88 = (bf16[48,8,128]{2,1,0:T(8,128)(2,1)}, bf16[256,96]{1,0:T(8,128)(2,1)}, bf16[64,192]{1,0:T(8,128)(2,1)}, bf16[16,384]{1,0:T(8,128)(2,1)}) custom-call(bf16[4,384,128]{2,1,0:T(8,128)(2,1)S(1)} %all-to-all-done.1.zb, bf16[720,720]{1,0:T(8,128)(2,1)S(1)} %copy-done, f32[1,720]{1,0:T(1,128)S(1)} %broadcast_in_dim.3.bias), custom_call_target="tpu_custom_call" | custom-call | tf_op jit(solution)/shard_map/pallas_call | solution.py:462
  (1 shorter events, 0.0 us)
Async XLA Ops:
  0.6 1.0 %copy-start.1 = (bf16[1,1,1,48,4096]{4,3,2,1,0:T(8,128)(2,1)S(1)}, bf16[1,1,1,48,4096]{4,3,2,1,0:T(8,128)(2,1)}, u32[]{:S(2)}) copy-start(bf16[1,1,1,48,4096]{4,3,2,1,0:T(8,128)(2,1)} %param.5) | copy-start | bytes 1179652
  2.1 10.6 %collective-permute-start = (bf16[48,128]{1,0:T(8,128)(2,1)S(1)}, bf16[48,128]{1,0:T(8,128)(2,1)S(1)}, u32[]{:S(2)}, u32[]{:S(2)}) collective-permute-start(bf16[48,128]{1,0:T(8,128)(2,1)S(1)} %get-tuple-element.26), channel_id=1, source_target_pairs={{1,2},{2,1},{3,4},{4,3},{5,6},{6,5},{7,8},{8,7},{9,10},{10,9},{11,... | collective-permute-start | bytes 36872 | tf_op jit(solution)/shard_map/ppermute | solution.py:480
  10.6 2.2 %collective-permute-start.1 = (bf16[48,128]{1,0:T(8,128)(2,1)S(1)}, bf16[48,128]{1,0:T(8,128)(2,1)S(1)}, u32[]{:S(2)}, u32[]{:S(2)}) collective-permute-start(bf16[48,128]{1,0:T(8,128)(2,1)S(1)} %get-tuple-element.27), channel_id=1, source_target_pairs={{0,1},{1,0},{2,3},{3,2},{4,5},{5,4},{6,7},{7,6},{8,9},{9,8},{10,11... | collective-permute-start | bytes 36872 | tf_op jit(solution)/shard_map/ppermute | solution.py:480
  12.7 15.6 %copy-start.2 = (f32[1,2,384]{2,1,0:T(2,128)S(1)}, f32[1,2,384]{2,1,0:T(2,128)}, u32[]{:S(2)}) copy-start(f32[1,2,384]{2,1,0:T(2,128)} %bias.1) | copy-start | bytes 9220
  28.4 10.7 %copy-start.3 = (f32[720]{0:T(1024)S(1)}, f32[720]{0:T(1024)}, u32[]{:S(2)}) copy-start(f32[720]{0:T(1024)} %param.9) | copy-start | bytes 8644
  28.4 21.0 %copy-start = (bf16[720,720]{1,0:T(8,128)(2,1)S(1)}, bf16[720,720]{1,0:T(8,128)(2,1)}, u32[]{:S(2)}) copy-start(bf16[720,720]{1,0:T(8,128)(2,1)} %weight.3) | copy-start | bytes 3110404
  32.4 17.0 %all-to-all-start.1 = ((bf16[4,384,128]{2,1,0:T(8,128)(2,1)}), bf16[4,384,128]{2,1,0:T(8,128)(2,1)S(1)}, u32[]{:S(2)}, u32[]{:S(2)}) async-start(bf16[4,384,128]{2,1,0:T(8,128)(2,1)} %shard_map.87), calls=%async_computation.1 | async-start | bytes 786432 | tf_op jit(solution)/shard_map/all_to_all | solution.py:484
